TPU v7x, 512 devices: a whole 4x4x16 slice. The times are simulated.
512 devices in a mesh: dp: 32 (over y_lo, z), tensor: 16 (over y_hi, x, core).
Axes of the slice: x: 4, y: 4 (y_hi: 2, y_lo: 2; y = y_hi * 2 + y_lo), z: 16, core: 2. Of those that a mesh axis runs over, the one named last changes fastest.
Arguments:
- inputs: bfloat16 [4096, 8192], P('dp', 'tensor'), may hold values from -6 to 6
- grad_context: bfloat16 [4096, 8192], P('dp', 'tensor'), may hold values from -24 to 24
- gain: float32 [8192], replicated, may hold values from 0.1 to 1.9
- w_query: bfloat16 [8192, 8192], P('dp', 'tensor'), may hold values from -0.0625 to 0.0625
- w_keyval: bfloat16 [8192, 1024], P('dp', 'tensor'), may hold values from -0.0625 to 0.0625
Outputs:
- grad_input: bfloat16 [4096, 8192], P('dp', 'tensor')
- grad_gain: float32 [8192], P('tensor')
- grad_w_keyval: bfloat16 [8192, 1024], P('dp', 'tensor')
All inputs are finite; a program needn't handle non-finite values.
Results may differ from a plain program's by a relative error of at most 0.023.
Values may be sent and summed in bfloat16 or wider, within the bound.
A program may use at most 64 MiB of HBM per device.

v0:
```python
import math

import jax
import jax.numpy as jnp
from jax import lax
from jax.sharding import PartitionSpec as P

HD = 128
KV_HEADS = 4
HEADS_DEV = 4


def rope_tables(length, head_size):
    positions = lax.broadcasted_iota(jnp.int32, (length, head_size // 2), 0).astype(jnp.float32)
    index_half = lax.broadcasted_iota(jnp.int32, (length, head_size // 2), 1).astype(jnp.float32)
    frequency = jnp.exp(-(2.0 * index_half / head_size) * math.log(500000.0))
    angles = positions * frequency
    return (jnp.cos(angles), jnp.sin(angles))


def rotate(vectors, cosine_table, sine_table):
    half_size = vectors.shape[-1] // 2
    first_half = vectors[..., :half_size]
    second_half = vectors[..., half_size:]
    return jnp.concatenate(
        [
            first_half * cosine_table - second_half * sine_table,
            first_half * sine_table + second_half * cosine_table,
        ],
        axis=-1,
    )


def unrotate(vectors, cosine_table, sine_table):
    half_size = vectors.shape[-1] // 2
    first_half = vectors[..., :half_size]
    second_half = vectors[..., half_size:]
    return jnp.concatenate(
        [
            first_half * cosine_table + second_half * sine_table,
            second_half * cosine_table - first_half * sine_table,
        ],
        axis=-1,
    )


def on_device(inputs, grad_context, gain, w_query, w_keyval):
    contract_last = (((1,), (1,)), ((), ()))
    contract_first = (((0,), (0,)), ((), ()))
    seq_length = inputs.shape[0]
    local_cols = inputs.shape[1]
    model_width = gain.shape[0]
    head_size = HD
    heads_here = HEADS_DEV
    group_cols = w_keyval.shape[1]
    tensor_count = lax.axis_size("tensor")
    keyval_total = group_cols * tensor_count
    kv_heads = KV_HEADS
    devices_per_group = tensor_count // kv_heads
    score_scale = head_size ** (-0.5)
    tensor_slot = lax.axis_index("tensor")
    gain_local = lax.dynamic_slice_in_dim(gain, tensor_slot * local_cols, local_cols, 0)
    as_float = inputs.astype(jnp.float32)
    row_sum = lax.psum(jnp.sum(as_float * as_float, axis=1, keepdims=True), "tensor")
    inv_rms = lax.rsqrt(row_sum / model_width + 1e-05)
    unit_rows = as_float * inv_rms
    normed = (unit_rows * gain_local).astype(jnp.bfloat16)
    normed_full = lax.all_gather(normed, "tensor", axis=1, tiled=True)
    query_weight, keyweight = (
        lax.all_gather(w_query, "dp", axis=0, tiled=True),
        lax.all_gather(w_keyval, "dp", axis=0, tiled=True),
    )
    query_proj = jnp.dot(normed_full, query_weight, preferred_element_type=jnp.float32).astype(
        jnp.bfloat16
    )
    keyval_part = jnp.dot(normed_full, keyweight, preferred_element_type=jnp.float32).astype(
        jnp.bfloat16
    )
    keyval_full = lax.all_gather(keyval_part, "tensor", axis=1, tiled=True)
    group_slot = tensor_slot // devices_per_group
    key_block = lax.dynamic_slice_in_dim(keyval_full, group_slot * head_size, head_size, 1)
    value_block = lax.dynamic_slice_in_dim(
        keyval_full, (kv_heads + group_slot) * head_size, head_size, 1
    )
    cosine_table, sine_table = rope_tables(seq_length, head_size)
    cos_heads = cosine_table[:, None, :]
    sin_heads = sine_table[:, None, :]
    query_heads = query_proj.astype(jnp.float32).reshape(seq_length, heads_here, head_size)
    q_rot = rotate(query_heads, cos_heads, sin_heads).astype(jnp.bfloat16)
    k_rot = rotate(key_block.astype(jnp.float32), cosine_table, sine_table).astype(jnp.bfloat16)
    scores = (
        jnp.einsum("shd,td->hst", q_rot, k_rot, preferred_element_type=jnp.float32) * score_scale
    )
    causal = lax.broadcasted_iota(jnp.int32, (seq_length, seq_length), 0) >= lax.broadcasted_iota(
        jnp.int32, (seq_length, seq_length), 1
    )
    exponent = jnp.where(causal[None, :, :], jnp.exp(scores), 0.0)
    softmax_probs = exponent / jnp.sum(exponent, axis=2, keepdims=True)
    prob_weights = softmax_probs.astype(jnp.bfloat16)
    context = jnp.einsum(
        "hst,td->shd", prob_weights, value_block, preferred_element_type=jnp.float32
    ).astype(jnp.bfloat16)
    grad_ctx = grad_context.reshape(seq_length, heads_here, head_size)
    grad_probs = jnp.einsum(
        "shd,td->hst", grad_ctx, value_block, preferred_element_type=jnp.float32
    )
    row_delta = jnp.sum(grad_ctx.astype(jnp.float32) * context.astype(jnp.float32), axis=2).T[
        :, :, None
    ]
    grad_scores = (softmax_probs * (grad_probs - row_delta) * score_scale).astype(jnp.bfloat16)
    grad_qrot = jnp.einsum("hst,td->shd", grad_scores, k_rot, preferred_element_type=jnp.float32)
    grad_krot = jnp.einsum("hst,shd->td", grad_scores, q_rot, preferred_element_type=jnp.float32)
    grad_value = jnp.einsum(
        "hst,shd->td", prob_weights, grad_ctx, preferred_element_type=jnp.float32
    )
    grad_query = (
        unrotate(grad_qrot, cos_heads, sin_heads)
        .astype(jnp.bfloat16)
        .reshape(seq_length, heads_here * head_size)
    )
    grad_terms = jnp.zeros((seq_length, keyval_total), jnp.float32)
    grad_terms = lax.dynamic_update_slice_in_dim(
        grad_terms, unrotate(grad_krot, cosine_table, sine_table), group_slot * head_size, 1
    )
    grad_terms = lax.dynamic_update_slice_in_dim(
        grad_terms, grad_value, (kv_heads + group_slot) * head_size, 1
    )
    grad_keyval = lax.psum_scatter(
        grad_terms.astype(jnp.bfloat16), "tensor", scatter_dimension=1, tiled=True
    )
    result = lax.dot_general(
        query_weight, grad_query, contract_last, preferred_element_type=jnp.float32
    )
    grad_normed = (
        lax.psum_scatter(
            (
                result
                + lax.dot_general(
                    keyweight, grad_keyval, contract_last, preferred_element_type=jnp.float32
                )
            ).astype(jnp.bfloat16),
            "tensor",
            scatter_dimension=0,
            tiled=True,
        )
        .astype(jnp.float32)
        .T
    )
    scaled_grad = grad_normed * gain_local
    product_sum = lax.psum(jnp.sum(scaled_grad * unit_rows, axis=1, keepdims=True), "tensor")
    grad_input = (inv_rms * (scaled_grad - unit_rows * (product_sum / model_width))).astype(
        jnp.bfloat16
    )
    grad_gain = lax.psum(jnp.sum(grad_normed * unit_rows, axis=0), "dp")
    keyval_all = lax.all_gather(grad_keyval, "dp", axis=0, tiled=True)
    rows_normed = lax.all_to_all(normed_full, "dp", split_axis=1, concat_axis=0, tiled=True)
    keyval_weight_grad = lax.dot_general(
        rows_normed, keyval_all, contract_first, preferred_element_type=jnp.float32
    )
    return (grad_input, grad_gain, keyval_weight_grad.astype(jnp.bfloat16))


def solution(mesh):
    in_specs = (P("dp", "tensor"), P("dp", "tensor"), P(), P("dp", "tensor"), P("dp", "tensor"))
    out_specs = (P("dp", "tensor"), P("tensor"), P("dp", "tensor"))
    return jax.shard_map(
        on_device, mesh=mesh, in_specs=in_specs, out_specs=out_specs, check_vma=False
    )
```

profile of v0, /device:TPU:6, one launch (start us, length us, event | category | flops | bytes accessed | tf_op | source)
XLA Modules:
  0.0 723.5 jit_solution(10159442751413504950)
XLA Ops:
  7.2 1.0 fusion.25
  8.2 29.9 %psum.21 = f32[128,1]{0,1:T(1,128)S(1)} all-reduce(f32[128,1]{0,1:T(1,128)S(1)} %bitcast.94), channel_id=1, replica_groups=mesh['dp'=32,'tensor'=16] {'tensor'}, use_global_device_ids=true, to_apply=%region_1.0 | all-reduce | flops 128 | bytes 1024 | tf_op jit(solution)/shard_map/psum | solution.py:64
  38.2 0.8 dynamic_slice.9
  38.9 1.7 fusion.19
  40.7 0.7 all-gather.6.cloned.1.call-update
  42.1 71.2 %all-gather.4.cloned.1.call-done = bf16[128,8192]{1,0:T(8,128)(2,1)} async-done(((bf16[128,512]{1,0:T(8,128)(2,1)}), bf16[128,8192]{1,0:T(8,128)(2,1)}) %all-gather.4.cloned.1.call-update) | async-done | bytes 2097168 | tf_op jit(solution)/shard_map/all_gather | solution.py:68
  113.3 3.2 copy.61
  116.4 12.9 %all-to-all-start = ((bf16[128,32,256]{2,0,1:T(8,128)(2,1)}), bf16[128,32,256]{2,0,1:T(8,128)(2,1)}, u32[]{:S(2)}, u32[]{:S(2)}) async-start(bf16[128,32,256]{2,0,1:T(8,128)(2,1)} %bitcast.87), calls=%async_computation.2 | async-start | bytes 4194304 | tf_op jit(solution)/shard_map/all_to_all | solution.py:156
  129.6 155.4 %all-gather.6.cloned.1.call-done = bf16[8192,64]{0,1:T(8,128)(2,1)} async-done(((bf16[256,64]{0,1:T(8,128)(2,1)}), bf16[8192,64]{0,1:T(8,128)(2,1)}) %all-gather.6.cloned.1.call-update) | async-done | bytes 1048592 | tf_op jit(solution)/shard_map/all_gather | solution.py:71
  285.0 2.1 convolution_convert_fusion.3
  287.0 19.6 %all_gather.17 = bf16[128,1024]{0,1:T(8,128)(2,1)S(1)} all-gather(bf16[128,64]{0,1:T(8,128)(2,1)S(1)} %convolution_convert_fusion.3), channel_id=1, replica_groups=mesh['dp'=32,'tensor'=16] {'tensor'}, dimensions={1}, use_global_device_ids=true | all-gather | bytes 278528 | tf_op jit(solution)/shard_map/all_gather | solution.py:79
  307.0 126.6 %all-gather.8.cloned.1.call-done = bf16[8192,512]{1,0:T(8,128)(2,1)} async-done(((bf16[256,512]{1,0:T(8,128)(2,1)}), bf16[8192,512]{1,0:T(8,128)(2,1)}) %all-gather.8.cloned.1.call-update) | async-done | bytes 8388624 | tf_op jit(solution)/shard_map/all_gather | solution.py:70
  433.6 4.6 fusion.12
  440.2 0.7 copy-done.3
  441.6 8.3 %fusion.59 = f32[128,8192]{1,0:T(8,128)} fusion(bf16[128,512]{0,1:T(8,128)(2,1)S(1)} %bitcast.91, bf16[8192,512]{1,0:T(8,128)(2,1)} %all-gather.8.cloned.1.call-done), kind=kOutput, calls=%fused_computation.88 | convolution fusion | flops 1073741824 | bytes 12713984 | tf_op jit(solution)/shard_map/dot_general | solution.py:131
  449.9 71.7 %reduce-scatter.3.cloned.1.call-done = bf16[128,64]{0,1:T(8,128)(2,1)} async-done(((bf16[128,1024]{0,1:T(8,128)(2,1)}), bf16[128,64]{0,1:T(8,128)(2,1)}) %reduce-scatter.3.cloned.1.call-update) | async-done | bytes 16400 | tf_op jit(solution)/shard_map/reduce_scatter | solution.py:128
  521.6 4.3 fusion.1
  526.6 65.7 %all_gather.19 = bf16[4096,64]{0,1:T(8,128)(2,1)S(1)} all-gather(bf16[128,64]{0,1:T(8,128)(2,1)S(1)} %copy-done.5), channel_id=1, replica_groups=mesh['dp'=32,'tensor'=16] {'dp'}, dimensions={0}, use_global_device_ids=true | all-gather | bytes 540672 | tf_op jit(solution)/shard_map/all_gather | solution.py:155
  592.3 2.7 convolution_convert_fusion.2
  594.9 25.2 %reduce-scatter.5.cloned.1.call-done = bf16[512,128]{0,1:T(8,128)(2,1)} async-done(((bf16[8192,128]{0,1:T(8,128)(2,1)}), bf16[512,128]{0,1:T(8,128)(2,1)}) %reduce-scatter.5.cloned.1.call-update) | async-done | bytes 131088 | tf_op jit(solution)/shard_map/reduce_scatter | solution.py:135
  620.2 1.1 fusion.24
  621.3 29.4 %psum.22 = f32[128,1]{0,1:T(1,128)S(1)} all-reduce(f32[128,1]{0,1:T(1,128)S(1)} %bitcast.93), channel_id=1, replica_groups=mesh['dp'=32,'tensor'=16] {'tensor'}, use_global_device_ids=true, to_apply=%region_7.8 | all-reduce | flops 128 | bytes 1024 | tf_op jit(solution)/shard_map/psum | solution.py:150
  650.7 64.6 %psum.23 = f32[512]{0:T(512)} all-reduce(f32[512]{0:T(512)S(1)} %get-tuple-element.3), channel_id=1, replica_groups=mesh['dp'=32,'tensor'=16] {'dp'}, use_global_device_ids=true, to_apply=%region_9.10 | all-reduce | flops 512 | bytes 4096 | tf_op jit(solution)/shard_map/psum | solution.py:154
  715.3 1.7 fusion.23
  (46 shorter events, 4.7 us)
Async XLA Ops:
  7.2 106.1 %all-gather.4.cloned.1.call-start = ((), (), s32[]{:S(2)}) async-start(), calls=%async_computation.3 | async-start | bytes 2228224 | tf_op jit(solution)/shard_map/all_gather | solution.py:68
  40.6 244.4 %all-gather.6.cloned.1.call-start = ((), (), s32[]{:S(2)}) async-start(), calls=%async_computation.4 | async-start | bytes 1081344 | tf_op jit(solution)/shard_map/all_gather | solution.py:71
  41.4 392.2 %all-gather.8.cloned.1.call-start = ((), (), s32[]{:S(2)}) async-start(), calls=%async_computation.5 | async-start | bytes 8650752 | tf_op jit(solution)/shard_map/all_gather | solution.py:70
  116.4 12.9 %copy-start.4 = (bf16[128,512]{1,0:T(8,128)(2,1)S(1)}, bf16[128,512]{1,0:T(8,128)(2,1)}, u32[]{:S(2)}) copy-start(bf16[128,512]{1,0:T(8,128)(2,1)} %param.6) | copy-start | bytes 393220
  116.4 168.5 %copy-start = (bf16[128,8192]{1,0:T(8,128)(2,1)S(1)}, bf16[128,8192]{1,0:T(8,128)(2,1)}, u32[]{:S(2)}) copy-start(bf16[128,8192]{1,0:T(8,128)(2,1)} %all-gather.4.cloned.1.call-done) | copy-start | bytes 6291460
  116.4 475.8 %all-to-all-start = ((bf16[128,32,256]{2,0,1:T(8,128)(2,1)}), bf16[128,32,256]{2,0,1:T(8,128)(2,1)}, u32[]{:S(2)}, u32[]{:S(2)}) async-start(bf16[128,32,256]{2,0,1:T(8,128)(2,1)} %bitcast.87), calls=%async_computation.2 | async-start | bytes 4194304 | tf_op jit(solution)/shard_map/all_to_all | solution.py:156
  129.3 392.2 %reduce-scatter.3.cloned.1.call-start = ((), (), s32[]{:S(2)}) async-start(), calls=%async_computation.6 | async-start | bytes 278528 | tf_op jit(solution)/shard_map/reduce_scatter | solution.py:128
  440.2 0.7 copy-start.3
  440.9 179.2 %reduce-scatter.5.cloned.1.call-start = ((), (), s32[]{:S(2)}) async-start(), calls=%async_computation.7 | async-start | bytes 2228224 | tf_op jit(solution)/shard_map/reduce_scatter | solution.py:135
  441.6 80.0 %copy-start.1 = (bf16[8192,64]{0,1:T(8,128)(2,1)S(1)}, bf16[8192,64]{0,1:T(8,128)(2,1)}, u32[]{:S(2)}) copy-start(bf16[8192,64]{0,1:T(8,128)(2,1)} %all-gather.6.cloned.1.call-done) | copy-start | bytes 3145732
  525.8 0.7 copy-start.5
  526.6 93.6 %copy-start.2 = (bf16[128,512]{1,0:T(8,128)(2,1)S(1)}, bf16[128,512]{1,0:T(8,128)(2,1)}, u32[]{:S(2)}) copy-start(bf16[128,512]{1,0:T(8,128)(2,1)} %param.5) | copy-start | bytes 393220
Sparse Core Ops, SparseCore 0:
  40.7 72.4 all-gather.3
  115.3 169.6 all-gather.5
  287.1 146.4 all-gather.7
  441.0 80.4 reduce-scatter.2
  526.9 93.1 reduce-scatter.4
where the time goes:
time: 728 us; the launch traced here: 723 us
  waiting for transfers between devices  451 us (62%)
  blocking collectives  209 us (29%)
  matrix products  23.4 us (3%)
  between operations  14 us (2%)
  starting transfers between devices  13.1 us (2%)
    all_gather x1, waiting for transfers between devices, on_device(): lax.all_gather(w_keyval, 'dp', axis=0, tiled=True)  155 us
    all_gather x1, waiting for transfers between devices, on_device(): lax.all_gather(w_query, 'dp', axis=0, tiled=True)  127 us
    reduce_scatter x1, waiting for transfers between devices, on_device(): lax.psum_scatter(grad_terms.astype(jnp.bfloat16), 'tensor', scatter_dimen...  71.7 us
    all_gather x1, waiting for transfers between devices, on_device(): normed_full = lax.all_gather(normed, 'tensor', axis=1, tiled=True)  71.2 us
    all_gather x1, blocking collectives, on_device(): keyval_all = lax.all_gather(grad_keyval, 'dp', axis=0, tiled=True)  65.7 us
    psum x1, blocking collectives, on_device(): grad_gain = lax.psum(jnp.sum(grad_normed * unit_rows, axis=0), 'dp')  64.6 us
    psum x1, blocking collectives, on_device(): lax.psum(jnp.sum(as_float * as_float, axis=1, keepdims=True), 'tensor')  29.9 us
    psum x1, blocking collectives, on_device(): lax.psum(jnp.sum(scaled_grad * unit_rows, axis=1, keepdims=True), 'tensor')  29.4 us
  transfers between devices with their start and end apart: 6, of which 5 were waited for; matrix products, arithmetic and copies ran while one was open for 4% of the time, Pallas kernels for 0%

commit v1 on v0

--- a/solution.py
+++ b/solution.py
@@ -60,16 +60,16 @@
     score_scale = head_size ** (-0.5)
     tensor_slot = lax.axis_index("tensor")
     gain_local = lax.dynamic_slice_in_dim(gain, tensor_slot * local_cols, local_cols, 0)
-    as_float = inputs.astype(jnp.float32)
-    row_sum = lax.psum(jnp.sum(as_float * as_float, axis=1, keepdims=True), "tensor")
+    weight_block = jnp.concatenate([w_query, w_keyval], axis=1)
+    weight_full = lax.all_gather(weight_block, "dp", axis=0, tiled=True)
+    query_weight = weight_full[:, : w_query.shape[1]]
+    keyweight = weight_full[:, w_query.shape[1] :]
+    inputs_full = lax.all_gather(inputs, "tensor", axis=1, tiled=True).astype(jnp.float32)
+    row_sum = jnp.sum(inputs_full * inputs_full, axis=1, keepdims=True)
     inv_rms = lax.rsqrt(row_sum / model_width + 1e-05)
-    unit_rows = as_float * inv_rms
-    normed = (unit_rows * gain_local).astype(jnp.bfloat16)
-    normed_full = lax.all_gather(normed, "tensor", axis=1, tiled=True)
-    query_weight, keyweight = (
-        lax.all_gather(w_query, "dp", axis=0, tiled=True),
-        lax.all_gather(w_keyval, "dp", axis=0, tiled=True),
-    )
+    unit_full = inputs_full * inv_rms
+    normed_full = (unit_full * gain[None, :]).astype(jnp.bfloat16)
+    unit_rows = inputs.astype(jnp.float32) * inv_rms
     query_proj = jnp.dot(normed_full, query_weight, preferred_element_type=jnp.float32).astype(
         jnp.bfloat16
     )

time: 728 us -> 639 us (0.88)
  waiting for transfers between devices: 451 us -> 384 us
  blocking collectives: 209 us -> 178 us
    all_gather x3 -> x2, waiting for transfers between devices: 353 us -> 288 us  [the longest x1 220 us: on_device(): weight_full = lax.all_gather(weight_block, 'dp', axis=0, tiled=True)]
    psum x1 -> x0, blocking collectives: 29.9 us -> none  [on_device(): lax.psum(jnp.sum(as_float * as_float, axis=1, keepdims=True), 'tensor')]
  transfers between devices with their start and end apart: 6 -> 5, of which waited for: 5 -> 4; matrix products, arithmetic and copies ran while one was open for 4% -> 6% of each run, Pallas kernels for 0% -> 0%
where the time goes in v1:
time: 639 us; the launch traced here: 634 us
  waiting for transfers between devices  384 us (60%)
  blocking collectives  178 us (28%)
  matrix products  25.2 us (4%)
  between operations  14 us (2%)
  starting transfers between devices  12.8 us (2%)
  other arithmetic  10.9 us (2%)
  local copies, waits for them, and re-layouts  8.49 us (1%)
    all_gather x1, waiting for transfers between devices, on_device(): weight_full = lax.all_gather(weight_block, 'dp', axis=0, tiled=True)  220 us
    reduce_scatter x1, waiting for transfers between devices, on_device(): lax.psum_scatter(grad_terms.astype(jnp.bfloat16), 'tensor', scatter_dimen...  73.7 us
    all_gather x1, waiting for transfers between devices, on_device(): lax.all_gather(inputs, 'tensor', axis=1, tiled=True).astype(jnp.float32)  68.3 us
    all_gather x1, blocking collectives, on_device(): keyval_all = lax.all_gather(grad_keyval, 'dp', axis=0, tiled=True)  65.4 us
    psum x1, blocking collectives, on_device(): grad_gain = lax.psum(jnp.sum(grad_normed * unit_rows, axis=0), 'dp')  64.5 us
    psum x1, blocking collectives, on_device(): lax.psum(jnp.sum(scaled_grad * unit_rows, axis=1, keepdims=True), 'tensor')  29.4 us
    reduce_scatter x1, waiting for transfers between devices, on_device(): lax.psum_scatter((result + lax.dot_general(keyweight, grad_keyval, contra...  22 us
    all_gather x1, blocking collectives, on_device(): keyval_full = lax.all_gather(keyval_part, 'tensor', axis=1, tiled=True)  19 us
  transfers between devices with their start and end apart: 5, of which 4 were waited for; matrix products, arithmetic and copies ran while one was open for 6% of the time, Pallas kernels for 0%

profile of v1, /device:TPU:6, one launch (start us, length us, event | category | flops | bytes accessed | tf_op | source)
XLA Modules:
  0.0 633.7 jit_solution(6820111288008653620)
XLA Ops:
  7.2 1.7 copy.45
  8.9 0.9 copy.46
  9.8 1.7 pad_maximum_fusion
  11.6 68.3 %all-gather.3.cloned.1.call-done = bf16[128,8192]{0,1:T(8,128)(2,1)} async-done(((bf16[128,512]{0,1:T(8,128)(2,1)}), bf16[128,8192]{0,1:T(8,128)(2,1)}) %all-gather.3.cloned.1.call-update) | async-done | bytes 2097168 | tf_op jit(solution)/shard_map/all_gather | solution.py:67
  79.9 2.7 fusion.5
  82.6 3.5 fusion.7
  86.1 12.6 %all-to-all-start = ((bf16[128,32,256]{0,2,1:T(8,128)(2,1)}), bf16[128,32,256]{0,2,1:T(8,128)(2,1)S(1)}, u32[]{:S(2)}, u32[]{:S(2)}) async-start(bf16[128,32,256]{0,2,1:T(8,128)(2,1)} %bitcast.82), calls=%async_computation.2 | async-start | bytes 4194304 | tf_op jit(solution)/shard_map/all_to_all | solution.py:156
  98.9 219.9 %all-gather.5.cloned.1.call-done = bf16[8192,576]{1,0:T(8,128)(2,1)} async-done(((bf16[256,576]{1,0:T(8,128)(2,1)}), bf16[8192,576]{1,0:T(8,128)(2,1)}) %all-gather.5.cloned.1.call-update) | async-done | bytes 9437200 | tf_op jit(solution)/shard_map/all_gather | solution.py:64
  318.9 3.1 fusion.29
  322.0 19.0 %all_gather.14 = bf16[128,1024]{0,1:T(8,128)(2,1)S(1)} all-gather(bf16[128,64]{0,1:T(8,128)(2,1)S(1)} %fusion.29), channel_id=1, replica_groups=mesh['dp'=32,'tensor'=16] {'tensor'}, dimensions={1}, use_global_device_ids=true | all-gather | bytes 278528 | tf_op jit(solution)/shard_map/all_gather | solution.py:79
  341.3 5.3 fusion.24
  350.0 7.8 %fusion.1 = f32[8192,128]{1,0:T(8,128)} fusion(bf16[128,512]{0,1:T(8,128)(2,1)S(1)} %bitcast.87, bf16[8192,576]{1,0:T(8,128)(2,1)} %all-gather.5.cloned.1.call-done), kind=kOutput, calls=%fused_computation.2 | convolution fusion | flops 1073741824 | bytes 12713984 | tf_op jit(solution)/shard_map/dot_general | solution.py:131
  357.8 73.7 %reduce-scatter.3.cloned.1.call-done = bf16[128,64]{0,1:T(8,128)(2,1)} async-done(((bf16[128,1024]{0,1:T(8,128)(2,1)}), bf16[128,64]{0,1:T(8,128)(2,1)}) %reduce-scatter.3.cloned.1.call-update) | async-done | bytes 16400 | tf_op jit(solution)/shard_map/reduce_scatter | solution.py:128
  431.5 4.9 fusion
  436.4 0.8 dynamic_slice.11
  437.2 2.9 copy.64
  440.1 65.4 %all_gather.15 = bf16[4096,64]{0,1:T(8,128)(2,1)S(1)} all-gather(bf16[128,64]{0,1:T(8,128)(2,1)S(1)} %copy-done.3), channel_id=1, replica_groups=mesh['dp'=32,'tensor'=16] {'dp'}, dimensions={0}, use_global_device_ids=true | all-gather | bytes 540672 | tf_op jit(solution)/shard_map/all_gather | solution.py:155
  505.6 2.7 convolution_convert_fusion.1
  508.2 22.0 %reduce-scatter.5.cloned.1.call-done = bf16[512,128]{1,0:T(8,128)(2,1)} async-done(((bf16[8192,128]{1,0:T(8,128)(2,1)}), bf16[512,128]{1,0:T(8,128)(2,1)}) %reduce-scatter.5.cloned.1.call-update) | async-done | bytes 131088 | tf_op jit(solution)/shard_map/reduce_scatter | solution.py:135
  530.2 1.1 fusion.37
  531.3 29.4 %psum.14 = f32[128,1]{0,1:T(1,128)S(1)} all-reduce(f32[128,1]{0,1:T(1,128)S(1)} %bitcast.89), channel_id=1, replica_groups=mesh['dp'=32,'tensor'=16] {'tensor'}, use_global_device_ids=true, to_apply=%region_6.7 | all-reduce | flops 128 | bytes 1024 | tf_op jit(solution)/shard_map/psum | solution.py:150
  560.8 1.0 fusion.36
  561.8 0.8 copy.65
  562.6 64.5 %psum.15 = f32[512]{0:T(512)} all-reduce(f32[512]{0:T(512)S(1)} %get-tuple-element.12), channel_id=1, replica_groups=mesh['dp'=32,'tensor'=16] {'dp'}, use_global_device_ids=true, to_apply=%region_8.9 | all-reduce | flops 512 | bytes 4096 | tf_op jit(solution)/shard_map/psum | solution.py:154
  (42 shorter events, 4.0 us)
Async XLA Ops:
  7.2 72.7 %all-gather.3.cloned.1.call-start = ((), (), s32[]{:S(2)}) async-start(), calls=%async_computation.3 | async-start | bytes 2228224 | tf_op jit(solution)/shard_map/all_gather | solution.py:67
  8.9 310.0 %all-gather.5.cloned.1.call-start = ((), (), s32[]{:S(2)}) async-start(), calls=%async_computation.4 | async-start | bytes 10813440 | tf_op jit(solution)/shard_map/all_gather | solution.py:64
  82.6 16.2 %copy-start.2 = (bf16[128,512]{1,0:T(8,128)(2,1)S(1)}, bf16[128,512]{1,0:T(8,128)(2,1)}, u32[]{:S(2)}) copy-start(bf16[128,512]{1,0:T(8,128)(2,1)} %param.6) | copy-start | bytes 393220
  86.1 351.1 %all-to-all-start = ((bf16[128,32,256]{0,2,1:T(8,128)(2,1)}), bf16[128,32,256]{0,2,1:T(8,128)(2,1)S(1)}, u32[]{:S(2)}, u32[]{:S(2)}) async-start(bf16[128,32,256]{0,2,1:T(8,128)(2,1)} %bitcast.82), calls=%async_computation.2 | async-start | bytes 4194304 | tf_op jit(solution)/shard_map/all_to_all | solution.py:156
  98.7 332.8 %reduce-scatter.3.cloned.1.call-start = ((), (), s32[]{:S(2)}) async-start(), calls=%async_computation.5 | async-start | bytes 278528 | tf_op jit(solution)/shard_map/reduce_scatter | solution.py:128
  348.6 0.7 copy-start.1
  349.3 180.9 %reduce-scatter.5.cloned.1.call-start = ((), (), s32[]{:S(2)}) async-start(), calls=%async_computation.6 | async-start | bytes 2228224 | tf_op jit(solution)/shard_map/reduce_scatter | solution.py:135
  436.4 3.8 copy-start.3
  436.4 93.8 %copy-start = (bf16[128,512]{0,1:T(8,128)(2,1)S(1)}, bf16[128,512]{0,1:T(8,128)(2,1)}, u32[]{:S(2)}) copy-start(bf16[128,512]{0,1:T(8,128)(2,1)} %copy.45) | copy-start | bytes 393220
Sparse Core Ops, SparseCore 0:
  11.9 67.9 all-gather.2
  81.9 236.8 all-gather.4
  349.4 82.0 reduce-scatter.2
  436.9 93.2 reduce-scatter.4

commit v2 on v1

--- a/solution.py
+++ b/solution.py
@@ -1,9 +1,72 @@
+import functools
 import math
 
 import jax
 import jax.numpy as jnp
 from jax import lax
+from jax.experimental import pallas as pl
+from jax.experimental.pallas import tpu as pltpu
 from jax.sharding import PartitionSpec as P
+
+MESH = pl.DeviceIdType.MESH
+
+
+def exchange_kernel(axis, n, per_peer, *refs):
+    count = len(per_peer)
+    src_refs = refs[:count]
+    out_refs = refs[count : 2 * count]
+    send_sems, recv_sems = refs[2 * count :]
+    me = lax.axis_index(axis)
+    barrier = pltpu.get_barrier_semaphore()
+    for step in range(1, n):
+        peer = lax.rem(me + step, n)
+        pl.semaphore_signal(barrier, inc=1, device_id={axis: peer}, device_id_type=MESH)
+    pl.semaphore_wait(barrier, n - 1)
+    copies = []
+    for index in range(count):
+        for step in range(1, n):
+            peer = lax.rem(me + step, n)
+            source = src_refs[index].at[peer] if per_peer[index] else src_refs[index]
+            copy = pltpu.make_async_remote_copy(
+                src_ref=source,
+                dst_ref=out_refs[index].at[me],
+                send_sem=send_sems.at[index, step],
+                recv_sem=recv_sems.at[index, step],
+                device_id={axis: peer},
+                device_id_type=MESH,
+            )
+            copy.start()
+            copies.append(copy)
+    for index in range(count):
+        own = src_refs[index][me] if per_peer[index] else src_refs[index][...]
+        out_refs[index][me] = own
+    for copy in copies:
+        copy.wait_send()
+    for copy in copies:
+        copy.wait_recv()
+
+
+def exchange(axis, blocks, per_peer, collective_id):
+    n = lax.axis_size(axis)
+    out_shapes = []
+    for block, spread in zip(blocks, per_peer):
+        shape = block.shape[1:] if spread else block.shape
+        out_shapes.append(jax.ShapeDtypeStruct((n,) + tuple(shape), block.dtype))
+    count = len(blocks)
+    sent = sum(b.size * b.dtype.itemsize * (1 if s else n) for b, s in zip(blocks, per_peer))
+    return pl.pallas_call(
+        functools.partial(exchange_kernel, axis, n, tuple(per_peer)),
+        out_shape=tuple(out_shapes),
+        in_specs=[pl.BlockSpec(memory_space=pltpu.VMEM)] * count,
+        out_specs=tuple(pl.BlockSpec(memory_space=pltpu.VMEM) for _ in range(count)),
+        scratch_shapes=[
+            pltpu.SemaphoreType.DMA((count, n)),
+            pltpu.SemaphoreType.DMA((count, n)),
+        ],
+        compiler_params=pltpu.CompilerParams(collective_id=collective_id, has_side_effects=True),
+        cost_estimate=pl.CostEstimate(flops=0, bytes_accessed=2 * sent, transcendentals=0),
+    )(*blocks)
+
 
 HD = 128
 KV_HEADS = 4
@@ -45,14 +108,13 @@
 
 
 def on_device(inputs, grad_context, gain, w_query, w_keyval):
-    contract_last = (((1,), (1,)), ((), ()))
-    contract_first = (((0,), (0,)), ((), ()))
     seq_length = inputs.shape[0]
     local_cols = inputs.shape[1]
     model_width = gain.shape[0]
     head_size = HD
     heads_here = HEADS_DEV
     group_cols = w_keyval.shape[1]
+    query_cols = w_query.shape[1]
     tensor_count = lax.axis_size("tensor")
     keyval_total = group_cols * tensor_count
     kv_heads = KV_HEADS
@@ -62,9 +124,12 @@
     gain_local = lax.dynamic_slice_in_dim(gain, tensor_slot * local_cols, local_cols, 0)
     weight_block = jnp.concatenate([w_query, w_keyval], axis=1)
     weight_full = lax.all_gather(weight_block, "dp", axis=0, tiled=True)
-    query_weight = weight_full[:, : w_query.shape[1]]
-    keyweight = weight_full[:, w_query.shape[1] :]
-    inputs_full = lax.all_gather(inputs, "tensor", axis=1, tiled=True).astype(jnp.float32)
+    query_weight = weight_full[:, :query_cols]
+    keyweight = weight_full[:, query_cols:]
+    (input_blocks,) = exchange("tensor", [inputs], [False], 0)
+    inputs_full = (
+        input_blocks.transpose(1, 0, 2).reshape(seq_length, model_width).astype(jnp.float32)
+    )
     row_sum = jnp.sum(inputs_full * inputs_full, axis=1, keepdims=True)
     inv_rms = lax.rsqrt(row_sum / model_width + 1e-05)
     unit_full = inputs_full * inv_rms
@@ -76,7 +141,8 @@
     keyval_part = jnp.dot(normed_full, keyweight, preferred_element_type=jnp.float32).astype(
         jnp.bfloat16
     )
-    keyval_full = lax.all_gather(keyval_part, "tensor", axis=1, tiled=True)
+    (keyval_blocks,) = exchange("tensor", [keyval_part], [False], 1)
+    keyval_full = keyval_blocks.transpose(1, 0, 2).reshape(seq_length, keyval_total)
     group_slot = tensor_slot // devices_per_group
     key_block = lax.dynamic_slice_in_dim(keyval_full, group_slot * head_size, head_size, 1)
     value_block = lax.dynamic_slice_in_dim(
@@ -125,37 +191,39 @@
     grad_terms = lax.dynamic_update_slice_in_dim(
         grad_terms, grad_value, (kv_heads + group_slot) * head_size, 1
     )
-    grad_keyval = lax.psum_scatter(
-        grad_terms.astype(jnp.bfloat16), "tensor", scatter_dimension=1, tiled=True
-    )
-    result = lax.dot_general(
-        query_weight, grad_query, contract_last, preferred_element_type=jnp.float32
-    )
-    grad_normed = (
-        lax.psum_scatter(
-            (
-                result
-                + lax.dot_general(
-                    keyweight, grad_keyval, contract_last, preferred_element_type=jnp.float32
-                )
-            ).astype(jnp.bfloat16),
-            "tensor",
-            scatter_dimension=0,
-            tiled=True,
+    term_blocks = grad_terms.reshape(seq_length, tensor_count, group_cols).transpose(1, 0, 2)
+    (keyval_terms,) = exchange("tensor", [term_blocks], [True], 2)
+    grad_keyval = jnp.sum(keyval_terms, axis=0).astype(jnp.bfloat16)
+    query_weight_blocks = query_weight.reshape(tensor_count, local_cols, query_cols)
+    keyweight_blocks = keyweight.reshape(tensor_count, local_cols, group_cols)
+    normed_terms = (
+        jnp.einsum("rc,pkc->prk", grad_query, query_weight_blocks, preferred_element_type=jnp.float32)
+        + jnp.einsum(
+            "rc,pkc->prk", grad_keyval, keyweight_blocks, preferred_element_type=jnp.float32
         )
-        .astype(jnp.float32)
-        .T
-    )
+    ).astype(jnp.bfloat16)
+    unit_blocks = unit_full.reshape(seq_length, tensor_count, local_cols).transpose(1, 0, 2)
+    gain_blocks = gain.reshape(tensor_count, 1, local_cols)
+    product_part = jnp.sum(
+        normed_terms.astype(jnp.float32) * gain_blocks * unit_blocks, axis=(0, 2)
+    ).reshape(1, seq_length)
+    normed_sums, product_parts = exchange(
+        "tensor", [normed_terms, product_part], [True, False], 3
+    )
+    grad_normed = jnp.sum(normed_sums.astype(jnp.float32), axis=0)
+    product_sum = jnp.sum(product_parts, axis=0).reshape(seq_length, 1)
     scaled_grad = grad_normed * gain_local
-    product_sum = lax.psum(jnp.sum(scaled_grad * unit_rows, axis=1, keepdims=True), "tensor")
     grad_input = (inv_rms * (scaled_grad - unit_rows * (product_sum / model_width))).astype(
         jnp.bfloat16
     )
-    grad_gain = lax.psum(jnp.sum(grad_normed * unit_rows, axis=0), "dp")
-    keyval_all = lax.all_gather(grad_keyval, "dp", axis=0, tiled=True)
+    gain_part = jnp.sum(grad_normed * unit_rows, axis=0).reshape(1, local_cols)
+    (gain_parts,) = exchange("dp", [gain_part], [False], 4)
+    grad_gain = jnp.sum(gain_parts, axis=(0, 1))
+    (keyval_rows,) = exchange("dp", [grad_keyval], [False], 5)
+    keyval_all = keyval_rows.reshape(-1, group_cols)
     rows_normed = lax.all_to_all(normed_full, "dp", split_axis=1, concat_axis=0, tiled=True)
     keyval_weight_grad = lax.dot_general(
-        rows_normed, keyval_all, contract_first, preferred_element_type=jnp.float32
+        rows_normed, keyval_all, (((0,), (0,)), ((), ())), preferred_element_type=jnp.float32
     )
     return (grad_input, grad_gain, keyval_weight_grad.astype(jnp.bfloat16))
 

time: 639 us -> 471 us (0.74)
  waiting for transfers between devices: 384 us -> 176 us
  Pallas kernels: 0 us -> 196 us
  blocking collectives: 178 us -> 0 us
  local copies, waits for them, and re-layouts: 8.49 us -> 25.3 us
  other arithmetic: 10.9 us -> 23.6 us
    pallas_call x0 -> x6, Pallas kernels: none -> 196 us  [exchange(): pl.pallas_call(functools.partial(exchange_kernel, axis, n, tuple(per_peer...]
    reduce_scatter x2 -> x0, waiting for transfers between devices: 95.6 us -> none  [the longest x1 73.7 us: on_device(): lax.psum_scatter(grad_terms.astype(jnp.bfloat16), 'tensor', scatter_dimen...]
    psum x2 -> x0, blocking collectives: 94 us -> none  [the longest x1 64.5 us: on_device(): grad_gain = lax.psum(jnp.sum(grad_normed * unit_rows, axis=0), 'dp')]
    all_gather x2 -> x0, blocking collectives: 84.4 us -> none  [the longest x1 65.4 us: on_device(): keyval_all = lax.all_gather(grad_keyval, 'dp', axis=0, tiled=True)]
    all_gather x1 -> x0, waiting for transfers between devices: 68.3 us -> none  [on_device(): lax.all_gather(inputs, 'tensor', axis=1, tiled=True).astype(jnp.float32)]
    all_gather x1, waiting for transfers between devices: 220 us -> 176 us  [on_device(): weight_full = lax.all_gather(weight_block, 'dp', axis=0, tiled=True)]
    convert_element_type x0 -> x3, local copies, waits for them, and re-layouts: none -> 11.9 us  [the longest x2 11.1 us: on_device(): input_blocks.transpose(1, 0, 2).reshape(seq_length, model_width)]
    slice x0 -> x3, local copies, waits for them, and re-layouts: none -> 7.25 us  [the longest x1 7.25 us: on_device(): query_weight = weight_full[:, :query_cols]]
  transfers between devices with their start and end apart: 5 -> 2, of which waited for: 4 -> 1; matrix products, arithmetic and copies ran while one was open for 6% -> 14% of each run, Pallas kernels for 0% -> 42%
where the time goes in v2:
time: 471 us; the launch traced here: 470 us
  Pallas kernels  196 us (42%)
  waiting for transfers between devices  176 us (37%)
  local copies, waits for them, and re-layouts  25.3 us (5%)
  other arithmetic  23.6 us (5%)
  matrix products  23.4 us (5%)
  between operations  14.5 us (3%)
  starting transfers between devices  10.9 us (2%)
    pallas_call x6, Pallas kernels, exchange(): pl.pallas_call(functools.partial(exchange_kernel, axis, n, tuple(per_peer...  196 us
    all_gather x1, waiting for transfers between devices, on_device(): weight_full = lax.all_gather(weight_block, 'dp', axis=0, tiled=True)  176 us
    convert_element_type x2, local copies, waits for them, and re-layouts, on_device(): input_blocks.transpose(1, 0, 2).reshape(seq_length, model_width)  11.1 us
    all_to_all x1, starting transfers between devices, on_device(): lax.all_to_all(normed_full, 'dp', split_axis=1, concat_axis=0, tiled=True)  10.8 us
  transfers between devices with their start and end apart: 2, of which 1 were waited for; matrix products, arithmetic and copies ran while one was open for 14% of the time, Pallas kernels for 42%

profile of v2, /device:TPU:6, one launch (start us, length us, event | category | flops | bytes accessed | tf_op | source)
XLA Modules:
  0.0 470.0 jit_solution(10740675951146734926)
XLA Ops:
  8.1 1.7 pad_maximum_fusion
  9.8 41.7 %shard_map.76 = bf16[16,128,512]{2,1,0:T(8,128)(2,1)} custom-call(bf16[128,512]{1,0:T(8,128)(2,1)} %refs_0_.1), custom_call_target="tpu_custom_call" | custom-call | bytes 4194304 | tf_op jit(solution)/shard_map/pallas_call | solution.py:57
  51.5 4.2 convert_bitcast_fusion
  55.6 5.3 %copy.60 = f32[128,16,512]{0,2,1:T(8,128)} copy(f32[128,16,512]{2,0,1:T(8,128)} %convert_bitcast_fusion) | data formatting | bytes 8388608 | tf_op jit(solution)/shard_map/convert_element_type | solution.py:131
  61.0 5.8 %copy.88 = f32[128,32,256]{2,0,1:T(8,128)} copy(f32[128,32,256]{0,2,1:T(8,128)} %bitcast.99) | data formatting | bytes 8388608 | tf_op jit(solution)/shard_map/convert_element_type | solution.py:131
  67.3 4.2 multiply_convert_fusion
  71.5 10.8 %all-to-all-start = ((bf16[128,32,256]{2,0,1:T(8,128)(2,1)}), bf16[128,32,256]{2,0,1:T(8,128)(2,1)}, u32[]{:S(2)}, u32[]{:S(2)}) async-start(bf16[128,32,256]{2,0,1:T(8,128)(2,1)} %multiply_convert_fusion), calls=%async_computation | async-start | bytes 4194304 | tf_op jit(solution)/shard_map/all_to_all | solution.py:224
  83.8 3.9 fusion.4
  87.7 176.2 %all-gather.2.cloned.1.call-done = bf16[8192,576]{1,0:T(8,128)(2,1)} async-done(((bf16[256,576]{1,0:T(8,128)(2,1)}), bf16[8192,576]{1,0:T(8,128)(2,1)}) %all-gather.2.cloned.1.call-update) | async-done | bytes 9437200 | tf_op jit(solution)/shard_map/all_gather | solution.py:126
  263.9 3.1 convolution_convert_fusion.2
  267.7 14.6 %shard_map.77 = bf16[16,128,64]{2,1,0:T(8,128)(2,1)} custom-call(bf16[128,64]{1,0:T(8,128)(2,1)} %copy.61.refs_0_), custom_call_target="tpu_custom_call" | custom-call | bytes 524288 | tf_op jit(solution)/shard_map/pallas_call | solution.py:57
  284.3 5.3 %fusion.18 = f32[128,512]{1,0:T(8,128)S(1)} fusion(bf16[128,8192]{0,1:T(8,128)(2,1)} %fusion.4, bf16[8192,576]{1,0:T(8,128)(2,1)} %all-gather.2.cloned.1.call-done), kind=kOutput, calls=%fused_computation.30 | convolution fusion | flops 1073872896 | bytes 10747904 | tf_op jit(solution)/shard_map/dot_general | solution.py:138
  295.7 21.5 %shard_map.78 = f32[16,128,64]{2,1,0:T(8,128)} custom-call(f32[16,128,64]{2,1,0:T(8,128)} %bitcast.102), custom_call_target="tpu_custom_call" | custom-call | bytes 1048576 | tf_op jit(solution)/shard_map/pallas_call | solution.py:57
  317.2 1.9 reduce_sum.84.refs_0_
  319.2 55.3 %shard_map.81 = bf16[32,128,64]{2,1,0:T(8,128)(2,1)} custom-call(bf16[128,64]{1,0:T(8,128)(2,1)} %reduce_sum.84.refs_0_), custom_call_target="tpu_custom_call" | custom-call | bytes 1048576 | tf_op jit(solution)/shard_map/pallas_call | solution.py:57
  375.1 7.2 %slice.40 = bf16[8192,512]{1,0:T(8,128)(2,1)} slice(bf16[8192,576]{1,0:T(8,128)(2,1)} %all-gather.2.cloned.1.call-done), slice={[0:8192], [0:512]} | slice | bytes 16777216 | tf_op jit(solution)/shard_map/slice | solution.py:127
  382.4 6.4 %fusion.62 = f32[16,512,128]{1,2,0:T(8,128)S(1)} fusion(bf16[16,512,512]{2,1,0:T(8,128)(2,1)} %bitcast.100, bf16[128,512,1]{0,1,2:T(8,128)(2,1)S(1)} %bitcast.108), kind=kOutput, calls=%fused_computation.93 | convolution fusion | flops 1073741824 | bytes 12713984 | tf_op jit(solution)/shard_map/rc,pkc->prk/dot_general | solution.py:200
  388.8 3.0 fusion.2
  391.8 42.8 %shard_map.79 = (bf16[16,128,512]{2,1,0:T(8,128)(2,1)}, f32[16,1,128]{2,1,0:T(1,128)}) custom-call(bf16[16,128,512]{2,1,0:T(8,128)(2,1)} %get-tuple-element.22.refs_0_, f32[1,128]{1,0:T(1,128)} %bitcast.114), custom_call_target="tpu_custom_call" | custom-call | bytes 4210688 | tf_op jit(solution)/shard_map/pallas_call | solution.py:57
  435.3 1.9 convert_reduce_fusion
  437.3 1.4 multiply_reduce_fusion
  438.6 20.3 %shard_map.80 = f32[32,1,512]{2,1,0:T(1,128)} custom-call(f32[1,512]{1,0:T(1,128)} %bitcast.113), custom_call_target="tpu_custom_call" | custom-call | bytes 131072 | tf_op jit(solution)/shard_map/pallas_call | solution.py:57
  459.0 1.5 reduce_sum.89
  460.5 2.7 fusion.24
  (75 shorter events, 12.9 us)
Async XLA Ops:
  7.2 256.7 %all-gather.2.cloned.1.call-start = ((), (), s32[]{:S(2)}) async-start(), calls=%async_computation.1 | async-start | bytes 10813440 | tf_op jit(solution)/shard_map/all_gather | solution.py:126
  61.0 5.8 %copy-start.4 = (f32[8192]{0:T(1024)S(1)}, f32[8192]{0:T(1024)}, u32[]{:S(2)}) copy-start(f32[8192]{0:T(1024)} %param.7) | copy-start | bytes 98308
  61.0 5.8 %copy-start = (bf16[16,128,512]{2,1,0:T(8,128)(2,1)S(1)}, bf16[16,128,512]{2,1,0:T(8,128)(2,1)}, u32[]{:S(2)}) copy-start(bf16[16,128,512]{2,1,0:T(8,128)(2,1)} %shard_map.76) | copy-start | bytes 6291460
  67.3 16.5 %copy-start.13 = (f32[128]{0:T(128)}, f32[128]{0:T(128)S(1)}, u32[]{:S(2)}) copy-start(f32[128]{0:T(128)S(1)} %add_rsqrt_fusion) | copy-start | bytes 1540
  67.3 15.7 %copy-start.11 = (bf16[128,512]{1,0:T(8,128)(2,1)S(1)}, bf16[128,512]{1,0:T(8,128)(2,1)}, u32[]{:S(2)}) copy-start(bf16[128,512]{1,0:T(8,128)(2,1)} %param.6) | copy-start | bytes 393220
  71.5 388.9 %all-to-all-start = ((bf16[128,32,256]{2,0,1:T(8,128)(2,1)}), bf16[128,32,256]{2,0,1:T(8,128)(2,1)}, u32[]{:S(2)}, u32[]{:S(2)}) async-start(bf16[128,32,256]{2,0,1:T(8,128)(2,1)} %multiply_convert_fusion), calls=%async_computation | async-start | bytes 4194304 | tf_op jit(solution)/shard_map/all_to_all | solution.py:224
  83.8 205.9 %copy-start.15 = (f32[128]{0:T(128)}, f32[128]{0:T(128)S(1)}, u32[]{:S(2)}) copy-start(f32[128]{0:T(128)S(1)} %iota_convert_fusion) | copy-start | bytes 1540
  83.8 205.9 %copy-start.16 = (f32[64]{0:T(128)}, f32[64]{0:T(128)S(1)}, u32[]{:S(2)}) copy-start(f32[64]{0:T(128)S(1)} %multiply_exponential_fusion) | copy-start | bytes 772
  283.6 0.7 copy-start.3
  290.0 1.6 copy-start.7
  290.0 1.6 copy-start.9
  292.9 81.5 %copy-start.8 = (bf16[128,64]{1,0:T(8,128)(2,1)S(1)}, bf16[128,64]{1,0:T(8,128)(2,1)}, u32[]{:S(2)}) copy-start(bf16[128,64]{1,0:T(8,128)(2,1)} %copy-done.7) | copy-start | bytes 49156
  292.9 81.5 %copy-start.10 = (bf16[128,64]{1,0:T(8,128)(2,1)S(1)}, bf16[128,64]{1,0:T(8,128)(2,1)}, u32[]{:S(2)}) copy-start(bf16[128,64]{1,0:T(8,128)(2,1)} %copy-done.9) | copy-start | bytes 49156
  382.4 6.4 %slice-start = ((bf16[8192,576]{1,0:T(8,128)(2,1)}), bf16[8192,64]{1,0:T(8,128)(2,1)S(1)}, s32[]{:S(2)}) async-start(bf16[8192,576]{1,0:T(8,128)(2,1)} %all-gather.2.cloned.1.call-done), calls=%async_computation.2 | async-start | bytes 4194304 | tf_op jit(solution)/shard_map/slice | solution.py:128
  382.4 6.4 %copy-start.5 = (bf16[128,64]{1,0:T(8,128)(2,1)S(1)}, bf16[128,64]{1,0:T(8,128)(2,1)}, u32[]{:S(2)}) copy-start(bf16[128,64]{1,0:T(8,128)(2,1)} %reduce_sum.84.refs_0_) | copy-start | bytes 49156
  382.4 6.4 %copy-start.6 = (f32[16,512]{1,0:T(8,128)S(1)}, f32[16,512]{1,0:T(8,128)}, u32[]{:S(2)}) copy-start(f32[16,512]{1,0:T(8,128)} %mul.316) | copy-start | bytes 98308
  382.4 6.4 %copy-start.14 = (f32[128]{0:T(128)S(1)}, f32[128]{0:T(128)}, u32[]{:S(2)}) copy-start(f32[128]{0:T(128)} %copy-done.13) | copy-start | bytes 1540
  391.8 45.5 %copy-start.2 = (bf16[128,512]{1,0:T(8,128)(2,1)S(1)}, bf16[128,512]{1,0:T(8,128)(2,1)}, u32[]{:S(2)}) copy-start(bf16[128,512]{1,0:T(8,128)(2,1)} %refs_0_.1) | copy-start | bytes 393220
  391.8 45.5 %copy-start.12 = (f32[512]{0:T(512)S(1)}, f32[512]{0:T(512)}, u32[]{:S(2)}) copy-start(f32[512]{0:T(512)} %dynamic_slice.11) | copy-start | bytes 6148
  391.8 68.7 %copy-start.1 = (bf16[32,128,64]{2,1,0:T(8,128)(2,1)S(1)}, bf16[32,128,64]{2,1,0:T(8,128)(2,1)}, u32[]{:S(2)}) copy-start(bf16[32,128,64]{2,1,0:T(8,128)(2,1)} %shard_map.81) | copy-start | bytes 1572868
Sparse Core Ops, SparseCore 0:
  10.1 253.7 all-gather.1

commit v3 on v2

--- a/solution.py
+++ b/solution.py
@@ -68,6 +68,92 @@
     )(*blocks)
 
 
+def ring_gather_kernel(pair_count, ring_count, block_ref, out_ref, send_sems, recv_sems):
+    pair_slot = lax.axis_index("dp") // ring_count
+    ring_slot = lax.axis_index("dp") % ring_count
+    partner = (1 - pair_slot) * ring_count + ring_slot
+    right = pair_slot * ring_count + lax.rem(ring_slot + 1, ring_count)
+    left = pair_slot * ring_count + lax.rem(ring_slot + ring_count - 1, ring_count)
+    me = pair_slot * ring_count + ring_slot
+    barrier = pltpu.get_barrier_semaphore()
+    for peer in (partner, right, left):
+        pl.semaphore_signal(barrier, inc=1, device_id={"dp": peer}, device_id_type=MESH)
+    pl.semaphore_wait(barrier, 3)
+    swap = pltpu.make_async_remote_copy(
+        src_ref=block_ref,
+        dst_ref=out_ref.at[me],
+        send_sem=send_sems.at[2, 0, 0],
+        recv_sem=recv_sems.at[2, 0, 0],
+        device_id={"dp": partner},
+        device_id_type=MESH,
+    )
+    swap.start()
+    own = pltpu.make_async_copy(block_ref, out_ref.at[me], send_sems.at[2, 1, 0])
+    own.start()
+    own.wait()
+    swap.wait_send()
+    swap.wait_recv()
+    right_steps = ring_count // 2
+    left_steps = ring_count - 1 - right_steps
+    sent = []
+
+    def send(direction, step, target, origin):
+        copies = []
+        for member in range(pair_count):
+            slot = member * ring_count + origin
+            copy = pltpu.make_async_remote_copy(
+                src_ref=out_ref.at[slot],
+                dst_ref=out_ref.at[slot],
+                send_sem=send_sems.at[direction, step, member],
+                recv_sem=recv_sems.at[direction, step, member],
+                device_id={"dp": target},
+                device_id_type=MESH,
+            )
+            copy.start()
+            copies.append(copy)
+        sent.extend(copies)
+        return copies
+
+    right_copies = send(0, 0, right, ring_slot)
+    left_copies = send(1, 0, left, ring_slot) if left_steps > 0 else []
+    for step in range(1, right_steps):
+        for copy in right_copies:
+            copy.wait_recv()
+        origin = lax.rem(ring_slot + ring_count - step, ring_count)
+        right_copies = send(0, step, right, origin)
+        if step < left_steps:
+            for copy in left_copies:
+                copy.wait_recv()
+            origin = lax.rem(ring_slot + step, ring_count)
+            left_copies = send(1, step, left, origin)
+    for copy in right_copies + left_copies:
+        copy.wait_recv()
+    for copy in sent:
+        copy.wait_send()
+
+
+def ring_gather(block, collective_id):
+    count = lax.axis_size("dp")
+    pair_count = 2
+    ring_count = count // pair_count
+    return pl.pallas_call(
+        functools.partial(ring_gather_kernel, pair_count, ring_count),
+        out_shape=jax.ShapeDtypeStruct((count,) + block.shape, block.dtype),
+        in_specs=[pl.BlockSpec(memory_space=pltpu.VMEM)],
+        out_specs=pl.BlockSpec(memory_space=pltpu.VMEM),
+        scratch_shapes=[
+            pltpu.SemaphoreType.DMA((3, ring_count, pair_count)),
+            pltpu.SemaphoreType.DMA((3, ring_count, pair_count)),
+        ],
+        compiler_params=pltpu.CompilerParams(
+            collective_id=collective_id, has_side_effects=True, vmem_limit_bytes=48 * 1024 * 1024
+        ),
+        cost_estimate=pl.CostEstimate(
+            flops=0, bytes_accessed=2 * count * block.size * block.dtype.itemsize, transcendentals=0
+        ),
+    )(block)
+
+
 HD = 128
 KV_HEADS = 4
 HEADS_DEV = 4
@@ -123,7 +209,7 @@
     tensor_slot = lax.axis_index("tensor")
     gain_local = lax.dynamic_slice_in_dim(gain, tensor_slot * local_cols, local_cols, 0)
     weight_block = jnp.concatenate([w_query, w_keyval], axis=1)
-    weight_full = lax.all_gather(weight_block, "dp", axis=0, tiled=True)
+    weight_full = ring_gather(weight_block, 6).reshape(-1, weight_block.shape[1])
     query_weight = weight_full[:, :query_cols]
     keyweight = weight_full[:, query_cols:]
     (input_blocks,) = exchange("tensor", [inputs], [False], 0)

time: 471 us -> 501 us (1.064)
  Pallas kernels: 196 us -> 416 us
  waiting for transfers between devices: 176 us -> 0.01 us
  between operations: 14.5 us -> 1.03 us
    pallas_call x0 -> x1, Pallas kernels: none -> 222 us  [ring_gather(): pl.pallas_call(functools.partial(ring_gather_kernel, pair_count, ring_cou...]
    all_gather x1 -> x0, waiting for transfers between devices: 176 us -> none  [on_device(): weight_full = lax.all_gather(weight_block, 'dp', axis=0, tiled=True)]
  transfers between devices with their start and end apart: 2 -> 1, of which waited for: 1 -> 0; matrix products, arithmetic and copies ran while one was open for 14% -> 9% of each run, Pallas kernels for 42% -> 76%
where the time goes in v3:
time: 501 us; the launch traced here: 500 us
  Pallas kernels  416 us (83%)
  local copies, waits for them, and re-layouts  27.9 us (6%)
  other arithmetic  21.8 us (4%)
  matrix products  20.1 us (4%)
  starting transfers between devices  12.9 us (3%)
    pallas_call x1, Pallas kernels, ring_gather(): pl.pallas_call(functools.partial(ring_gather_kernel, pair_count, ring_cou...  222 us
    pallas_call x6, Pallas kernels, exchange(): pl.pallas_call(functools.partial(exchange_kernel, axis, n, tuple(per_peer...  194 us
    all_to_all x1, starting transfers between devices, on_device(): lax.all_to_all(normed_full, 'dp', split_axis=1, concat_axis=0, tiled=True)  12.9 us
    convert_element_type x2, local copies, waits for them, and re-layouts, on_device(): input_blocks.transpose(1, 0, 2).reshape(seq_length, model_width)  11 us
  transfers between devices with their start and end apart: 1, of which 0 were waited for; matrix products, arithmetic and copies ran while one was open for 9% of the time, Pallas kernels for 76%

profile of v3, /device:TPU:6, one launch (start us, length us, event | category | flops | bytes accessed | tf_op | source)
XLA Modules:
  0.0 499.7 jit_solution(3767144320379216156)
XLA Ops:
  0.6 37.6 %shard_map.76 = bf16[16,128,512]{2,1,0:T(8,128)(2,1)} custom-call(bf16[128,512]{1,0:T(8,128)(2,1)} %refs_0_.1), custom_call_target="tpu_custom_call" | custom-call | bytes 4194304 | tf_op jit(solution)/shard_map/pallas_call | solution.py:57
  38.3 2.1 fusion
  40.4 4.1 convert_bitcast_fusion
  44.5 5.4 %copy.60 = f32[128,16,512]{0,2,1:T(8,128)} copy(f32[128,16,512]{2,0,1:T(8,128)} %convert_bitcast_fusion) | data formatting | bytes 8388608 | tf_op jit(solution)/shard_map/convert_element_type | solution.py:217
  49.9 5.6 %copy.88 = f32[128,32,256]{2,0,1:T(8,128)} copy(f32[128,32,256]{0,2,1:T(8,128)} %bitcast.102) | data formatting | bytes 8388608 | tf_op jit(solution)/shard_map/convert_element_type | solution.py:217
  55.5 4.2 multiply_convert_fusion
  59.7 12.9 %all-to-all-start = ((bf16[128,32,256]{2,0,1:T(8,128)(2,1)}), bf16[128,32,256]{2,0,1:T(8,128)(2,1)}, u32[]{:S(2)}, u32[]{:S(2)}) async-start(bf16[128,32,256]{2,0,1:T(8,128)(2,1)} %multiply_convert_fusion), calls=%async_computation | async-start | bytes 4194304 | tf_op jit(solution)/shard_map/all_to_all | solution.py:310
  72.8 221.7 %shard_map.77 = bf16[32,256,576]{2,1,0:T(8,128)(2,1)} custom-call(bf16[256,576]{1,0:T(8,128)(2,1)S(1)} %pad_maximum_fusion.block_ref), custom_call_target="tpu_custom_call" | custom-call | bytes 18874368 | tf_op jit(solution)/shard_map/pallas_call | solution.py:139
  294.4 3.1 slice.41
  297.5 7.3 %slice.40 = bf16[8192,512]{1,0:T(8,128)(2,1)} slice(bf16[8192,576]{1,0:T(8,128)(2,1)} %bitcast.99), slice={[0:8192], [0:512]} | slice | bytes 16777216 | tf_op jit(solution)/shard_map/slice | solution.py:213
  305.0 2.9 fusion.4
  307.9 4.7 fusion.18
  312.7 2.3 convolution_convert_fusion.2
  315.7 17.5 %shard_map.78 = bf16[16,128,64]{2,1,0:T(8,128)(2,1)} custom-call(bf16[128,64]{1,0:T(8,128)(2,1)} %copy.62.refs_0_), custom_call_target="tpu_custom_call" | custom-call | bytes 524288 | tf_op jit(solution)/shard_map/pallas_call | solution.py:57
  339.1 20.9 %shard_map.79 = f32[16,128,64]{2,1,0:T(8,128)} custom-call(f32[16,128,64]{2,1,0:T(8,128)} %bitcast.105), custom_call_target="tpu_custom_call" | custom-call | bytes 1048576 | tf_op jit(solution)/shard_map/pallas_call | solution.py:57
  360.0 1.9 reduce_sum.84.refs_0_
  361.9 56.6 %shard_map.82 = bf16[32,128,64]{2,1,0:T(8,128)(2,1)} custom-call(bf16[128,64]{1,0:T(8,128)(2,1)} %reduce_sum.84.refs_0_), custom_call_target="tpu_custom_call" | custom-call | bytes 1048576 | tf_op jit(solution)/shard_map/pallas_call | solution.py:57
  418.5 2.2 copy.84
  421.4 8.2 %fusion.2 = (f32[128]{0:T(128)}, bf16[16,128,512]{2,1,0:T(8,128)(2,1)}) fusion(bf16[16,128,512]{2,1,0:T(8,128)(2,1)S(1)} %copy-done, f32[128]{0:T(128)S(1)} %add_rsqrt_fusion, f32[16,512]{1,0:T(8,128)S(1)} %mul.316, f32[16,512,128]{1,2,0:T(8,128)S(1)} %fusion.47, bf16[16,512,512]{2,1,0:T(8,128)(2,1)} %bitcast.103, bf16[128,512,1]{0,1,2:T(8,128)(2,1)S(1)} %bitcast.111), kind=kOutput, calls=%fused_computation.5 | convolution fusion | flops 1082130304 | bytes 16942080 | tf_op jit(solution)/shard_map/rc,pkc->prk/dot_general | solution.py:286
  429.7 42.8 %shard_map.80 = (bf16[16,128,512]{2,1,0:T(8,128)(2,1)}, f32[16,1,128]{2,1,0:T(1,128)}) custom-call(bf16[16,128,512]{2,1,0:T(8,128)(2,1)} %get-tuple-element.22.refs_0_, f32[1,128]{1,0:T(1,128)} %bitcast.117), custom_call_target="tpu_custom_call" | custom-call | bytes 4210688 | tf_op jit(solution)/shard_map/pallas_call | solution.py:57
  473.2 1.9 convert_reduce_fusion
  476.5 18.9 %shard_map.81 = f32[32,1,512]{2,1,0:T(1,128)} custom-call(f32[1,512]{1,0:T(1,128)} %bitcast.116), custom_call_target="tpu_custom_call" | custom-call | bytes 131072 | tf_op jit(solution)/shard_map/pallas_call | solution.py:57
  495.5 1.5 reduce_sum.89
  497.0 2.7 fusion.24
  (55 shorter events, 9.7 us)
Async XLA Ops:
  38.3 6.2 %copy-start.3 = (f32[8192]{0:T(1024)S(1)}, f32[8192]{0:T(1024)}, u32[]{:S(2)}) copy-start(f32[8192]{0:T(1024)} %param.7) | copy-start | bytes 98308
  55.4 17.2 %copy-start.7 = (bf16[256,64]{0,1:T(8,128)(2,1)S(1)}, bf16[256,64]{0,1:T(8,128)(2,1)}, u32[]{:S(2)}) copy-start(bf16[256,64]{0,1:T(8,128)(2,1)} %param.9) | copy-start | bytes 98308
  55.5 17.3 %copy-start.5 = (bf16[256,512]{1,0:T(8,128)(2,1)S(1)}, bf16[256,512]{1,0:T(8,128)(2,1)}, u32[]{:S(2)}) copy-start(bf16[256,512]{1,0:T(8,128)(2,1)} %param.8) | copy-start | bytes 786436
  59.7 437.3 %all-to-all-start = ((bf16[128,32,256]{2,0,1:T(8,128)(2,1)}), bf16[128,32,256]{2,0,1:T(8,128)(2,1)}, u32[]{:S(2)}, u32[]{:S(2)}) async-start(bf16[128,32,256]{2,0,1:T(8,128)(2,1)} %multiply_convert_fusion), calls=%async_computation | async-start | bytes 4194304 | tf_op jit(solution)/shard_map/all_to_all | solution.py:310
  297.5 7.4 %copy-start.6 = (bf16[128,512]{1,0:T(8,128)(2,1)S(1)}, bf16[128,512]{1,0:T(8,128)(2,1)}, u32[]{:S(2)}) copy-start(bf16[128,512]{1,0:T(8,128)(2,1)} %param.6) | copy-start | bytes 393220
  361.9 58.8 %copy-start.4 = (bf16[128,64]{1,0:T(8,128)(2,1)S(1)}, bf16[128,64]{1,0:T(8,128)(2,1)}, u32[]{:S(2)}) copy-start(bf16[128,64]{1,0:T(8,128)(2,1)} %reduce_sum.84.refs_0_) | copy-start | bytes 49156
  418.5 2.9 copy-start
  429.7 45.5 %copy-start.2 = (bf16[128,512]{1,0:T(8,128)(2,1)S(1)}, bf16[128,512]{1,0:T(8,128)(2,1)}, u32[]{:S(2)}) copy-start(bf16[128,512]{1,0:T(8,128)(2,1)} %refs_0_.1) | copy-start | bytes 393220
  429.7 67.3 %copy-start.1 = (bf16[32,128,64]{2,1,0:T(8,128)(2,1)S(1)}, bf16[32,128,64]{2,1,0:T(8,128)(2,1)}, u32[]{:S(2)}) copy-start(bf16[32,128,64]{2,1,0:T(8,128)(2,1)} %shard_map.82) | copy-start | bytes 1572868

commit v4 on v3

--- a/solution.py
+++ b/solution.py
@@ -208,10 +208,10 @@
     score_scale = head_size ** (-0.5)
     tensor_slot = lax.axis_index("tensor")
     gain_local = lax.dynamic_slice_in_dim(gain, tensor_slot * local_cols, local_cols, 0)
-    weight_block = jnp.concatenate([w_query, w_keyval], axis=1)
-    weight_full = ring_gather(weight_block, 6).reshape(-1, weight_block.shape[1])
-    query_weight = weight_full[:, :query_cols]
-    keyweight = weight_full[:, query_cols:]
+    split_cols = query_cols // 2
+    engine_block = jnp.concatenate([w_query[:, :split_cols], w_keyval], axis=1)
+    engine_full = lax.all_gather(engine_block, "dp", axis=0, tiled=True)
+    ring_full = ring_gather(w_query[:, split_cols:], 6).reshape(-1, query_cols - split_cols)
     (input_blocks,) = exchange("tensor", [inputs], [False], 0)
     inputs_full = (
         input_blocks.transpose(1, 0, 2).reshape(seq_length, model_width).astype(jnp.float32)
@@ -221,12 +221,14 @@
     unit_full = inputs_full * inv_rms
     normed_full = (unit_full * gain[None, :]).astype(jnp.bfloat16)
     unit_rows = inputs.astype(jnp.float32) * inv_rms
-    query_proj = jnp.dot(normed_full, query_weight, preferred_element_type=jnp.float32).astype(
+    engine_proj = jnp.dot(normed_full, engine_full, preferred_element_type=jnp.float32).astype(
         jnp.bfloat16
     )
-    keyval_part = jnp.dot(normed_full, keyweight, preferred_element_type=jnp.float32).astype(
+    ring_proj = jnp.dot(normed_full, ring_full, preferred_element_type=jnp.float32).astype(
         jnp.bfloat16
     )
+    query_proj = jnp.concatenate([engine_proj[:, :split_cols], ring_proj], axis=1)
+    keyval_part = engine_proj[:, split_cols:]
     (keyval_blocks,) = exchange("tensor", [keyval_part], [False], 1)
     keyval_full = keyval_blocks.transpose(1, 0, 2).reshape(seq_length, keyval_total)
     group_slot = tensor_slot // devices_per_group
@@ -280,12 +282,16 @@
     term_blocks = grad_terms.reshape(seq_length, tensor_count, group_cols).transpose(1, 0, 2)
     (keyval_terms,) = exchange("tensor", [term_blocks], [True], 2)
     grad_keyval = jnp.sum(keyval_terms, axis=0).astype(jnp.bfloat16)
-    query_weight_blocks = query_weight.reshape(tensor_count, local_cols, query_cols)
-    keyweight_blocks = keyweight.reshape(tensor_count, local_cols, group_cols)
+    engine_blocks = engine_full.reshape(tensor_count, local_cols, split_cols + group_cols)
+    ring_blocks = ring_full.reshape(tensor_count, local_cols, query_cols - split_cols)
+    engine_grads = jnp.concatenate([grad_query[:, :split_cols], grad_keyval], axis=1)
     normed_terms = (
-        jnp.einsum("rc,pkc->prk", grad_query, query_weight_blocks, preferred_element_type=jnp.float32)
+        jnp.einsum("rc,pkc->prk", engine_grads, engine_blocks, preferred_element_type=jnp.float32)
         + jnp.einsum(
-            "rc,pkc->prk", grad_keyval, keyweight_blocks, preferred_element_type=jnp.float32
+            "rc,pkc->prk",
+            grad_query[:, split_cols:],
+            ring_blocks,
+            preferred_element_type=jnp.float32,
         )
     ).astype(jnp.bfloat16)
     unit_blocks = unit_full.reshape(seq_length, tensor_count, local_cols).transpose(1, 0, 2)
@@ -307,7 +313,8 @@
     grad_gain = jnp.sum(gain_parts, axis=(0, 1))
     (keyval_rows,) = exchange("dp", [grad_keyval], [False], 5)
     keyval_all = keyval_rows.reshape(-1, group_cols)
-    rows_normed = lax.all_to_all(normed_full, "dp", split_axis=1, concat_axis=0, tiled=True)
+    normed_late, _ = lax.optimization_barrier((normed_full, grad_keyval))
+    rows_normed = lax.all_to_all(normed_late, "dp", split_axis=1, concat_axis=0, tiled=True)
     keyval_weight_grad = lax.dot_general(
         rows_normed, keyval_all, (((0,), (0,)), ((), ())), preferred_element_type=jnp.float32
     )

time: 501 us -> 478 us (0.954)
  Pallas kernels: 416 us -> 387 us
  between operations: 1.03 us -> 14.5 us
  local copies, waits for them, and re-layouts: 27.9 us -> 22.1 us
    pallas_call x1, Pallas kernels: 222 us -> 105 us  [ring_gather(): pl.pallas_call(functools.partial(ring_gather_kernel, pair_count, ring_cou...]
    pallas_call x6, Pallas kernels: 194 us -> 282 us  [exchange(): pl.pallas_call(functools.partial(exchange_kernel, axis, n, tuple(per_peer...]
    slice x2 -> x3, local copies, waits for them, and re-layouts: 7.49 us -> 1.61 us  [the longest x1 0.99 us: on_device(): w_query[:, split_cols:]]
    convert_element_type x2 -> x1, local copies, waits for them, and re-layouts: 11 us -> 5.47 us  [on_device(): input_blocks.transpose(1, 0, 2).reshape(seq_length, model_width)]
  transfers between devices with their start and end apart: 1 -> 2, of which waited for: 0 -> 0; matrix products, arithmetic and copies ran while one was open for 9% -> 8% of each run, Pallas kernels for 76% -> 74%
where the time goes in v4:
time: 478 us; the launch traced here: 477 us
  Pallas kernels  387 us (81%)
  local copies, waits for them, and re-layouts  22.1 us (5%)
  matrix products  21.6 us (5%)
  other arithmetic  18.4 us (4%)
  between operations  14.5 us (3%)
  starting transfers between devices  13 us (3%)
    pallas_call x6, Pallas kernels, exchange(): pl.pallas_call(functools.partial(exchange_kernel, axis, n, tuple(per_peer...  282 us
    pallas_call x1, Pallas kernels, ring_gather(): pl.pallas_call(functools.partial(ring_gather_kernel, pair_count, ring_cou...  105 us
    all_to_all x1, starting transfers between devices, on_device(): lax.all_to_all(normed_late, 'dp', split_axis=1, concat_axis=0, tiled=True)  12.9 us
  transfers between devices with their start and end apart: 2, of which 0 were waited for; matrix products, arithmetic and copies ran while one was open for 8% of the time, Pallas kernels for 74%

profile of v4, /device:TPU:6, one launch (start us, length us, event | category | flops | bytes accessed | tf_op | source)
XLA Modules:
  0.0 476.7 jit_solution(2299541209627492668)
XLA Ops:
  9.8 41.7 %shard_map.76 = bf16[16,128,512]{2,1,0:T(8,128)(2,1)} custom-call(bf16[128,512]{1,0:T(8,128)(2,1)} %refs_0_.1), custom_call_target="tpu_custom_call" | custom-call | bytes 4194304 | tf_op jit(solution)/shard_map/pallas_call | solution.py:57
  51.5 4.2 convert_bitcast_fusion
  55.7 5.5 %copy.31 = f32[128,16,512]{0,2,1:T(8,128)} copy(f32[128,16,512]{2,0,1:T(8,128)} %convert_bitcast_fusion) | data formatting | bytes 8388608 | tf_op jit(solution)/shard_map/convert_element_type | solution.py:217
  61.7 2.0 fusion.8
  63.7 4.0 copy.35
  67.6 105.2 %shard_map.78 = bf16[32,256,256]{2,1,0:T(8,128)(2,1)S(1)} custom-call(bf16[256,256]{1,0:T(8,128)(2,1)S(1)} %get-tuple-element.15.block_ref), custom_call_target="tpu_custom_call" | custom-call | bytes 8388608 | tf_op jit(solution)/shard_map/pallas_call | solution.py:139
  172.9 2.0 copy-done
  175.1 3.9 fusion.26
  179.1 2.5 fusion.7
  181.6 4.7 convolution_convert_fusion.1
  186.9 14.6 %shard_map.77 = bf16[16,128,64]{2,1,0:T(8,128)(2,1)} custom-call(bf16[128,64]{1,0:T(8,128)(2,1)} %slice.56.refs_0_), custom_call_target="tpu_custom_call" | custom-call | bytes 524288 | tf_op jit(solution)/shard_map/pallas_call | solution.py:57
  206.6 20.8 %shard_map.79 = f32[16,128,64]{2,1,0:T(8,128)} custom-call(f32[16,128,64]{2,1,0:T(8,128)} %bitcast.124), custom_call_target="tpu_custom_call" | custom-call | bytes 1048576 | tf_op jit(solution)/shard_map/pallas_call | solution.py:57
  227.4 1.9 reduce_sum.84.refs_0_
  229.4 4.1 copy.58
  233.5 12.9 %all-to-all-start = ((bf16[128,32,256]{2,0,1:T(8,128)(2,1)}), bf16[128,32,256]{2,0,1:T(8,128)(2,1)}, u32[]{:S(2)}, u32[]{:S(2)}) async-start(bf16[128,32,256]{2,0,1:T(8,128)(2,1)} %copy.58), calls=%async_computation | async-start | bytes 4194304 | tf_op jit(solution)/shard_map/all_to_all | solution.py:317
  247.2 147.4 %shard_map.82 = bf16[32,128,64]{2,1,0:T(8,128)(2,1)} custom-call(bf16[128,64]{1,0:T(8,128)(2,1)} %reduce_sum.84.refs_0_), custom_call_target="tpu_custom_call" | custom-call | bytes 1048576 | tf_op jit(solution)/shard_map/pallas_call | solution.py:57
  395.4 5.0 %fusion.40 = f32[16,512,128]{1,2,0:T(8,128)S(1)} fusion(bf16[16,512,320]{2,1,0:T(8,128)(2,1)} %bitcast.121, bf16[128,64]{0,1:T(8,128)(2,1)S(1)} %copy.54, bf16[128,256]{0,1:T(8,128)(2,1)S(1)} %slice.64), kind=kOutput, calls=%fused_computation.64 | convolution fusion | flops 671252480 | bytes 9519104 | tf_op jit(solution)/shard_map/rc,pkc->prk/dot_general | solution.py:289
  400.5 3.7 fusion.3
  404.2 41.4 %shard_map.80 = (bf16[16,128,512]{2,1,0:T(8,128)(2,1)}, f32[16,1,128]{2,1,0:T(1,128)}) custom-call(bf16[16,128,512]{2,1,0:T(8,128)(2,1)} %get-tuple-element.24.refs_0_, f32[1,128]{1,0:T(1,128)} %bitcast.137), custom_call_target="tpu_custom_call" | custom-call | bytes 4210688 | tf_op jit(solution)/shard_map/pallas_call | solution.py:57
  446.3 1.9 convert_reduce_fusion
  448.3 1.4 multiply_reduce_fusion
  449.6 16.0 %shard_map.81 = f32[32,1,512]{2,1,0:T(1,128)} custom-call(f32[1,512]{1,0:T(1,128)} %bitcast.136), custom_call_target="tpu_custom_call" | custom-call | bytes 131072 | tf_op jit(solution)/shard_map/pallas_call | solution.py:57
  465.6 1.5 reduce_sum.89
  467.1 2.7 fusion.27
  (72 shorter events, 11.1 us)
Async XLA Ops:
  7.2 174.4 %all-gather.2.cloned.1.call-start = ((), (), s32[]{:S(2)}) async-start(), calls=%async_computation.1 | async-start | bytes 6488064 | tf_op jit(solution)/shard_map/all_gather | solution.py:213
  55.7 5.5 %copy-start.9 = (f32[8192]{0:T(1024)S(1)}, f32[8192]{0:T(1024)}, u32[]{:S(2)}) copy-start(f32[8192]{0:T(1024)} %param.7) | copy-start | bytes 98308
  55.7 5.5 %copy-start.2 = (bf16[16,128,512]{2,1,0:T(8,128)(2,1)S(1)}, bf16[16,128,512]{2,1,0:T(8,128)(2,1)}, u32[]{:S(2)}) copy-start(bf16[16,128,512]{2,1,0:T(8,128)(2,1)} %shard_map.76) | copy-start | bytes 6291460
  61.2 6.4 %copy-start.6 = (f32[16,512]{1,0:T(8,128)}, f32[16,512]{1,0:T(8,128)S(1)}, u32[]{:S(2)}) copy-start(f32[16,512]{1,0:T(8,128)S(1)} %mul.295) | copy-start | bytes 98308
  63.7 111.2 %copy-start.14 = (bf16[128,512]{1,0:T(8,128)(2,1)S(1)}, bf16[128,512]{1,0:T(8,128)(2,1)}, u32[]{:S(2)}) copy-start(bf16[128,512]{1,0:T(8,128)(2,1)} %param.6) | copy-start | bytes 393220
  172.9 2.0 copy-start
  175.0 4.0 copy-start.3
  203.3 0.7 copy-start.10
  203.3 0.7 copy-start.12
  229.4 165.3 %copy-start.8 = (bf16[128,64]{1,0:T(8,128)(2,1)S(1)}, bf16[128,64]{1,0:T(8,128)(2,1)}, u32[]{:S(2)}) copy-start(bf16[128,64]{1,0:T(8,128)(2,1)} %reduce_sum.84.refs_0_) | copy-start | bytes 49156
  229.4 165.4 %copy-start.11 = (bf16[128,64]{1,0:T(8,128)(2,1)S(1)}, bf16[128,64]{1,0:T(8,128)(2,1)}, u32[]{:S(2)}) copy-start(bf16[128,64]{1,0:T(8,128)(2,1)} %copy-done.10) | copy-start | bytes 49156
  229.4 165.4 %copy-start.13 = (bf16[128,64]{1,0:T(8,128)(2,1)S(1)}, bf16[128,64]{1,0:T(8,128)(2,1)}, u32[]{:S(2)}) copy-start(bf16[128,64]{1,0:T(8,128)(2,1)} %copy-done.12) | copy-start | bytes 49156
  233.5 233.7 %all-to-all-start = ((bf16[128,32,256]{2,0,1:T(8,128)(2,1)}), bf16[128,32,256]{2,0,1:T(8,128)(2,1)}, u32[]{:S(2)}, u32[]{:S(2)}) async-start(bf16[128,32,256]{2,0,1:T(8,128)(2,1)} %copy.58), calls=%async_computation | async-start | bytes 4194304 | tf_op jit(solution)/shard_map/all_to_all | solution.py:317
  395.4 5.0 %copy-start.1 = (bf16[32,256,256]{2,1,0:T(8,128)(2,1)S(1)}, bf16[32,256,256]{2,1,0:T(8,128)(2,1)}, u32[]{:S(2)}) copy-start(bf16[32,256,256]{2,1,0:T(8,128)(2,1)} %copy-done) | copy-start | bytes 12582916
  395.4 5.0 %copy-start.7 = (f32[16,512]{1,0:T(8,128)S(1)}, f32[16,512]{1,0:T(8,128)}, u32[]{:S(2)}) copy-start(f32[16,512]{1,0:T(8,128)} %copy-done.6) | copy-start | bytes 98308
  404.2 44.0 %copy-start.5 = (bf16[128,512]{1,0:T(8,128)(2,1)S(1)}, bf16[128,512]{1,0:T(8,128)(2,1)}, u32[]{:S(2)}) copy-start(bf16[128,512]{1,0:T(8,128)(2,1)} %refs_0_.1) | copy-start | bytes 393220
  404.2 62.9 %copy-start.4 = (bf16[32,128,64]{2,1,0:T(8,128)(2,1)S(1)}, bf16[32,128,64]{2,1,0:T(8,128)(2,1)}, u32[]{:S(2)}) copy-start(bf16[32,128,64]{2,1,0:T(8,128)(2,1)} %shard_map.82) | copy-start | bytes 1572868
Sparse Core Ops, SparseCore 0:
  10.1 167.4 all-gather.1

commit v5 on v4

--- a/solution.py
+++ b/solution.py
@@ -11,19 +11,25 @@
 MESH = pl.DeviceIdType.MESH
 
 
-def exchange_kernel(axis, n, per_peer, *refs):
+def exchange_kernel(axes, sizes, per_peer, *refs):
     count = len(per_peer)
     src_refs = refs[:count]
     out_refs = refs[count : 2 * count]
     send_sems, recv_sems = refs[2 * count :]
-    me = lax.axis_index(axis)
     barrier = pltpu.get_barrier_semaphore()
-    for step in range(1, n):
-        peer = lax.rem(me + step, n)
-        pl.semaphore_signal(barrier, inc=1, device_id={axis: peer}, device_id_type=MESH)
-    pl.semaphore_wait(barrier, n - 1)
+    waits = 0
+    for axis in dict.fromkeys(axes):
+        n = sizes[axes.index(axis)]
+        me = lax.axis_index(axis)
+        for step in range(1, n):
+            peer = lax.rem(me + step, n)
+            pl.semaphore_signal(barrier, inc=1, device_id={axis: peer}, device_id_type=MESH)
+        waits += n - 1
+    pl.semaphore_wait(barrier, waits)
     copies = []
     for index in range(count):
+        axis, n = axes[index], sizes[index]
+        me = lax.axis_index(axis)
         for step in range(1, n):
             peer = lax.rem(me + step, n)
             source = src_refs[index].at[peer] if per_peer[index] else src_refs[index]
@@ -38,6 +44,7 @@
             copy.start()
             copies.append(copy)
     for index in range(count):
+        me = lax.axis_index(axes[index])
         own = src_refs[index][me] if per_peer[index] else src_refs[index][...]
         out_refs[index][me] = own
     for copy in copies:
@@ -46,26 +53,34 @@
         copy.wait_recv()
 
 
-def exchange(axis, blocks, per_peer, collective_id):
-    n = lax.axis_size(axis)
+def exchange_multi(items, collective_id):
+    axes = tuple(axis for axis, _, _ in items)
+    sizes = tuple(lax.axis_size(axis) for axis in axes)
+    blocks = [block for _, block, _ in items]
+    per_peer = tuple(spread for _, _, spread in items)
     out_shapes = []
-    for block, spread in zip(blocks, per_peer):
+    sent = 0
+    for n, block, spread in zip(sizes, blocks, per_peer):
         shape = block.shape[1:] if spread else block.shape
         out_shapes.append(jax.ShapeDtypeStruct((n,) + tuple(shape), block.dtype))
+        sent += block.size * block.dtype.itemsize * (1 if spread else n)
     count = len(blocks)
-    sent = sum(b.size * b.dtype.itemsize * (1 if s else n) for b, s in zip(blocks, per_peer))
     return pl.pallas_call(
-        functools.partial(exchange_kernel, axis, n, tuple(per_peer)),
+        functools.partial(exchange_kernel, axes, sizes, per_peer),
         out_shape=tuple(out_shapes),
         in_specs=[pl.BlockSpec(memory_space=pltpu.VMEM)] * count,
         out_specs=tuple(pl.BlockSpec(memory_space=pltpu.VMEM) for _ in range(count)),
         scratch_shapes=[
-            pltpu.SemaphoreType.DMA((count, n)),
-            pltpu.SemaphoreType.DMA((count, n)),
+            pltpu.SemaphoreType.DMA((count, max(sizes))),
+            pltpu.SemaphoreType.DMA((count, max(sizes))),
         ],
         compiler_params=pltpu.CompilerParams(collective_id=collective_id, has_side_effects=True),
         cost_estimate=pl.CostEstimate(flops=0, bytes_accessed=2 * sent, transcendentals=0),
     )(*blocks)
+
+
+def exchange(axis, blocks, per_peer, collective_id):
+    return exchange_multi([(axis, b, s) for b, s in zip(blocks, per_peer)], collective_id)
 
 
 def ring_gather_kernel(pair_count, ring_count, block_ref, out_ref, send_sems, recv_sems):
@@ -299,8 +314,18 @@
     product_part = jnp.sum(
         normed_terms.astype(jnp.float32) * gain_blocks * unit_blocks, axis=(0, 2)
     ).reshape(1, seq_length)
-    normed_sums, product_parts = exchange(
-        "tensor", [normed_terms, product_part], [True, False], 3
+    keyval_partials = (
+        jnp.einsum("rk,rc->kc", normed_full, grad_keyval, preferred_element_type=jnp.float32)
+        .astype(jnp.bfloat16)
+        .reshape(lax.axis_size("dp"), -1, group_cols)
+    )
+    normed_sums, product_parts, keyval_sums = exchange_multi(
+        [
+            ("tensor", normed_terms, True),
+            ("tensor", product_part, False),
+            ("dp", keyval_partials, True),
+        ],
+        3,
     )
     grad_normed = jnp.sum(normed_sums.astype(jnp.float32), axis=0)
     product_sum = jnp.sum(product_parts, axis=0).reshape(seq_length, 1)
@@ -311,13 +336,7 @@
     gain_part = jnp.sum(grad_normed * unit_rows, axis=0).reshape(1, local_cols)
     (gain_parts,) = exchange("dp", [gain_part], [False], 4)
     grad_gain = jnp.sum(gain_parts, axis=(0, 1))
-    (keyval_rows,) = exchange("dp", [grad_keyval], [False], 5)
-    keyval_all = keyval_rows.reshape(-1, group_cols)
-    normed_late, _ = lax.optimization_barrier((normed_full, grad_keyval))
-    rows_normed = lax.all_to_all(normed_late, "dp", split_axis=1, concat_axis=0, tiled=True)
-    keyval_weight_grad = lax.dot_general(
-        rows_normed, keyval_all, (((0,), (0,)), ((), ())), preferred_element_type=jnp.float32
-    )
+    keyval_weight_grad = jnp.sum(keyval_sums.astype(jnp.float32), axis=0)
     return (grad_input, grad_gain, keyval_weight_grad.astype(jnp.bfloat16))
 
 

time: 478 us -> 395 us (0.83)
  Pallas kernels: 387 us -> 318 us
  starting transfers between devices: 13 us -> 0.04 us
    pallas_call x6 -> x5, Pallas kernels: 282 us -> 213 us  [exchange_multi(): pl.pallas_call(functools.partial(exchange_kernel, axes, sizes, per_peer),...]
    all_to_all x1 -> x0, starting transfers between devices: 12.9 us -> none  [on_device(): lax.all_to_all(normed_late, 'dp', split_axis=1, concat_axis=0, tiled=True)]
  transfers between devices with their start and end apart: 2 -> 1, of which waited for: 0 -> 0; matrix products, arithmetic and copies ran while one was open for 8% -> 6% of each run, Pallas kernels for 74% -> 37%
where the time goes in v5:
time: 395 us; the launch traced here: 393 us
  Pallas kernels  318 us (81%)
  matrix products  21.2 us (5%)
  local copies, waits for them, and re-layouts  20.4 us (5%)
  other arithmetic  18.4 us (5%)
  between operations  14.4 us (4%)
    pallas_call x5, Pallas kernels, exchange_multi(): pl.pallas_call(functools.partial(exchange_kernel, axes, sizes, per_peer),...  213 us
    pallas_call x1, Pallas kernels, ring_gather(): pl.pallas_call(functools.partial(ring_gather_kernel, pair_count, ring_cou...  105 us
  transfers between devices with their start and end apart: 1, of which 0 were waited for; matrix products, arithmetic and copies ran while one was open for 6% of the time, Pallas kernels for 37%

profile of v5, /device:TPU:6, one launch (start us, length us, event | category | flops | bytes accessed | tf_op | source)
XLA Modules:
  0.0 392.7 jit_solution(12013792968183155112)
XLA Ops:
  9.8 41.7 %shard_map.76 = bf16[16,128,512]{2,1,0:T(8,128)(2,1)} custom-call(bf16[128,512]{1,0:T(8,128)(2,1)} %refs_0_.1), custom_call_target="tpu_custom_call" | custom-call | bytes 4194304 | tf_op jit(solution)/shard_map/pallas_call | solution.py:68
  51.5 4.2 %convert_bitcast_fusion = f32[128,16,512]{2,0,1:T(8,128)} fusion(bf16[16,128,512]{2,1,0:T(8,128)(2,1)} %shard_map.76), kind=kLoop, calls=%fused_computation.1 | loop fusion | flops 1048576 | bytes 6291456 | tf_op jit(solution)/shard_map/convert_element_type | solution.py:232
  55.7 5.5 %copy.59 = f32[128,16,512]{0,2,1:T(8,128)} copy(f32[128,16,512]{2,0,1:T(8,128)} %convert_bitcast_fusion) | data formatting | bytes 8388608 | tf_op jit(solution)/shard_map/convert_element_type | solution.py:232
  61.7 2.0 fusion.8
  63.7 3.9 %copy.63 = bf16[128,16,512]{0,2,1:T(8,128)(2,1)} copy(bf16[128,16,512]{2,0,1:T(8,128)(2,1)} %fusion.8) | data formatting | bytes 4194304 | tf_op jit(solution)/shard_map/mul | solution.py:237
  67.7 104.8 %shard_map.78 = bf16[32,256,256]{2,1,0:T(8,128)(2,1)S(1)} custom-call(bf16[256,256]{1,0:T(8,128)(2,1)S(1)} %get-tuple-element.18.block_ref), custom_call_target="tpu_custom_call" | custom-call | bytes 8388608 | tf_op jit(solution)/shard_map/pallas_call | solution.py:154
  172.5 2.0 copy-done
  175.3 3.9 %fusion.21 = bf16[16,2,8,128]{3,2,1,0:T(8,128)(2,1)S(1)} fusion(bf16[128,8192]{0,1:T(8,128)(2,1)} %bitcast.112, bf16[8192,256]{1,0:T(8,128)(2,1)} %bitcast.109), kind=kOutput, calls=%fused_computation.36 | convolution fusion | flops 536903680 | bytes 6356992 | tf_op jit(solution)/shard_map/dot_general | solution.py:242
  179.3 2.5 fusion.7
  181.8 4.7 %convolution_convert_fusion.2 = bf16[128,320]{1,0:T(8,128)(2,1)S(1)} fusion(bf16[128,8192]{0,1:T(8,128)(2,1)} %fusion.7, bf16[8192,320]{1,0:T(8,128)(2,1)} %all-gather.2.cloned.1.call-done), kind=kOutput, calls=%fused_computation.30 | convolution fusion | flops 671129600 | bytes 7421952 | tf_op jit(solution)/shard_map/dot_general | solution.py:239
  187.1 15.1 %shard_map.77 = bf16[16,128,64]{2,1,0:T(8,128)(2,1)} custom-call(bf16[128,64]{1,0:T(8,128)(2,1)} %slice.56.refs_0_), custom_call_target="tpu_custom_call" | custom-call | bytes 524288 | tf_op jit(solution)/shard_map/pallas_call | solution.py:68
  202.2 1.3 copy.61
  206.2 1.4 copy.81
  207.6 21.6 %shard_map.79 = f32[16,128,64]{2,1,0:T(8,128)} custom-call(f32[16,128,64]{2,1,0:T(8,128)} %bitcast.114), custom_call_target="tpu_custom_call" | custom-call | bytes 1048576 | tf_op jit(solution)/shard_map/pallas_call | solution.py:68
  229.2 1.3 reduce_sum.96
  230.6 2.4 convolution_convert_fusion
  233.1 1.8 copy.86
  235.3 5.0 %fusion.32 = f32[16,512,128]{1,2,0:T(8,128)S(1)} fusion(bf16[16,512,320]{2,1,0:T(8,128)(2,1)} %bitcast.111, bf16[128,64]{0,1:T(8,128)(2,1)S(1)} %copy.82, bf16[128,256]{0,1:T(8,128)(2,1)S(1)} %slice.64), kind=kOutput, calls=%fused_computation.61 | convolution fusion | flops 671252480 | bytes 9519104 | tf_op jit(solution)/shard_map/rc,pkc->prk/dot_general | solution.py:304
  240.3 3.7 fusion.3
  244.0 116.0 %shard_map.80 = (bf16[16,128,512]{2,1,0:T(8,128)(2,1)}, f32[16,1,128]{2,1,0:T(1,128)}, bf16[32,256,64]{2,1,0:T(8,128)(2,1)}) custom-call(bf16[16,128,512]{2,1,0:T(8,128)(2,1)} %get-tuple-element.27.refs_0_, f32[1,128]{1,0:T(1,128)} %bitcast.127, bf16[32,256,64]{2,1,0:T(8,128)(2,1)} %bitcast.113), custom_call_target="tpu_custom_call" | custom-call | bytes 6307840 | tf_op jit(solution)/shard_map/pallas_call | solution.py:68
  360.0 2.0 convert_reduce_fusion
  362.8 1.4 multiply_reduce_fusion
  364.2 19.1 %shard_map.81 = f32[32,1,512]{2,1,0:T(1,128)} custom-call(f32[1,512]{1,0:T(1,128)} %bitcast.126), custom_call_target="tpu_custom_call" | custom-call | bytes 131072 | tf_op jit(solution)/shard_map/pallas_call | solution.py:68
  383.3 1.5 reduce_sum.101
  (67 shorter events, 9.6 us)
Async XLA Ops:
  7.2 174.6 %all-gather.2.cloned.1.call-start = ((), (), s32[]{:S(2)}) async-start(), calls=%async_computation | async-start | bytes 6488064 | tf_op jit(solution)/shard_map/all_gather | solution.py:228
  55.7 5.5 %copy-start.8 = (f32[8192]{0:T(1024)S(1)}, f32[8192]{0:T(1024)}, u32[]{:S(2)}) copy-start(f32[8192]{0:T(1024)} %param.7) | copy-start | bytes 98308
  55.7 5.5 %copy-start.2 = (bf16[16,128,512]{2,1,0:T(8,128)(2,1)S(1)}, bf16[16,128,512]{2,1,0:T(8,128)(2,1)}, u32[]{:S(2)}) copy-start(bf16[16,128,512]{2,1,0:T(8,128)(2,1)} %shard_map.76) | copy-start | bytes 6291460
  61.2 6.5 %copy-start.6 = (f32[16,512]{1,0:T(8,128)}, f32[16,512]{1,0:T(8,128)S(1)}, u32[]{:S(2)}) copy-start(f32[16,512]{1,0:T(8,128)S(1)} %mul.295) | copy-start | bytes 98308
  61.7 117.5 %copy-start.11 = (f32[128]{0:T(128)}, f32[128]{0:T(128)S(1)}, u32[]{:S(2)}) copy-start(f32[128]{0:T(128)S(1)} %add_rsqrt_fusion) | copy-start | bytes 1540
  63.7 110.8 %copy-start.9 = (bf16[128,512]{1,0:T(8,128)(2,1)S(1)}, bf16[128,512]{1,0:T(8,128)(2,1)}, u32[]{:S(2)}) copy-start(bf16[128,512]{1,0:T(8,128)(2,1)} %param.6) | copy-start | bytes 393220
  172.4 2.0 copy-start
  175.3 4.0 %copy-start.3 = (f32[128,16,512]{0,2,1:T(8,128)S(1)}, f32[128,16,512]{0,2,1:T(8,128)}, u32[]{:S(2)}) copy-start(f32[128,16,512]{0,2,1:T(8,128)} %copy.59) | copy-start | bytes 12582916
  235.3 5.0 %copy-start.1 = (bf16[32,256,256]{2,1,0:T(8,128)(2,1)S(1)}, bf16[32,256,256]{2,1,0:T(8,128)(2,1)}, u32[]{:S(2)}) copy-start(bf16[32,256,256]{2,1,0:T(8,128)(2,1)} %copy-done) | copy-start | bytes 12582916
  235.3 5.0 %copy-start.7 = (f32[16,512]{1,0:T(8,128)S(1)}, f32[16,512]{1,0:T(8,128)}, u32[]{:S(2)}) copy-start(f32[16,512]{1,0:T(8,128)} %copy-done.6) | copy-start | bytes 98308
  235.3 5.0 %copy-start.12 = (f32[128]{0:T(128)S(1)}, f32[128]{0:T(128)}, u32[]{:S(2)}) copy-start(f32[128]{0:T(128)} %copy-done.11) | copy-start | bytes 1540
  244.0 118.8 %copy-start.5 = (bf16[128,512]{1,0:T(8,128)(2,1)S(1)}, bf16[128,512]{1,0:T(8,128)(2,1)}, u32[]{:S(2)}) copy-start(bf16[128,512]{1,0:T(8,128)(2,1)} %refs_0_.1) | copy-start | bytes 393220
  244.0 118.8 %copy-start.10 = (f32[512]{0:T(512)S(1)}, f32[512]{0:T(512)}, u32[]{:S(2)}) copy-start(f32[512]{0:T(512)} %dynamic_slice.11) | copy-start | bytes 6148
  360.0 24.8 %copy-start.4 = (bf16[32,256,64]{2,1,0:T(8,128)(2,1)S(1)}, bf16[32,256,64]{2,1,0:T(8,128)(2,1)}, u32[]{:S(2)}) copy-start(bf16[32,256,64]{2,1,0:T(8,128)(2,1)} %get-tuple-element.8) | copy-start | bytes 3145732
Sparse Core Ops, SparseCore 0:
  10.1 167.6 all-gather.1

commit v6 on v5

--- a/solution.py
+++ b/solution.py
@@ -314,18 +314,13 @@
     product_part = jnp.sum(
         normed_terms.astype(jnp.float32) * gain_blocks * unit_blocks, axis=(0, 2)
     ).reshape(1, seq_length)
-    keyval_partials = (
-        jnp.einsum("rk,rc->kc", normed_full, grad_keyval, preferred_element_type=jnp.float32)
-        .astype(jnp.bfloat16)
-        .reshape(lax.axis_size("dp"), -1, group_cols)
-    )
-    normed_sums, product_parts, keyval_sums = exchange_multi(
-        [
-            ("tensor", normed_terms, True),
-            ("tensor", product_part, False),
-            ("dp", keyval_partials, True),
-        ],
-        3,
+    dp_count = lax.axis_size("dp")
+    keyval_partials = jnp.einsum(
+        "rk,rc->kc", normed_full, grad_keyval, preferred_element_type=jnp.float32
+    )
+    keyval_sums = lax.psum_scatter(keyval_partials, "dp", scatter_dimension=0, tiled=True)
+    normed_sums, product_parts = exchange(
+        "tensor", [normed_terms, product_part], [True, False], 3
     )
     grad_normed = jnp.sum(normed_sums.astype(jnp.float32), axis=0)
     product_sum = jnp.sum(product_parts, axis=0).reshape(seq_length, 1)
@@ -336,7 +331,7 @@
     gain_part = jnp.sum(grad_normed * unit_rows, axis=0).reshape(1, local_cols)
     (gain_parts,) = exchange("dp", [gain_part], [False], 4)
     grad_gain = jnp.sum(gain_parts, axis=(0, 1))
-    keyval_weight_grad = jnp.sum(keyval_sums.astype(jnp.float32), axis=0)
+    keyval_weight_grad = keyval_sums
     return (grad_input, grad_gain, keyval_weight_grad.astype(jnp.bfloat16))
 
 

time: 395 us -> 389 us (0.985)
  Pallas kernels: 318 us -> 246 us
  waiting for transfers between devices: 0.02 us -> 67.8 us
    pallas_call x5, Pallas kernels: 213 us -> 141 us  [exchange_multi(): pl.pallas_call(functools.partial(exchange_kernel, axes, sizes, per_peer),...]
    reduce_scatter x0 -> x1, waiting for transfers between devices: none -> 67.7 us  [on_device(): lax.psum_scatter(keyval_partials, 'dp', scatter_dimension=0, tiled=True)]
  transfers between devices with their start and end apart: 1 -> 2, of which waited for: 0 -> 1; matrix products, arithmetic and copies ran while one was open for 6% -> 10% of each run, Pallas kernels for 37% -> 54%
where the time goes in v6:
time: 389 us; the launch traced here: 388 us
  Pallas kernels  246 us (63%)
  waiting for transfers between devices  67.8 us (17%)
  matrix products  22.6 us (6%)
  other arithmetic  19.3 us (5%)
  local copies, waits for them, and re-layouts  18 us (5%)
  between operations  14.5 us (4%)
    pallas_call x5, Pallas kernels, exchange_multi(): pl.pallas_call(functools.partial(exchange_kernel, axes, sizes, per_peer),...  141 us
    pallas_call x1, Pallas kernels, ring_gather(): pl.pallas_call(functools.partial(ring_gather_kernel, pair_count, ring_cou...  105 us
    reduce_scatter x1, waiting for transfers between devices, on_device(): lax.psum_scatter(keyval_partials, 'dp', scatter_dimension=0, tiled=True)  67.7 us
  transfers between devices with their start and end apart: 2, of which 1 were waited for; matrix products, arithmetic and copies ran while one was open for 10% of the time, Pallas kernels for 54%

profile of v6, /device:TPU:6, one launch (start us, length us, event | category | flops | bytes accessed | tf_op | source)
XLA Modules:
  0.0 388.1 jit_solution(3646639206630256104)
XLA Ops:
  9.9 41.7 %shard_map.76 = bf16[16,128,512]{2,1,0:T(8,128)(2,1)} custom-call(bf16[128,512]{1,0:T(8,128)(2,1)} %refs_0_.1), custom_call_target="tpu_custom_call" | custom-call | bytes 4194304 | tf_op jit(solution)/shard_map/pallas_call | solution.py:68
  51.6 4.2 %convert_bitcast_fusion = f32[128,16,512]{2,0,1:T(8,128)} fusion(bf16[16,128,512]{2,1,0:T(8,128)(2,1)} %shard_map.76), kind=kLoop, calls=%fused_computation | loop fusion | flops 1048576 | bytes 6291456 | tf_op jit(solution)/shard_map/convert_element_type | solution.py:232
  55.8 5.5 %copy.57 = f32[128,16,512]{0,2,1:T(8,128)} copy(f32[128,16,512]{2,0,1:T(8,128)} %convert_bitcast_fusion) | data formatting | bytes 8388608 | tf_op jit(solution)/shard_map/convert_element_type | solution.py:232
  61.8 2.0 fusion.8
  63.7 3.9 %copy.61 = bf16[128,16,512]{0,2,1:T(8,128)(2,1)} copy(bf16[128,16,512]{2,0,1:T(8,128)(2,1)} %fusion.8) | data formatting | bytes 4194304 | tf_op jit(solution)/shard_map/mul | solution.py:237
  67.7 105.4 %shard_map.78 = bf16[32,256,256]{2,1,0:T(8,128)(2,1)S(1)} custom-call(bf16[256,256]{1,0:T(8,128)(2,1)S(1)} %get-tuple-element.13.block_ref), custom_call_target="tpu_custom_call" | custom-call | bytes 8388608 | tf_op jit(solution)/shard_map/pallas_call | solution.py:154
  173.1 2.0 copy-done
  175.3 3.9 %fusion.21 = bf16[16,2,8,128]{3,2,1,0:T(8,128)(2,1)S(1)} fusion(bf16[128,8192]{0,1:T(8,128)(2,1)} %bitcast.111, bf16[8192,256]{1,0:T(8,128)(2,1)} %bitcast.108), kind=kOutput, calls=%fused_computation.35 | convolution fusion | flops 536903680 | bytes 6356992 | tf_op jit(solution)/shard_map/dot_general | solution.py:242
  179.3 2.5 fusion.7
  181.8 4.7 %convolution_convert_fusion.1 = bf16[128,320]{1,0:T(8,128)(2,1)S(1)} fusion(bf16[128,8192]{0,1:T(8,128)(2,1)} %fusion.7, bf16[8192,320]{1,0:T(8,128)(2,1)} %all-gather.2.cloned.1.call-done), kind=kOutput, calls=%fused_computation.29 | convolution fusion | flops 671129600 | bytes 7421952 | tf_op jit(solution)/shard_map/dot_general | solution.py:239
  187.1 14.6 %shard_map.77 = bf16[16,128,64]{2,1,0:T(8,128)(2,1)} custom-call(bf16[128,64]{1,0:T(8,128)(2,1)} %slice.56.refs_0_), custom_call_target="tpu_custom_call" | custom-call | bytes 524288 | tf_op jit(solution)/shard_map/pallas_call | solution.py:68
  205.5 1.3 copy.79
  206.9 21.5 %shard_map.79 = f32[16,128,64]{2,1,0:T(8,128)} custom-call(f32[16,128,64]{2,1,0:T(8,128)} %bitcast.112), custom_call_target="tpu_custom_call" | custom-call | bytes 1048576 | tf_op jit(solution)/shard_map/pallas_call | solution.py:68
  228.4 1.3 reduce_sum.84
  229.8 3.7 fusion.58
  235.1 5.0 %fusion.32 = f32[16,512,128]{1,2,0:T(8,128)S(1)} fusion(bf16[16,512,320]{2,1,0:T(8,128)(2,1)} %bitcast.110, bf16[128,64]{0,1:T(8,128)(2,1)S(1)} %copy.80, bf16[128,256]{0,1:T(8,128)(2,1)S(1)} %slice.64), kind=kOutput, calls=%fused_computation.60 | convolution fusion | flops 671252480 | bytes 9519104 | tf_op jit(solution)/shard_map/rc,pkc->prk/dot_general | solution.py:304
  240.1 3.7 fusion.3
  243.9 45.4 %shard_map.80 = (bf16[16,128,512]{2,1,0:T(8,128)(2,1)}, f32[16,1,128]{2,1,0:T(1,128)}) custom-call(bf16[16,128,512]{2,1,0:T(8,128)(2,1)} %get-tuple-element.22.refs_0_, f32[1,128]{1,0:T(1,128)} %bitcast.125), custom_call_target="tpu_custom_call" | custom-call | bytes 4210688 | tf_op jit(solution)/shard_map/pallas_call | solution.py:68
  290.0 1.9 convert_reduce_fusion
  292.0 1.4 multiply_reduce_fusion
  293.3 17.3 %shard_map.81 = f32[32,1,512]{2,1,0:T(1,128)} custom-call(f32[1,512]{1,0:T(1,128)} %bitcast.124), custom_call_target="tpu_custom_call" | custom-call | bytes 131072 | tf_op jit(solution)/shard_map/pallas_call | solution.py:68
  310.6 1.5 reduce_sum.89
  312.1 67.7 %reduce-scatter.2.cloned.1.call-done = f32[256,64]{0,1:T(8,128)} async-done(((f32[8192,64]{0,1:T(8,128)}), f32[256,64]{0,1:T(8,128)}) %reduce-scatter.2.cloned.1.call-update) | async-done | bytes 65552 | tf_op jit(solution)/shard_map/reduce_scatter | solution.py:321
  379.8 1.5 convert_element_type.175
  (68 shorter events, 9.9 us)
Async XLA Ops:
  7.2 174.6 %all-gather.2.cloned.1.call-start = ((), (), s32[]{:S(2)}) async-start(), calls=%async_computation.1 | async-start | bytes 6488064 | tf_op jit(solution)/shard_map/all_gather | solution.py:228
  9.8 370.0 %reduce-scatter.2.cloned.1.call-start = ((), (), s32[]{:S(2)}) async-start(), calls=%async_computation.2 | async-start | bytes 2162688 | tf_op jit(solution)/shard_map/reduce_scatter | solution.py:321
  55.8 5.5 %copy-start.7 = (f32[8192]{0:T(1024)S(1)}, f32[8192]{0:T(1024)}, u32[]{:S(2)}) copy-start(f32[8192]{0:T(1024)} %param.7) | copy-start | bytes 98308
  55.8 5.5 %copy-start.2 = (bf16[16,128,512]{2,1,0:T(8,128)(2,1)S(1)}, bf16[16,128,512]{2,1,0:T(8,128)(2,1)}, u32[]{:S(2)}) copy-start(bf16[16,128,512]{2,1,0:T(8,128)(2,1)} %shard_map.76) | copy-start | bytes 6291460
  61.3 6.4 %copy-start.5 = (f32[16,512]{1,0:T(8,128)}, f32[16,512]{1,0:T(8,128)S(1)}, u32[]{:S(2)}) copy-start(f32[16,512]{1,0:T(8,128)S(1)} %mul.295) | copy-start | bytes 98308
  63.7 111.4 %copy-start.12 = (bf16[128,512]{1,0:T(8,128)(2,1)S(1)}, bf16[128,512]{1,0:T(8,128)(2,1)}, u32[]{:S(2)}) copy-start(bf16[128,512]{1,0:T(8,128)(2,1)} %param.6) | copy-start | bytes 393220
  173.1 2.0 copy-start
  175.3 4.0 %copy-start.3 = (f32[128,16,512]{0,2,1:T(8,128)S(1)}, f32[128,16,512]{0,2,1:T(8,128)}, u32[]{:S(2)}) copy-start(f32[128,16,512]{0,2,1:T(8,128)} %copy.57) | copy-start | bytes 12582916
  203.6 0.7 copy-start.8
  203.6 0.7 copy-start.10
  229.8 4.6 %copy-start.9 = (bf16[128,64]{1,0:T(8,128)(2,1)S(1)}, bf16[128,64]{1,0:T(8,128)(2,1)}, u32[]{:S(2)}) copy-start(bf16[128,64]{1,0:T(8,128)(2,1)} %copy-done.8) | copy-start | bytes 49156
  229.8 4.6 %copy-start.11 = (bf16[128,64]{1,0:T(8,128)(2,1)S(1)}, bf16[128,64]{1,0:T(8,128)(2,1)}, u32[]{:S(2)}) copy-start(bf16[128,64]{1,0:T(8,128)(2,1)} %copy-done.10) | copy-start | bytes 49156
  235.1 5.0 %copy-start.1 = (bf16[32,256,256]{2,1,0:T(8,128)(2,1)S(1)}, bf16[32,256,256]{2,1,0:T(8,128)(2,1)}, u32[]{:S(2)}) copy-start(bf16[32,256,256]{2,1,0:T(8,128)(2,1)} %copy-done) | copy-start | bytes 12582916
  235.1 5.0 %copy-start.6 = (f32[16,512]{1,0:T(8,128)S(1)}, f32[16,512]{1,0:T(8,128)}, u32[]{:S(2)}) copy-start(f32[16,512]{1,0:T(8,128)} %copy-done.5) | copy-start | bytes 98308
  243.9 48.1 %copy-start.4 = (bf16[128,512]{1,0:T(8,128)(2,1)S(1)}, bf16[128,512]{1,0:T(8,128)(2,1)}, u32[]{:S(2)}) copy-start(bf16[128,512]{1,0:T(8,128)(2,1)} %refs_0_.1) | copy-start | bytes 393220
Sparse Core Ops, SparseCore 0:
  10.1 167.4 all-gather.1
  233.7 146.0 reduce-scatter.1

commit v7 on v6

--- a/solution.py
+++ b/solution.py
@@ -83,17 +83,36 @@
     return exchange_multi([(axis, b, s) for b, s in zip(blocks, per_peer)], collective_id)
 
 
-def ring_gather_kernel(pair_count, ring_count, block_ref, out_ref, send_sems, recv_sems):
+def ring_gather_kernel(
+    pair_count, ring_count, side_count, block_ref, side_ref, out_ref, side_out, send_sems, recv_sems, side_send, side_recv
+):
     pair_slot = lax.axis_index("dp") // ring_count
     ring_slot = lax.axis_index("dp") % ring_count
     partner = (1 - pair_slot) * ring_count + ring_slot
     right = pair_slot * ring_count + lax.rem(ring_slot + 1, ring_count)
     left = pair_slot * ring_count + lax.rem(ring_slot + ring_count - 1, ring_count)
     me = pair_slot * ring_count + ring_slot
+    side_me = lax.axis_index("tensor")
     barrier = pltpu.get_barrier_semaphore()
     for peer in (partner, right, left):
         pl.semaphore_signal(barrier, inc=1, device_id={"dp": peer}, device_id_type=MESH)
-    pl.semaphore_wait(barrier, 3)
+    for step in range(1, side_count):
+        peer = lax.rem(side_me + step, side_count)
+        pl.semaphore_signal(barrier, inc=1, device_id={"tensor": peer}, device_id_type=MESH)
+    pl.semaphore_wait(barrier, 3 + side_count - 1)
+    side_copies = []
+    for step in range(1, side_count):
+        peer = lax.rem(side_me + step, side_count)
+        copy = pltpu.make_async_remote_copy(
+            src_ref=side_ref,
+            dst_ref=side_out.at[side_me],
+            send_sem=side_send.at[step],
+            recv_sem=side_recv.at[step],
+            device_id={"tensor": peer},
+            device_id_type=MESH,
+        )
+        copy.start()
+        side_copies.append(copy)
     swap = pltpu.make_async_remote_copy(
         src_ref=block_ref,
         dst_ref=out_ref.at[me],
@@ -105,6 +124,7 @@
     swap.start()
     own = pltpu.make_async_copy(block_ref, out_ref.at[me], send_sems.at[2, 1, 0])
     own.start()
+    side_out[side_me] = side_ref[...]
     own.wait()
     swap.wait_send()
     swap.wait_recv()
@@ -143,31 +163,37 @@
             left_copies = send(1, step, left, origin)
     for copy in right_copies + left_copies:
         copy.wait_recv()
-    for copy in sent:
+    for copy in sent + side_copies:
         copy.wait_send()
-
-
-def ring_gather(block, collective_id):
+    for copy in side_copies:
+        copy.wait_recv()
+
+
+def ring_gather(block, side, collective_id):
     count = lax.axis_size("dp")
+    side_count = lax.axis_size("tensor")
     pair_count = 2
     ring_count = count // pair_count
+    sent = count * block.size * block.dtype.itemsize + side_count * side.size * side.dtype.itemsize
     return pl.pallas_call(
-        functools.partial(ring_gather_kernel, pair_count, ring_count),
-        out_shape=jax.ShapeDtypeStruct((count,) + block.shape, block.dtype),
-        in_specs=[pl.BlockSpec(memory_space=pltpu.VMEM)],
-        out_specs=pl.BlockSpec(memory_space=pltpu.VMEM),
+        functools.partial(ring_gather_kernel, pair_count, ring_count, side_count),
+        out_shape=(
+            jax.ShapeDtypeStruct((count,) + block.shape, block.dtype),
+            jax.ShapeDtypeStruct((side_count,) + side.shape, side.dtype),
+        ),
+        in_specs=[pl.BlockSpec(memory_space=pltpu.VMEM)] * 2,
+        out_specs=(pl.BlockSpec(memory_space=pltpu.VMEM), pl.BlockSpec(memory_space=pltpu.VMEM)),
         scratch_shapes=[
             pltpu.SemaphoreType.DMA((3, ring_count, pair_count)),
             pltpu.SemaphoreType.DMA((3, ring_count, pair_count)),
+            pltpu.SemaphoreType.DMA((side_count,)),
+            pltpu.SemaphoreType.DMA((side_count,)),
         ],
         compiler_params=pltpu.CompilerParams(
             collective_id=collective_id, has_side_effects=True, vmem_limit_bytes=48 * 1024 * 1024
         ),
-        cost_estimate=pl.CostEstimate(
-            flops=0, bytes_accessed=2 * count * block.size * block.dtype.itemsize, transcendentals=0
-        ),
-    )(block)
-
+        cost_estimate=pl.CostEstimate(flops=0, bytes_accessed=2 * sent, transcendentals=0),
+    )(block, side)
 
 HD = 128
 KV_HEADS = 4
@@ -226,8 +252,8 @@
     split_cols = query_cols // 2
     engine_block = jnp.concatenate([w_query[:, :split_cols], w_keyval], axis=1)
     engine_full = lax.all_gather(engine_block, "dp", axis=0, tiled=True)
-    ring_full = ring_gather(w_query[:, split_cols:], 6).reshape(-1, query_cols - split_cols)
-    (input_blocks,) = exchange("tensor", [inputs], [False], 0)
+    ring_blocks_out, input_blocks = ring_gather(w_query[:, split_cols:], inputs, 6)
+    ring_full = ring_blocks_out.reshape(-1, query_cols - split_cols)
     inputs_full = (
         input_blocks.transpose(1, 0, 2).reshape(seq_length, model_width).astype(jnp.float32)
     )
@@ -317,7 +343,7 @@
     dp_count = lax.axis_size("dp")
     keyval_partials = jnp.einsum(
         "rk,rc->kc", normed_full, grad_keyval, preferred_element_type=jnp.float32
-    )
+    ).reshape(model_width // 2, 2 * group_cols)
     keyval_sums = lax.psum_scatter(keyval_partials, "dp", scatter_dimension=0, tiled=True)
     normed_sums, product_parts = exchange(
         "tensor", [normed_terms, product_part], [True, False], 3
@@ -331,7 +357,7 @@
     gain_part = jnp.sum(grad_normed * unit_rows, axis=0).reshape(1, local_cols)
     (gain_parts,) = exchange("dp", [gain_part], [False], 4)
     grad_gain = jnp.sum(gain_parts, axis=(0, 1))
-    keyval_weight_grad = keyval_sums
+    keyval_weight_grad = keyval_sums.reshape(-1, group_cols)
     return (grad_input, grad_gain, keyval_weight_grad.astype(jnp.bfloat16))
 
 

time: 389 us -> 389 us (level)
  Pallas kernels: 246 us -> 225 us
  waiting for transfers between devices: 67.8 us -> 85.6 us
  local copies, waits for them, and re-layouts: 18 us -> 22.2 us
    pallas_call x5 -> x4, Pallas kernels: 141 us -> 108 us  [exchange_multi(): pl.pallas_call(functools.partial(exchange_kernel, axes, sizes, per_peer),...]
    all_gather x1, waiting for transfers between devices: 0.01 us -> 25.6 us  [on_device(): engine_full = lax.all_gather(engine_block, 'dp', axis=0, tiled=True)]
    pallas_call x1, Pallas kernels: 105 us -> 117 us  [ring_gather(): pl.pallas_call(functools.partial(ring_gather_kernel, pair_count, ring_cou...]
    reduce_scatter x1, waiting for transfers between devices: 67.7 us -> 59.9 us  [on_device(): lax.psum_scatter(keyval_partials, 'dp', scatter_dimension=0, tiled=True)]
    reshape x0 -> x1, local copies, waits for them, and re-layouts: none -> 4.64 us  [on_device(): keyval_partials = jnp.einsum('rk,rc->kc', normed_full, grad_keyval, prefe...]
  transfers between devices with their start and end apart: 2 -> 2, of which waited for: 1 -> 2; matrix products, arithmetic and copies ran while one was open for 10% -> 9% of each run, Pallas kernels for 54% -> 47%
where the time goes in v7:
time: 389 us; the launch traced here: 388 us
  Pallas kernels  225 us (58%)
  waiting for transfers between devices  85.6 us (22%)
  matrix products  23.1 us (6%)
  local copies, waits for them, and re-layouts  22.2 us (6%)
  other arithmetic  17.1 us (4%)
  between operations  14.5 us (4%)
    pallas_call x1, Pallas kernels, ring_gather(): pl.pallas_call(functools.partial(ring_gather_kernel, pair_count, ring_cou...  117 us
    pallas_call x4, Pallas kernels, exchange_multi(): pl.pallas_call(functools.partial(exchange_kernel, axes, sizes, per_peer),...  108 us
    reduce_scatter x1, waiting for transfers between devices, on_device(): lax.psum_scatter(keyval_partials, 'dp', scatter_dimension=0, tiled=True)  59.9 us
    all_gather x1, waiting for transfers between devices, on_device(): engine_full = lax.all_gather(engine_block, 'dp', axis=0, tiled=True)  25.6 us
  transfers between devices with their start and end apart: 2, of which 2 were waited for; matrix products, arithmetic and copies ran while one was open for 9% of the time, Pallas kernels for 47%

profile of v7, /device:TPU:6, one launch (start us, length us, event | category | flops | bytes accessed | tf_op | source)
XLA Modules:
  0.0 387.7 jit_solution(6565738213383779814)
XLA Ops:
  10.8 117.5 %shard_map.76 = (bf16[32,256,256]{2,1,0:T(8,128)(2,1)}, bf16[16,128,512]{2,1,0:T(8,128)(2,1)S(1)}) custom-call(bf16[256,256]{1,0:T(8,128)(2,1)S(1)} %get-tuple-element.23.block_ref, bf16[128,512]{1,0:T(8,128)(2,1)S(1)} %copy-done), custom_call_target="tpu_custom_call" | custom-call | bytes 12582912 | tf_op jit(solution)/shard_map/pallas_call | solution.py:178
  128.3 2.5 convert_bitcast_fusion
  130.8 5.3 %copy.61 = f32[128,16,512]{0,2,1:T(8,128)} copy(f32[128,16,512]{2,0,1:T(8,128)} %convert_bitcast_fusion) | data formatting | bytes 8388608 | tf_op jit(solution)/shard_map/convert_element_type | solution.py:258
  136.7 2.0 fusion.7
  138.7 3.9 %copy.65 = bf16[128,16,512]{0,2,1:T(8,128)(2,1)} copy(bf16[128,16,512]{2,0,1:T(8,128)(2,1)} %fusion.7) | data formatting | bytes 4194304 | tf_op jit(solution)/shard_map/mul | solution.py:263
  142.8 4.0 %fusion.21 = bf16[16,2,8,128]{3,2,1,0:T(8,128)(2,1)S(1)} fusion(bf16[128,8192]{0,1:T(8,128)(2,1)} %bitcast.107, bf16[8192,256]{1,0:T(8,128)(2,1)} %bitcast.105), kind=kOutput, calls=%fused_computation.35 | convolution fusion | flops 536903680 | bytes 6356992 | tf_op jit(solution)/shard_map/dot_general | solution.py:268
  146.8 2.5 fusion.6
  149.3 25.6 %all-gather.2.cloned.1.call-done = bf16[8192,320]{1,0:T(8,128)(2,1)} async-done(((bf16[256,320]{1,0:T(8,128)(2,1)}), bf16[8192,320]{1,0:T(8,128)(2,1)}) %all-gather.2.cloned.1.call-update) | async-done | bytes 5242896 | tf_op jit(solution)/shard_map/all_gather | solution.py:254
  175.0 4.7 %convolution_convert_fusion.1 = bf16[128,320]{1,0:T(8,128)(2,1)S(1)} fusion(bf16[128,8192]{0,1:T(8,128)(2,1)} %fusion.6, bf16[8192,320]{1,0:T(8,128)(2,1)} %all-gather.2.cloned.1.call-done), kind=kOutput, calls=%fused_computation.29 | convolution fusion | flops 671129600 | bytes 7421952 | tf_op jit(solution)/shard_map/dot_general | solution.py:265
  180.3 23.0 %shard_map.77 = bf16[16,128,64]{2,1,0:T(8,128)(2,1)} custom-call(bf16[128,64]{1,0:T(8,128)(2,1)} %slice.56.refs_0_), custom_call_target="tpu_custom_call" | custom-call | bytes 524288 | tf_op jit(solution)/shard_map/pallas_call | solution.py:68
  203.3 1.3 copy.63
  207.1 1.3 copy.83
  208.4 21.7 %shard_map.78 = f32[16,128,64]{2,1,0:T(8,128)} custom-call(f32[16,128,64]{2,1,0:T(8,128)} %bitcast.108), custom_call_target="tpu_custom_call" | custom-call | bytes 1048576 | tf_op jit(solution)/shard_map/pallas_call | solution.py:68
  230.1 1.3 reduce_sum.84
  231.5 4.4 %fusion.58 = f32[8192,64]{1,0:T(8,128)} fusion(bf16[128,8192]{0,1:T(8,128)(2,1)} %fusion.6, bf16[128,64]{0,1:T(8,128)(2,1)S(1)} %copy.84), kind=kOutput, calls=%fused_computation.98 | convolution fusion | flops 134217728 | bytes 4210688 | tf_op jit(solution)/shard_map/rk,rc->kc/dot_general | solution.py:344
  235.9 4.6 %reshape.132 = f32[4096,128]{1,0:T(8,128)} reshape(f32[8192,64]{1,0:T(8,128)} %fusion.58) | data formatting | bytes 4194304 | tf_op jit(solution)/shard_map/reshape | solution.py:346
  242.0 5.0 %fusion.32 = f32[16,512,128]{1,2,0:T(8,128)S(1)} fusion(bf16[16,512,320]{2,1,0:T(8,128)(2,1)} %bitcast.104, bf16[128,64]{0,1:T(8,128)(2,1)S(1)} %copy.84, bf16[128,256]{0,1:T(8,128)(2,1)S(1)} %slice.64), kind=kOutput, calls=%fused_computation.60 | convolution fusion | flops 671252480 | bytes 9519104 | tf_op jit(solution)/shard_map/rc,pkc->prk/dot_general | solution.py:330
  247.0 3.5 fusion.3
  250.6 45.3 %shard_map.79 = (bf16[16,128,512]{2,1,0:T(8,128)(2,1)}, f32[16,1,128]{2,1,0:T(1,128)}) custom-call(bf16[16,128,512]{2,1,0:T(8,128)(2,1)} %get-tuple-element.32.refs_0_, f32[1,128]{1,0:T(1,128)} %bitcast.121), custom_call_target="tpu_custom_call" | custom-call | bytes 4210688 | tf_op jit(solution)/shard_map/pallas_call | solution.py:68
  296.6 1.9 convert_reduce_fusion
  298.6 1.4 multiply_reduce_fusion
  299.9 17.9 %shard_map.80 = f32[32,1,512]{2,1,0:T(1,128)} custom-call(f32[1,512]{1,0:T(1,128)} %bitcast.120), custom_call_target="tpu_custom_call" | custom-call | bytes 131072 | tf_op jit(solution)/shard_map/pallas_call | solution.py:68
  317.9 1.5 reduce_sum.89
  319.3 59.9 %reduce-scatter.2.cloned.1.call-done = f32[128,128]{1,0:T(8,128)} async-done(((f32[4096,128]{1,0:T(8,128)}), f32[128,128]{1,0:T(8,128)}) %reduce-scatter.2.cloned.1.call-update) | async-done | bytes 65552 | tf_op jit(solution)/shard_map/reduce_scatter | solution.py:347
  (68 shorter events, 11.2 us)
Async XLA Ops:
  7.2 167.8 %all-gather.2.cloned.1.call-start = ((), (), s32[]{:S(2)}) async-start(), calls=%async_computation.1 | async-start | bytes 6488064 | tf_op jit(solution)/shard_map/all_gather | solution.py:254
  9.8 369.4 %reduce-scatter.2.cloned.1.call-start = ((), (), s32[]{:S(2)}) async-start(), calls=%async_computation.2 | async-start | bytes 2162688 | tf_op jit(solution)/shard_map/reduce_scatter | solution.py:347
  9.9 0.9 copy-start
  130.8 5.3 %copy-start.6 = (f32[8192]{0:T(1024)S(1)}, f32[8192]{0:T(1024)}, u32[]{:S(2)}) copy-start(f32[8192]{0:T(1024)} %param.7) | copy-start | bytes 98308
  136.2 6.4 %copy-start.4 = (f32[16,512]{1,0:T(8,128)}, f32[16,512]{1,0:T(8,128)S(1)}, u32[]{:S(2)}) copy-start(f32[16,512]{1,0:T(8,128)S(1)} %mul.295) | copy-start | bytes 98308
  136.7 5.9 %copy-start.11 = (bf16[128,512]{1,0:T(8,128)(2,1)S(1)}, bf16[128,512]{1,0:T(8,128)(2,1)}, u32[]{:S(2)}) copy-start(bf16[128,512]{1,0:T(8,128)(2,1)} %param.6) | copy-start | bytes 393220
  142.8 4.1 %copy-start.3 = (f32[128,16,512]{0,2,1:T(8,128)S(1)}, f32[128,16,512]{0,2,1:T(8,128)}, u32[]{:S(2)}) copy-start(f32[128,16,512]{0,2,1:T(8,128)} %copy.61) | copy-start | bytes 12582916
  205.1 0.7 copy-start.7
  205.1 0.7 copy-start.9
  235.9 5.4 %copy-start.8 = (bf16[128,64]{1,0:T(8,128)(2,1)S(1)}, bf16[128,64]{1,0:T(8,128)(2,1)}, u32[]{:S(2)}) copy-start(bf16[128,64]{1,0:T(8,128)(2,1)} %copy-done.7) | copy-start | bytes 49156
  235.9 5.4 %copy-start.10 = (bf16[128,64]{1,0:T(8,128)(2,1)S(1)}, bf16[128,64]{1,0:T(8,128)(2,1)}, u32[]{:S(2)}) copy-start(bf16[128,64]{1,0:T(8,128)(2,1)} %copy-done.9) | copy-start | bytes 49156
  242.0 5.0 %copy-start.2 = (bf16[32,256,256]{2,1,0:T(8,128)(2,1)S(1)}, bf16[32,256,256]{2,1,0:T(8,128)(2,1)}, u32[]{:S(2)}) copy-start(bf16[32,256,256]{2,1,0:T(8,128)(2,1)} %get-tuple-element.8) | copy-start | bytes 12582916
  242.0 5.0 %copy-start.5 = (f32[16,512]{1,0:T(8,128)S(1)}, f32[16,512]{1,0:T(8,128)}, u32[]{:S(2)}) copy-start(f32[16,512]{1,0:T(8,128)} %copy-done.4) | copy-start | bytes 98308
  250.6 48.0 %copy-start.1 = (bf16[128,512]{1,0:T(8,128)(2,1)S(1)}, bf16[128,512]{1,0:T(8,128)(2,1)}, u32[]{:S(2)}) copy-start(bf16[128,512]{1,0:T(8,128)(2,1)} %side_ref.1) | copy-start | bytes 393220
Sparse Core Ops, SparseCore 0:
  10.1 164.8 all-gather.1
  240.6 138.5 reduce-scatter.1

commit v8 on v7

--- a/solution.py
+++ b/solution.py
@@ -343,7 +343,7 @@
     dp_count = lax.axis_size("dp")
     keyval_partials = jnp.einsum(
         "rk,rc->kc", normed_full, grad_keyval, preferred_element_type=jnp.float32
-    ).reshape(model_width // 2, 2 * group_cols)
+    ).reshape(model_width // 2, 2 * group_cols).astype(jnp.bfloat16)
     keyval_sums = lax.psum_scatter(keyval_partials, "dp", scatter_dimension=0, tiled=True)
     normed_sums, product_parts = exchange(
         "tensor", [normed_terms, product_part], [True, False], 3

time: 389 us -> 387 us (level)
    convert_element_type x1 -> x2, local copies, waits for them, and re-layouts: 0.09 us -> 5.66 us  [on_device(): keyval_partials = jnp.einsum('rk,rc->kc', normed_full, grad_keyval, prefe...]
  transfers between devices with their start and end apart: 2 -> 2, of which waited for: 2 -> 2; matrix products, arithmetic and copies ran while one was open for 9% -> 9% of each run, Pallas kernels for 47% -> 46%
where the time goes in v8:
time: 387 us; the launch traced here: 386 us
  Pallas kernels  224 us (58%)
  waiting for transfers between devices  86 us (22%)
  local copies, waits for them, and re-layouts  23.9 us (6%)
  matrix products  21.1 us (5%)
  other arithmetic  16.2 us (4%)
  between operations  14.4 us (4%)
    pallas_call x1, Pallas kernels, ring_gather(): pl.pallas_call(functools.partial(ring_gather_kernel, pair_count, ring_cou...  117 us
    pallas_call x4, Pallas kernels, exchange_multi(): pl.pallas_call(functools.partial(exchange_kernel, axes, sizes, per_peer),...  107 us
    reduce_scatter x1, waiting for transfers between devices, on_device(): lax.psum_scatter(keyval_partials, 'dp', scatter_dimension=0, tiled=True)  60.9 us
    all_gather x1, waiting for transfers between devices, on_device(): engine_full = lax.all_gather(engine_block, 'dp', axis=0, tiled=True)  25 us
  transfers between devices with their start and end apart: 2, of which 2 were waited for; matrix products, arithmetic and copies ran while one was open for 9% of the time, Pallas kernels for 46%

profile of v8, /device:TPU:6, one launch (start us, length us, event | category | flops | bytes accessed | tf_op | source)
XLA Modules:
  0.0 385.7 jit_solution(7037245405438627466)
XLA Ops:
  10.8 117.5 %shard_map.76 = (bf16[32,256,256]{2,1,0:T(8,128)(2,1)}, bf16[16,128,512]{2,1,0:T(8,128)(2,1)S(1)}) custom-call(bf16[256,256]{1,0:T(8,128)(2,1)S(1)} %get-tuple-element.23.block_ref, bf16[128,512]{1,0:T(8,128)(2,1)S(1)} %copy-done), custom_call_target="tpu_custom_call" | custom-call | bytes 12582912 | tf_op jit(solution)/shard_map/pallas_call | solution.py:178
  128.3 2.5 convert_bitcast_fusion
  130.8 5.3 %copy.61 = f32[128,16,512]{0,2,1:T(8,128)} copy(f32[128,16,512]{2,0,1:T(8,128)} %convert_bitcast_fusion) | data formatting | bytes 8388608 | tf_op jit(solution)/shard_map/convert_element_type | solution.py:258
  136.7 1.9 fusion.7
  138.6 3.9 %copy.65 = bf16[128,16,512]{0,2,1:T(8,128)(2,1)} copy(bf16[128,16,512]{2,0,1:T(8,128)(2,1)} %fusion.7) | data formatting | bytes 4194304 | tf_op jit(solution)/shard_map/mul | solution.py:263
  143.4 4.0 %fusion.21 = bf16[16,2,8,128]{3,2,1,0:T(8,128)(2,1)S(1)} fusion(bf16[128,8192]{0,1:T(8,128)(2,1)} %bitcast.107, bf16[8192,256]{1,0:T(8,128)(2,1)} %bitcast.105), kind=kOutput, calls=%fused_computation.36 | convolution fusion | flops 536903680 | bytes 6356992 | tf_op jit(solution)/shard_map/dot_general | solution.py:268
  147.5 2.5 fusion.6
  149.9 25.0 %all-gather.2.cloned.1.call-done = bf16[8192,320]{1,0:T(8,128)(2,1)} async-done(((bf16[256,320]{1,0:T(8,128)(2,1)}), bf16[8192,320]{1,0:T(8,128)(2,1)}) %all-gather.2.cloned.1.call-update) | async-done | bytes 5242896 | tf_op jit(solution)/shard_map/all_gather | solution.py:254
  175.0 4.7 %convolution_convert_fusion.2 = bf16[128,320]{1,0:T(8,128)(2,1)S(1)} fusion(bf16[128,8192]{0,1:T(8,128)(2,1)} %fusion.6, bf16[8192,320]{1,0:T(8,128)(2,1)} %all-gather.2.cloned.1.call-done), kind=kOutput, calls=%fused_computation.30 | convolution fusion | flops 671129600 | bytes 7421952 | tf_op jit(solution)/shard_map/dot_general | solution.py:265
  180.3 23.6 %shard_map.77 = bf16[16,128,64]{2,1,0:T(8,128)(2,1)} custom-call(bf16[128,64]{1,0:T(8,128)(2,1)} %slice.56.refs_0_), custom_call_target="tpu_custom_call" | custom-call | bytes 524288 | tf_op jit(solution)/shard_map/pallas_call | solution.py:68
  207.9 1.4 copy.83
  209.3 21.7 %shard_map.78 = f32[16,128,64]{2,1,0:T(8,128)} custom-call(f32[16,128,64]{2,1,0:T(8,128)} %bitcast.108), custom_call_target="tpu_custom_call" | custom-call | bytes 1048576 | tf_op jit(solution)/shard_map/pallas_call | solution.py:68
  231.0 1.3 reduce_sum.84
  232.4 2.4 convolution_convert_fusion
  234.8 1.8 copy.89
  236.6 3.9 %convert_element_type.182 = bf16[4096,128]{1,0:T(8,128)(2,1)} reshape(bf16[8192,64]{1,0:T(8,128)(2,1)} %copy.89) | data formatting | bytes 2097152 | tf_op jit(solution)/shard_map/convert_element_type | solution.py:346
  241.0 5.0 %fusion.32 = f32[16,512,128]{1,2,0:T(8,128)S(1)} fusion(bf16[16,512,320]{2,1,0:T(8,128)(2,1)} %bitcast.104, bf16[128,64]{0,1:T(8,128)(2,1)S(1)} %copy.84, bf16[128,256]{0,1:T(8,128)(2,1)S(1)} %slice.64), kind=kOutput, calls=%fused_computation.61 | convolution fusion | flops 671252480 | bytes 9519104 | tf_op jit(solution)/shard_map/rc,pkc->prk/dot_general | solution.py:330
  246.0 3.5 fusion.3
  249.6 43.7 %shard_map.79 = (bf16[16,128,512]{2,1,0:T(8,128)(2,1)}, f32[16,1,128]{2,1,0:T(1,128)}) custom-call(bf16[16,128,512]{2,1,0:T(8,128)(2,1)} %get-tuple-element.32.refs_0_, f32[1,128]{1,0:T(1,128)} %bitcast.121), custom_call_target="tpu_custom_call" | custom-call | bytes 4210688 | tf_op jit(solution)/shard_map/pallas_call | solution.py:68
  294.0 1.9 convert_reduce_fusion
  295.9 1.4 multiply_reduce_fusion
  297.3 17.7 %shard_map.80 = f32[32,1,512]{2,1,0:T(1,128)} custom-call(f32[1,512]{1,0:T(1,128)} %bitcast.120), custom_call_target="tpu_custom_call" | custom-call | bytes 131072 | tf_op jit(solution)/shard_map/pallas_call | solution.py:68
  314.9 1.5 reduce_sum.89
  316.4 60.9 %reduce-scatter.2.cloned.1.call-done = bf16[128,128]{1,0:T(8,128)(2,1)} async-done(((bf16[4096,128]{1,0:T(8,128)(2,1)}), bf16[128,128]{1,0:T(8,128)(2,1)}) %reduce-scatter.2.cloned.1.call-update) | async-done | bytes 32784 | tf_op jit(solution)/shard_map/reduce_scatter | solution.py:347
  (66 shorter events, 12.2 us)
Async XLA Ops:
  7.2 167.8 %all-gather.2.cloned.1.call-start = ((), (), s32[]{:S(2)}) async-start(), calls=%async_computation.1 | async-start | bytes 6488064 | tf_op jit(solution)/shard_map/all_gather | solution.py:254
  9.8 367.5 %reduce-scatter.2.cloned.1.call-start = ((), (), s32[]{:S(2)}) async-start(), calls=%async_computation.2 | async-start | bytes 1081344 | tf_op jit(solution)/shard_map/reduce_scatter | solution.py:347
  9.9 0.9 copy-start
  130.8 5.3 %copy-start.6 = (f32[8192]{0:T(1024)S(1)}, f32[8192]{0:T(1024)}, u32[]{:S(2)}) copy-start(f32[8192]{0:T(1024)} %param.7) | copy-start | bytes 98308
  136.2 6.4 %copy-start.4 = (f32[16,512]{1,0:T(8,128)}, f32[16,512]{1,0:T(8,128)S(1)}, u32[]{:S(2)}) copy-start(f32[16,512]{1,0:T(8,128)S(1)} %mul.295) | copy-start | bytes 98308
  136.7 10.7 %copy-start.9 = (f32[128]{0:T(128)}, f32[128]{0:T(128)S(1)}, u32[]{:S(2)}) copy-start(f32[128]{0:T(128)S(1)} %add_rsqrt_fusion) | copy-start | bytes 1540
  136.7 5.9 %copy-start.7 = (bf16[128,512]{1,0:T(8,128)(2,1)S(1)}, bf16[128,512]{1,0:T(8,128)(2,1)}, u32[]{:S(2)}) copy-start(bf16[128,512]{1,0:T(8,128)(2,1)} %param.6) | copy-start | bytes 393220
  143.4 4.1 %copy-start.3 = (f32[128,16,512]{0,2,1:T(8,128)S(1)}, f32[128,16,512]{0,2,1:T(8,128)}, u32[]{:S(2)}) copy-start(f32[128,16,512]{0,2,1:T(8,128)} %copy.61) | copy-start | bytes 12582916
  240.9 5.1 %copy-start.2 = (bf16[32,256,256]{2,1,0:T(8,128)(2,1)S(1)}, bf16[32,256,256]{2,1,0:T(8,128)(2,1)}, u32[]{:S(2)}) copy-start(bf16[32,256,256]{2,1,0:T(8,128)(2,1)} %get-tuple-element.8) | copy-start | bytes 12582916
  240.9 5.1 %copy-start.5 = (f32[16,512]{1,0:T(8,128)S(1)}, f32[16,512]{1,0:T(8,128)}, u32[]{:S(2)}) copy-start(f32[16,512]{1,0:T(8,128)} %copy-done.4) | copy-start | bytes 98308
  241.0 5.1 %copy-start.10 = (f32[128]{0:T(128)S(1)}, f32[128]{0:T(128)}, u32[]{:S(2)}) copy-start(f32[128]{0:T(128)} %copy-done.9) | copy-start | bytes 1540
  249.6 46.3 %copy-start.1 = (bf16[128,512]{1,0:T(8,128)(2,1)S(1)}, bf16[128,512]{1,0:T(8,128)(2,1)}, u32[]{:S(2)}) copy-start(bf16[128,512]{1,0:T(8,128)(2,1)} %side_ref.1) | copy-start | bytes 393220
  249.6 46.3 %copy-start.8 = (f32[512]{0:T(512)S(1)}, f32[512]{0:T(512)}, u32[]{:S(2)}) copy-start(f32[512]{0:T(512)} %dynamic_slice.11) | copy-start | bytes 6148
Sparse Core Ops, SparseCore 0:
  10.1 164.8 all-gather.1
  240.6 136.6 reduce-scatter.1

commit v9 on v8

--- a/solution.py
+++ b/solution.py
@@ -195,6 +195,41 @@
         cost_estimate=pl.CostEstimate(flops=0, bytes_accessed=2 * sent, transcendentals=0),
     )(block, side)
 
+def pair_sum_kernel(ring_count, block_ref, out_ref, landing, sems):
+    pair_slot = lax.axis_index("dp") // ring_count
+    ring_slot = lax.axis_index("dp") % ring_count
+    partner = (1 - pair_slot) * ring_count + ring_slot
+    barrier = pltpu.get_barrier_semaphore()
+    pl.semaphore_signal(barrier, inc=1, device_id={"dp": partner}, device_id_type=MESH)
+    pl.semaphore_wait(barrier, 1)
+    copy = pltpu.make_async_remote_copy(
+        src_ref=block_ref.at[1 - pair_slot],
+        dst_ref=landing,
+        send_sem=sems.at[0],
+        recv_sem=sems.at[1],
+        device_id={"dp": partner},
+        device_id_type=MESH,
+    )
+    copy.start()
+    copy.wait_send()
+    copy.wait_recv()
+    out_ref[...] = block_ref[pair_slot] + landing[...]
+
+
+def pair_sum(blocks, ring_count, collective_id):
+    return pl.pallas_call(
+        functools.partial(pair_sum_kernel, ring_count),
+        out_shape=jax.ShapeDtypeStruct(blocks.shape[1:], blocks.dtype),
+        in_specs=[pl.BlockSpec(memory_space=pltpu.VMEM)],
+        out_specs=pl.BlockSpec(memory_space=pltpu.VMEM),
+        scratch_shapes=[pltpu.VMEM(blocks.shape[1:], blocks.dtype), pltpu.SemaphoreType.DMA((2,))],
+        compiler_params=pltpu.CompilerParams(collective_id=collective_id, has_side_effects=True),
+        cost_estimate=pl.CostEstimate(
+            flops=0, bytes_accessed=3 * blocks.size * blocks.dtype.itemsize, transcendentals=0
+        ),
+    )(blocks)
+
+
 HD = 128
 KV_HEADS = 4
 HEADS_DEV = 4
@@ -341,10 +376,20 @@
         normed_terms.astype(jnp.float32) * gain_blocks * unit_blocks, axis=(0, 2)
     ).reshape(1, seq_length)
     dp_count = lax.axis_size("dp")
-    keyval_partials = jnp.einsum(
-        "rk,rc->kc", normed_full, grad_keyval, preferred_element_type=jnp.float32
-    ).reshape(model_width // 2, 2 * group_cols).astype(jnp.bfloat16)
-    keyval_sums = lax.psum_scatter(keyval_partials, "dp", scatter_dimension=0, tiled=True)
+    pair_count = 2
+    ring_count = dp_count // pair_count
+    keyval_partials = (
+        jnp.einsum("rk,rc->kc", normed_full, grad_keyval, preferred_element_type=jnp.float32)
+        .reshape(pair_count, ring_count, -1, group_cols)
+        .transpose(1, 0, 2, 3)
+        .reshape(model_width // 2, 2 * group_cols)
+    )
+    ring_groups = [
+        [pair * ring_count + slot for slot in range(ring_count)] for pair in range(pair_count)
+    ]
+    ring_sums = lax.psum_scatter(
+        keyval_partials, "dp", scatter_dimension=0, tiled=True, axis_index_groups=ring_groups
+    )
     normed_sums, product_parts = exchange(
         "tensor", [normed_terms, product_part], [True, False], 3
     )
@@ -357,6 +402,8 @@
     gain_part = jnp.sum(grad_normed * unit_rows, axis=0).reshape(1, local_cols)
     (gain_parts,) = exchange("dp", [gain_part], [False], 4)
     grad_gain = jnp.sum(gain_parts, axis=(0, 1))
+    lane_rows = ring_sums.size // (pair_count * 128)
+    keyval_sums = pair_sum(ring_sums.reshape(pair_count, lane_rows, 128), ring_count, 7)
     keyval_weight_grad = keyval_sums.reshape(-1, group_cols)
     return (grad_input, grad_gain, keyval_weight_grad.astype(jnp.bfloat16))
 

time: 387 us -> 335 us (0.87)
  waiting for transfers between devices: 86 us -> 25.7 us
  Pallas kernels: 224 us -> 228 us
    reduce_scatter x1, waiting for transfers between devices: 60.9 us -> 0.01 us  [on_device(): lax.psum_scatter(keyval_partials, 'dp', scatter_dimension=0, tiled=True,...]
    pallas_call x0 -> x1, Pallas kernels: none -> 6.5 us  [pair_sum(): pl.pallas_call(functools.partial(pair_sum_kernel, ring_count), out_shape=...]
    convert_element_type x2 -> x1, local copies, waits for them, and re-layouts: 5.66 us -> 0.09 us  [on_device(): return (grad_input, grad_gain, keyval_weight_grad.astype(jnp.bfloat16))]
    transpose x0 -> x1, local copies, waits for them, and re-layouts: none -> 3.91 us  [on_device(): keyval_partials = jnp.einsum('rk,rc->kc', normed_full, grad_keyval, prefe...]
  transfers between devices with their start and end apart: 2 -> 2, of which waited for: 2 -> 1; matrix products, arithmetic and copies ran while one was open for 9% -> 11% of each run, Pallas kernels for 46% -> 53%
where the time goes in v9:
time: 335 us; the launch traced here: 334 us
  Pallas kernels  228 us (68%)
  local copies, waits for them, and re-layouts  26.2 us (8%)
  waiting for transfers between devices  25.7 us (8%)
  matrix products  22.5 us (7%)
  other arithmetic  17 us (5%)
  between operations  14.5 us (4%)
    pallas_call x1, Pallas kernels, ring_gather(): pl.pallas_call(functools.partial(ring_gather_kernel, pair_count, ring_cou...  117 us
    pallas_call x4, Pallas kernels, exchange_multi(): pl.pallas_call(functools.partial(exchange_kernel, axes, sizes, per_peer),...  104 us
    all_gather x1, waiting for transfers between devices, on_device(): engine_full = lax.all_gather(engine_block, 'dp', axis=0, tiled=True)  25.7 us
  transfers between devices with their start and end apart: 2, of which 1 were waited for; matrix products, arithmetic and copies ran while one was open for 11% of the time, Pallas kernels for 53%

profile of v9, /device:TPU:6, one launch (start us, length us, event | category | flops | bytes accessed | tf_op | source)
XLA Modules:
  0.0 334.3 jit_solution(588727326501814285)
XLA Ops:
  10.8 117.5 %shard_map.76 = (bf16[32,256,256]{2,1,0:T(8,128)(2,1)}, bf16[16,128,512]{2,1,0:T(8,128)(2,1)S(1)}) custom-call(bf16[256,256]{1,0:T(8,128)(2,1)S(1)} %get-tuple-element.26.block_ref, bf16[128,512]{1,0:T(8,128)(2,1)S(1)} %copy-done), custom_call_target="tpu_custom_call" | custom-call | bytes 12582912 | tf_op jit(solution)/shard_map/pallas_call | solution.py:178
  128.3 2.5 convert_bitcast_fusion
  130.8 5.3 %copy.62 = f32[128,16,512]{0,2,1:T(8,128)} copy(f32[128,16,512]{2,0,1:T(8,128)} %convert_bitcast_fusion) | data formatting | bytes 8388608 | tf_op jit(solution)/shard_map/convert_element_type | solution.py:293
  136.7 1.9 fusion.7
  138.6 3.9 %copy.66 = bf16[128,16,512]{0,2,1:T(8,128)(2,1)} copy(bf16[128,16,512]{2,0,1:T(8,128)(2,1)} %fusion.7) | data formatting | bytes 4194304 | tf_op jit(solution)/shard_map/mul | solution.py:298
  142.8 4.0 %fusion.21 = bf16[16,2,8,128]{3,2,1,0:T(8,128)(2,1)S(1)} fusion(bf16[128,8192]{0,1:T(8,128)(2,1)} %bitcast.120, bf16[8192,256]{1,0:T(8,128)(2,1)} %bitcast.118), kind=kOutput, calls=%fused_computation.36 | convolution fusion | flops 536903680 | bytes 6356992 | tf_op jit(solution)/shard_map/dot_general | solution.py:303
  146.8 2.5 fusion.6
  149.3 25.7 %all-gather.2.cloned.1.call-done = bf16[8192,320]{1,0:T(8,128)(2,1)} async-done(((bf16[256,320]{1,0:T(8,128)(2,1)}), bf16[8192,320]{1,0:T(8,128)(2,1)}) %all-gather.2.cloned.1.call-update) | async-done | bytes 5242896 | tf_op jit(solution)/shard_map/all_gather | solution.py:289
  175.0 4.7 %convolution_convert_fusion.1 = bf16[128,320]{1,0:T(8,128)(2,1)S(1)} fusion(bf16[128,8192]{0,1:T(8,128)(2,1)} %fusion.6, bf16[8192,320]{1,0:T(8,128)(2,1)} %all-gather.2.cloned.1.call-done), kind=kOutput, calls=%fused_computation.30 | convolution fusion | flops 671129600 | bytes 7421952 | tf_op jit(solution)/shard_map/dot_general | solution.py:300
  180.3 22.9 %shard_map.77 = bf16[16,128,64]{2,1,0:T(8,128)(2,1)} custom-call(bf16[128,64]{1,0:T(8,128)(2,1)} %slice.56.refs_0_), custom_call_target="tpu_custom_call" | custom-call | bytes 524288 | tf_op jit(solution)/shard_map/pallas_call | solution.py:68
  207.0 1.4 copy.84
  208.4 21.7 %shard_map.78 = f32[16,128,64]{2,1,0:T(8,128)} custom-call(f32[16,128,64]{2,1,0:T(8,128)} %bitcast.121), custom_call_target="tpu_custom_call" | custom-call | bytes 1048576 | tf_op jit(solution)/shard_map/pallas_call | solution.py:68
  230.1 1.3 reduce_sum.84
  231.5 3.8 %convolution_bitcast_fusion = f32[16,2,256,64]{2,3,0,1:T(8,128)} fusion(bf16[2,16,256,128]{3,2,1,0:T(8,128)(2,1)} %bitcast.117, bf16[128,64]{0,1:T(8,128)(2,1)S(1)} %copy.85), kind=kOutput, calls=%fused_computation.15 | convolution fusion | flops 134217728 | bytes 4210688 | tf_op jit(solution)/shard_map/rk,rc->kc/dot_general | solution.py:382
  235.3 3.9 %copy.90 = f32[16,2,256,64]{3,2,1,0:T(8,128)} copy(f32[16,2,256,64]{2,3,0,1:T(8,128)} %convolution_bitcast_fusion) | data formatting | bytes 4194304 | tf_op jit(solution)/shard_map/transpose | solution.py:384
  239.2 4.7 %reshape.137 = f32[4096,128]{1,0:T(8,128)} reshape(f32[16,2,256,64]{3,2,1,0:T(8,128)} %copy.90) | data formatting | bytes 4194304 | tf_op jit(solution)/shard_map/reshape | solution.py:385
  245.3 5.0 %fusion.32 = f32[16,512,128]{1,2,0:T(8,128)S(1)} fusion(bf16[16,512,320]{2,1,0:T(8,128)(2,1)} %bitcast.116, bf16[128,64]{0,1:T(8,128)(2,1)S(1)} %copy.85, bf16[128,256]{0,1:T(8,128)(2,1)S(1)} %slice.64), kind=kOutput, calls=%fused_computation.61 | convolution fusion | flops 671252480 | bytes 9519104 | tf_op jit(solution)/shard_map/rc,pkc->prk/dot_general | solution.py:365
  250.4 3.5 %fusion.3 = (f32[128]{0:T(128)}, bf16[16,128,512]{2,1,0:T(8,128)(2,1)}) fusion(bf16[16,128,512]{2,1,0:T(8,128)(2,1)S(1)} %get-tuple-element.7, f32[16,512]{1,0:T(8,128)S(1)} %copy-done.5, f32[128]{0:T(128)S(1)} %add_rsqrt_fusion, f32[16,512,128]{1,2,0:T(8,128)S(1)} %fusion.32, bf16[16,512,256]{2,1,0:T(8,128)(2,1)S(1)} %bitcast.119, ...), kind=kOutput, calls=%fused_computation.6 | convolution fusion | flops 545259392 | bytes 12682240 | tf_op jit(solution)/shard_map/rc,pkc->prk/dot_general | solution.py:366
  253.9 41.9 %shard_map.79 = (bf16[16,128,512]{2,1,0:T(8,128)(2,1)}, f32[16,1,128]{2,1,0:T(1,128)}) custom-call(bf16[16,128,512]{2,1,0:T(8,128)(2,1)} %get-tuple-element.35.refs_0_, f32[1,128]{1,0:T(1,128)} %bitcast.135), custom_call_target="tpu_custom_call" | custom-call | bytes 4210688 | tf_op jit(solution)/shard_map/pallas_call | solution.py:68
  296.5 1.9 convert_reduce_fusion
  298.5 1.4 multiply_reduce_fusion
  299.9 17.9 %shard_map.80 = f32[32,1,512]{2,1,0:T(1,128)} custom-call(f32[1,512]{1,0:T(1,128)} %bitcast.134), custom_call_target="tpu_custom_call" | custom-call | bytes 131072 | tf_op jit(solution)/shard_map/pallas_call | solution.py:68
  317.8 1.5 reduce_sum.89
  319.3 6.5 %shard_map.81 = f32[128,128]{1,0:T(8,128)} custom-call(f32[2,128,128]{2,1,0:T(8,128)} %bitcast.132), custom_call_target="tpu_custom_call" | custom-call | bytes 393216 | tf_op jit(solution)/shard_map/pallas_call | solution.py:220
  (70 shorter events, 12.4 us)
Async XLA Ops:
  7.2 167.8 %all-gather.2.cloned.1.call-start = ((), (), s32[]{:S(2)}) async-start(), calls=%async_computation.1 | async-start | bytes 6488064 | tf_op jit(solution)/shard_map/all_gather | solution.py:289
  9.8 309.5 %reduce-scatter.2.cloned.1.call-start = ((), (), s32[]{:S(2)}) async-start(), calls=%async_computation.2 | async-start | bytes 2228224 | tf_op jit(solution)/shard_map/reduce_scatter | solution.py:390
  9.9 0.9 copy-start
  130.8 5.3 %copy-start.6 = (f32[8192]{0:T(1024)S(1)}, f32[8192]{0:T(1024)}, u32[]{:S(2)}) copy-start(f32[8192]{0:T(1024)} %param.7) | copy-start | bytes 98308
  136.2 6.4 %copy-start.4 = (f32[16,512]{1,0:T(8,128)}, f32[16,512]{1,0:T(8,128)S(1)}, u32[]{:S(2)}) copy-start(f32[16,512]{1,0:T(8,128)S(1)} %mul.295) | copy-start | bytes 98308
  136.7 5.9 %copy-start.11 = (bf16[128,512]{1,0:T(8,128)(2,1)S(1)}, bf16[128,512]{1,0:T(8,128)(2,1)}, u32[]{:S(2)}) copy-start(bf16[128,512]{1,0:T(8,128)(2,1)} %param.6) | copy-start | bytes 393220
  142.7 4.1 %copy-start.3 = (f32[128,16,512]{0,2,1:T(8,128)S(1)}, f32[128,16,512]{0,2,1:T(8,128)}, u32[]{:S(2)}) copy-start(f32[128,16,512]{0,2,1:T(8,128)} %copy.62) | copy-start | bytes 12582916
  205.0 0.7 copy-start.7
  205.0 0.7 copy-start.9
  239.2 5.5 %copy-start.8 = (bf16[128,64]{1,0:T(8,128)(2,1)S(1)}, bf16[128,64]{1,0:T(8,128)(2,1)}, u32[]{:S(2)}) copy-start(bf16[128,64]{1,0:T(8,128)(2,1)} %copy-done.7) | copy-start | bytes 49156
  239.2 5.5 %copy-start.10 = (bf16[128,64]{1,0:T(8,128)(2,1)S(1)}, bf16[128,64]{1,0:T(8,128)(2,1)}, u32[]{:S(2)}) copy-start(bf16[128,64]{1,0:T(8,128)(2,1)} %copy-done.9) | copy-start | bytes 49156
  245.3 5.0 %copy-start.2 = (bf16[32,256,256]{2,1,0:T(8,128)(2,1)S(1)}, bf16[32,256,256]{2,1,0:T(8,128)(2,1)}, u32[]{:S(2)}) copy-start(bf16[32,256,256]{2,1,0:T(8,128)(2,1)} %get-tuple-element.8) | copy-start | bytes 12582916
  245.3 5.0 %copy-start.5 = (f32[16,512]{1,0:T(8,128)S(1)}, f32[16,512]{1,0:T(8,128)}, u32[]{:S(2)}) copy-start(f32[16,512]{1,0:T(8,128)} %copy-done.4) | copy-start | bytes 98308
  253.9 44.5 %copy-start.1 = (bf16[128,512]{1,0:T(8,128)(2,1)S(1)}, bf16[128,512]{1,0:T(8,128)(2,1)}, u32[]{:S(2)}) copy-start(bf16[128,512]{1,0:T(8,128)(2,1)} %side_ref.1) | copy-start | bytes 393220
Sparse Core Ops, SparseCore 0:
  10.1 164.8 all-gather.1
  244.0 67.7 reduce-scatter.1

commit v10 on v9

--- a/solution.py
+++ b/solution.py
@@ -289,13 +289,13 @@
     engine_full = lax.all_gather(engine_block, "dp", axis=0, tiled=True)
     ring_blocks_out, input_blocks = ring_gather(w_query[:, split_cols:], inputs, 6)
     ring_full = ring_blocks_out.reshape(-1, query_cols - split_cols)
-    inputs_full = (
-        input_blocks.transpose(1, 0, 2).reshape(seq_length, model_width).astype(jnp.float32)
-    )
-    row_sum = jnp.sum(inputs_full * inputs_full, axis=1, keepdims=True)
+    input_values = input_blocks.astype(jnp.float32)
+    row_sum = jnp.sum(input_values * input_values, axis=(0, 2)).reshape(seq_length, 1)
     inv_rms = lax.rsqrt(row_sum / model_width + 1e-05)
-    unit_full = inputs_full * inv_rms
-    normed_full = (unit_full * gain[None, :]).astype(jnp.bfloat16)
+    gain_blocks = gain.reshape(tensor_count, 1, local_cols)
+    unit_blocks = input_values * inv_rms[None, :, :]
+    normed_blocks = (unit_blocks * gain_blocks).astype(jnp.bfloat16)
+    normed_full = normed_blocks.transpose(1, 0, 2).reshape(seq_length, model_width)
     unit_rows = inputs.astype(jnp.float32) * inv_rms
     engine_proj = jnp.dot(normed_full, engine_full, preferred_element_type=jnp.float32).astype(
         jnp.bfloat16
@@ -370,8 +370,6 @@
             preferred_element_type=jnp.float32,
         )
     ).astype(jnp.bfloat16)
-    unit_blocks = unit_full.reshape(seq_length, tensor_count, local_cols).transpose(1, 0, 2)
-    gain_blocks = gain.reshape(tensor_count, 1, local_cols)
     product_part = jnp.sum(
         normed_terms.astype(jnp.float32) * gain_blocks * unit_blocks, axis=(0, 2)
     ).reshape(1, seq_length)
@@ -379,7 +377,7 @@
     pair_count = 2
     ring_count = dp_count // pair_count
     keyval_partials = (
-        jnp.einsum("rk,rc->kc", normed_full, grad_keyval, preferred_element_type=jnp.float32)
+        jnp.einsum("prk,rc->pkc", normed_blocks, grad_keyval, preferred_element_type=jnp.float32)
         .reshape(pair_count, ring_count, -1, group_cols)
         .transpose(1, 0, 2, 3)
         .reshape(model_width // 2, 2 * group_cols)

time: 335 us -> 329 us (0.982)
  other arithmetic: 17 us -> 12 us
    pallas_call x4, Pallas kernels: 104 us -> 95.1 us  [exchange_multi(): pl.pallas_call(functools.partial(exchange_kernel, axes, sizes, per_peer),...]
    pallas_call x1, Pallas kernels: 117 us -> 123 us  [ring_gather(): pl.pallas_call(functools.partial(ring_gather_kernel, pair_count, ring_cou...]
    convert_element_type x1 -> x0, local copies, waits for them, and re-layouts: 5.34 us -> none  [on_device(): input_blocks.transpose(1, 0, 2).reshape(seq_length, model_width)]
    convert_element_type x2 -> x0, other arithmetic: 5.03 us -> none  [the longest x1 2.55 us: on_device(): input_blocks.transpose(1, 0, 2).reshape(seq_length, model_width)]
    transpose x1 -> x2, local copies, waits for them, and re-layouts: 3.91 us -> 7.87 us  [the longest x1 3.94 us: on_device(): normed_blocks.transpose(1, 0, 2).reshape(seq_length, model_width)]
    reshape x1 -> x2, local copies, waits for them, and re-layouts: 4.66 us -> 7.37 us  [on_device(): keyval_partials = jnp.einsum('prk,rc->pkc', normed_blocks, grad_keyval, p...]
  transfers between devices with their start and end apart: 2 -> 2, of which waited for: 1 -> 1; matrix products, arithmetic and copies ran while one was open for 11% -> 8% of each run, Pallas kernels for 53% -> 56%
where the time goes in v10:
time: 329 us; the launch traced here: 328 us
  Pallas kernels  225 us (68%)
  waiting for transfers between devices  28.1 us (9%)
  local copies, waits for them, and re-layouts  27.4 us (8%)
  matrix products  20.9 us (6%)
  between operations  14.4 us (4%)
  other arithmetic  12 us (4%)
    pallas_call x1, Pallas kernels, ring_gather(): pl.pallas_call(functools.partial(ring_gather_kernel, pair_count, ring_cou...  123 us
    pallas_call x4, Pallas kernels, exchange_multi(): pl.pallas_call(functools.partial(exchange_kernel, axes, sizes, per_peer),...  95.1 us
    all_gather x1, waiting for transfers between devices, on_device(): engine_full = lax.all_gather(engine_block, 'dp', axis=0, tiled=True)  28.1 us
    reshape x2, local copies, waits for them, and re-layouts, on_device(): keyval_partials = jnp.einsum('prk,rc->pkc', normed_blocks, grad_keyval, p...  7.37 us
  transfers between devices with their start and end apart: 2, of which 1 were waited for; matrix products, arithmetic and copies ran while one was open for 8% of the time, Pallas kernels for 56%

profile of v10, /device:TPU:6, one launch (start us, length us, event | category | flops | bytes accessed | tf_op | source)
XLA Modules:
  0.0 327.9 jit_solution(4653128649181414397)
XLA Ops:
  7.2 1.0 fusion.58
  11.6 123.4 %shard_map.76 = (bf16[32,256,256]{2,1,0:T(8,128)(2,1)}, bf16[16,128,512]{2,1,0:T(8,128)(2,1)S(1)}) custom-call(bf16[256,256]{1,0:T(8,128)(2,1)S(1)} %get-tuple-element.26.block_ref, bf16[128,512]{1,0:T(8,128)(2,1)S(1)} %copy-done), custom_call_target="tpu_custom_call" | custom-call | bytes 12582912 | tf_op jit(solution)/shard_map/pallas_call | solution.py:178
  135.5 2.0 fusion.21
  137.5 3.9 %copy.62 = bf16[128,16,512]{0,2,1:T(8,128)(2,1)} copy(bf16[128,16,512]{2,0,1:T(8,128)(2,1)} %fusion.21) | data formatting | bytes 4194304 | tf_op jit(solution)/shard_map/transpose | solution.py:298
  141.6 3.8 %fusion.18 = bf16[16,2,8,128]{3,2,1,0:T(8,128)(2,1)S(1)} fusion(bf16[128,8192]{0,1:T(8,128)(2,1)} %bitcast.104, bf16[8192,256]{1,0:T(8,128)(2,1)} %bitcast.106), kind=kOutput, calls=%fused_computation.30 | convolution fusion | flops 536903680 | bytes 6356992 | tf_op jit(solution)/shard_map/dot_general | solution.py:303
  145.4 28.1 %all-gather.2.cloned.1.call-done = bf16[8192,320]{1,0:T(8,128)(2,1)} async-done(((bf16[256,320]{1,0:T(8,128)(2,1)}), bf16[8192,320]{1,0:T(8,128)(2,1)}) %all-gather.2.cloned.1.call-update) | async-done | bytes 5242896 | tf_op jit(solution)/shard_map/all_gather | solution.py:289
  173.5 4.7 %convolution_convert_fusion.1 = bf16[128,320]{1,0:T(8,128)(2,1)S(1)} fusion(bf16[128,8192]{0,1:T(8,128)(2,1)} %bitcast.105, bf16[8192,320]{1,0:T(8,128)(2,1)} %all-gather.2.cloned.1.call-done), kind=kOutput, calls=%fused_computation.24 | convolution fusion | flops 671129600 | bytes 7421952 | tf_op jit(solution)/shard_map/dot_general | solution.py:300
  178.9 15.1 %shard_map.77 = bf16[16,128,64]{2,1,0:T(8,128)(2,1)} custom-call(bf16[128,64]{1,0:T(8,128)(2,1)} %slice.56.refs_0_), custom_call_target="tpu_custom_call" | custom-call | bytes 524288 | tf_op jit(solution)/shard_map/pallas_call | solution.py:68
  194.0 1.3 copy.64
  199.9 1.3 copy.83
  201.3 21.0 %shard_map.78 = f32[16,128,64]{2,1,0:T(8,128)} custom-call(f32[16,128,64]{2,1,0:T(8,128)} %bitcast.109), custom_call_target="tpu_custom_call" | custom-call | bytes 1048576 | tf_op jit(solution)/shard_map/pallas_call | solution.py:68
  222.3 1.3 reduce_sum.84
  224.5 2.5 copy.89
  227.0 2.7 reshape.128
  229.8 3.9 %copy.90 = f32[16,2,256,64]{3,2,1,0:T(8,128)} copy(f32[16,2,256,64]{2,0,1,3:T(8,128)} %bitcast.108) | data formatting | bytes 4194304 | tf_op jit(solution)/shard_map/transpose | solution.py:382
  233.7 4.6 %reshape.129 = f32[4096,128]{1,0:T(8,128)} reshape(f32[16,2,256,64]{3,2,1,0:T(8,128)} %copy.90) | data formatting | bytes 4194304 | tf_op jit(solution)/shard_map/reshape | solution.py:383
  239.8 5.0 %fusion.32 = f32[16,512,128]{1,2,0:T(8,128)S(1)} fusion(bf16[16,512,320]{2,1,0:T(8,128)(2,1)} %bitcast.103, bf16[128,64]{0,1:T(8,128)(2,1)S(1)} %copy.84, bf16[128,256]{0,1:T(8,128)(2,1)S(1)} %slice.64), kind=kOutput, calls=%fused_computation.57 | convolution fusion | flops 671252480 | bytes 9519104 | tf_op jit(solution)/shard_map/rc,pkc->prk/dot_general | solution.py:365
  244.8 3.5 %fusion.3 = (f32[128]{0:T(128)}, bf16[16,128,512]{2,1,0:T(8,128)(2,1)}) fusion(bf16[16,128,512]{2,1,0:T(8,128)(2,1)S(1)} %get-tuple-element.7, f32[16,512]{1,0:T(8,128)S(1)} %mul.265, f32[128]{0:T(128)S(1)} %add_rsqrt_fusion, f32[16,512,128]{1,2,0:T(8,128)S(1)} %fusion.32, bf16[16,512,256]{2,1,0:T(8,128)(2,1)S(1)} %bitcast.107, ...), kind=kOutput, calls=%fused_computation.5 | convolution fusion | flops 545259392 | bytes 12682240 | tf_op jit(solution)/shard_map/rc,pkc->prk/dot_general | solution.py:366
  248.4 42.6 %shard_map.79 = (bf16[16,128,512]{2,1,0:T(8,128)(2,1)}, f32[16,1,128]{2,1,0:T(1,128)}) custom-call(bf16[16,128,512]{2,1,0:T(8,128)(2,1)} %get-tuple-element.35.refs_0_, f32[1,128]{1,0:T(1,128)} %bitcast.123), custom_call_target="tpu_custom_call" | custom-call | bytes 4210688 | tf_op jit(solution)/shard_map/pallas_call | solution.py:68
  291.7 1.9 convert_reduce_fusion
  293.7 1.4 multiply_reduce_fusion
  295.0 16.4 %shard_map.80 = f32[32,1,512]{2,1,0:T(1,128)} custom-call(f32[1,512]{1,0:T(1,128)} %bitcast.122), custom_call_target="tpu_custom_call" | custom-call | bytes 131072 | tf_op jit(solution)/shard_map/pallas_call | solution.py:68
  311.4 1.5 reduce_sum.89
  312.9 6.5 %shard_map.81 = f32[128,128]{1,0:T(8,128)} custom-call(f32[2,128,128]{2,1,0:T(8,128)} %bitcast.120), custom_call_target="tpu_custom_call" | custom-call | bytes 393216 | tf_op jit(solution)/shard_map/pallas_call | solution.py:220
  (55 shorter events, 13.9 us)
Async XLA Ops:
  7.2 166.3 %all-gather.2.cloned.1.call-start = ((), (), s32[]{:S(2)}) async-start(), calls=%async_computation.1 | async-start | bytes 6488064 | tf_op jit(solution)/shard_map/all_gather | solution.py:289
  9.8 303.1 %reduce-scatter.2.cloned.1.call-start = ((), (), s32[]{:S(2)}) async-start(), calls=%async_computation.2 | async-start | bytes 2228224 | tf_op jit(solution)/shard_map/reduce_scatter | solution.py:388
  10.7 0.9 copy-start
  135.5 5.9 %copy-start.4 = (bf16[128,512]{1,0:T(8,128)(2,1)S(1)}, bf16[128,512]{1,0:T(8,128)(2,1)}, u32[]{:S(2)}) copy-start(bf16[128,512]{1,0:T(8,128)(2,1)} %param.6) | copy-start | bytes 393220
  195.3 0.7 copy-start.3
  239.8 5.0 %copy-start.2 = (bf16[32,256,256]{2,1,0:T(8,128)(2,1)S(1)}, bf16[32,256,256]{2,1,0:T(8,128)(2,1)}, u32[]{:S(2)}) copy-start(bf16[32,256,256]{2,1,0:T(8,128)(2,1)} %get-tuple-element.8) | copy-start | bytes 12582916
  248.4 45.3 %copy-start.1 = (bf16[128,512]{1,0:T(8,128)(2,1)S(1)}, bf16[128,512]{1,0:T(8,128)(2,1)}, u32[]{:S(2)}) copy-start(bf16[128,512]{1,0:T(8,128)(2,1)} %side_ref.1) | copy-start | bytes 393220
Sparse Core Ops, SparseCore 0:
  10.1 163.3 all-gather.1
  238.5 66.3 reduce-scatter.1

commit v11 on v10

--- a/solution.py
+++ b/solution.py
@@ -376,12 +376,22 @@
     dp_count = lax.axis_size("dp")
     pair_count = 2
     ring_count = dp_count // pair_count
-    keyval_partials = (
-        jnp.einsum("prk,rc->pkc", normed_blocks, grad_keyval, preferred_element_type=jnp.float32)
-        .reshape(pair_count, ring_count, -1, group_cols)
-        .transpose(1, 0, 2, 3)
-        .reshape(model_width // 2, 2 * group_cols)
-    )
+    block_rows = model_width // dp_count
+    normed_pairs = normed_full.reshape(
+        seq_length, pair_count, ring_count, block_rows // 2, 2
+    ).transpose(0, 2, 1, 3, 4)
+    keyval_partials = jnp.concatenate(
+        [
+            jnp.einsum(
+                "rbaq,rc->baqc",
+                normed_pairs[..., half],
+                grad_keyval,
+                preferred_element_type=jnp.float32,
+            )
+            for half in range(2)
+        ],
+        axis=-1,
+    ).reshape(model_width // 2, 2 * group_cols)
     ring_groups = [
         [pair * ring_count + slot for slot in range(ring_count)] for pair in range(pair_count)
     ]

time: 329 us -> 327 us (level)
  Pallas kernels: 225 us -> 231 us
  local copies, waits for them, and re-layouts: 27.4 us -> 22 us
  waiting for transfers between devices: 28.1 us -> 23.3 us
    reshape x2 -> x0, local copies, waits for them, and re-layouts: 7.37 us -> none  [on_device(): keyval_partials = jnp.einsum('prk,rc->pkc', normed_blocks, grad_keyval, p...]
    pallas_call x4, Pallas kernels: 95.1 us -> 102 us  [exchange_multi(): pl.pallas_call(functools.partial(exchange_kernel, axes, sizes, per_peer),...]
    another operation x0 -> x1, local copies, waits for them, and re-layouts: none -> 6.17 us  [on_device(): normed_full.reshape(seq_length, pair_count, ring_count, block_rows // 2, 2)]
    all_gather x1, waiting for transfers between devices: 28.1 us -> 23.3 us  [on_device(): engine_full = lax.all_gather(engine_block, 'dp', axis=0, tiled=True)]
    transpose x1 -> x0, local copies, waits for them, and re-layouts: 3.93 us -> none  [on_device(): keyval_partials = jnp.einsum('prk,rc->pkc', normed_blocks, grad_keyval, p...]
  transfers between devices with their start and end apart: 2 -> 2, of which waited for: 1 -> 1; matrix products, arithmetic and copies ran while one was open for 8% -> 10% of each run, Pallas kernels for 56% -> 56%
where the time goes in v11:
time: 327 us; the launch traced here: 326 us
  Pallas kernels  231 us (71%)
  waiting for transfers between devices  23.3 us (7%)
  local copies, waits for them, and re-layouts  22 us (7%)
  matrix products  21.6 us (7%)
  between operations  14.4 us (4%)
  other arithmetic  13.5 us (4%)
    pallas_call x1, Pallas kernels, ring_gather(): pl.pallas_call(functools.partial(ring_gather_kernel, pair_count, ring_cou...  122 us
    pallas_call x4, Pallas kernels, exchange_multi(): pl.pallas_call(functools.partial(exchange_kernel, axes, sizes, per_peer),...  102 us
    all_gather x1, waiting for transfers between devices, on_device(): engine_full = lax.all_gather(engine_block, 'dp', axis=0, tiled=True)  23.3 us
  transfers between devices with their start and end apart: 2, of which 1 were waited for; matrix products, arithmetic and copies ran while one was open for 10% of the time, Pallas kernels for 56%

profile of v11, /device:TPU:6, one launch (start us, length us, event | category | flops | bytes accessed | tf_op | source)
XLA Modules:
  0.0 325.7 jit_solution(3767889419235541393)
XLA Ops:
  11.6 122.3 %shard_map.76 = (bf16[32,256,256]{2,1,0:T(8,128)(2,1)}, bf16[16,128,512]{2,1,0:T(8,128)(2,1)S(1)}) custom-call(bf16[256,256]{1,0:T(8,128)(2,1)S(1)} %get-tuple-element.26.block_ref, bf16[128,512]{1,0:T(8,128)(2,1)S(1)} %copy-done), custom_call_target="tpu_custom_call" | custom-call | bytes 12582912 | tf_op jit(solution)/shard_map/pallas_call | solution.py:178
  134.4 1.9 fusion.5
  136.3 3.9 %copy.63 = bf16[128,16,512]{0,2,1:T(8,128)(2,1)} copy(bf16[128,16,512]{2,0,1:T(8,128)(2,1)} %fusion.5) | data formatting | bytes 4194304 | tf_op jit(solution)/shard_map/transpose | solution.py:298
  140.3 6.2 %copy.91 = bf16[128,2,16,128,2]{3,0,1,2,4:T(8,128)(2,1)} copy(bf16[128,2,16,128,2]{0,4,3,2,1:T(2,128)(2,1)} %bitcast.112) | data formatting | bytes 4194304 | tf_op jit(solution)/shard_map/reshape;reshape | solution.py:380
  146.6 3.8 %fusion.19 = bf16[16,2,8,128]{3,2,1,0:T(8,128)(2,1)S(1)} fusion(bf16[128,8192]{0,1:T(8,128)(2,1)} %bitcast.113, bf16[8192,256]{1,0:T(8,128)(2,1)} %bitcast.115), kind=kOutput, calls=%fused_computation.32 | convolution fusion | flops 536903680 | bytes 6356992 | tf_op jit(solution)/shard_map/dot_general | solution.py:303
  150.4 23.3 %all-gather.2.cloned.1.call-done = bf16[8192,320]{1,0:T(8,128)(2,1)} async-done(((bf16[256,320]{1,0:T(8,128)(2,1)}), bf16[8192,320]{1,0:T(8,128)(2,1)}) %all-gather.2.cloned.1.call-update) | async-done | bytes 5242896 | tf_op jit(solution)/shard_map/all_gather | solution.py:289
  173.7 4.7 %convolution_convert_fusion.1 = bf16[128,320]{1,0:T(8,128)(2,1)S(1)} fusion(bf16[128,8192]{0,1:T(8,128)(2,1)} %bitcast.114, bf16[8192,320]{1,0:T(8,128)(2,1)} %all-gather.2.cloned.1.call-done), kind=kOutput, calls=%fused_computation.26 | convolution fusion | flops 671129600 | bytes 7421952 | tf_op jit(solution)/shard_map/dot_general | solution.py:300
  179.0 20.4 %shard_map.77 = bf16[16,128,64]{2,1,0:T(8,128)(2,1)} custom-call(bf16[128,64]{1,0:T(8,128)(2,1)} %slice.64.refs_0_), custom_call_target="tpu_custom_call" | custom-call | bytes 524288 | tf_op jit(solution)/shard_map/pallas_call | solution.py:68
  199.4 1.3 copy.65
  203.2 1.4 copy.84
  204.6 21.4 %shard_map.78 = f32[16,128,64]{2,1,0:T(8,128)} custom-call(f32[16,128,64]{2,1,0:T(8,128)} %bitcast.120), custom_call_target="tpu_custom_call" | custom-call | bytes 1048576 | tf_op jit(solution)/shard_map/pallas_call | solution.py:68
  226.0 1.3 reduce_sum.84
  227.4 1.5 fusion.21
  228.9 1.5 fusion.20
  230.4 1.5 pad_maximum_fusion
  232.0 2.9 copy.92
  236.3 5.0 %fusion.32 = f32[16,512,128]{1,2,0:T(8,128)S(1)} fusion(bf16[16,512,320]{2,1,0:T(8,128)(2,1)} %bitcast.111, bf16[128,64]{0,1:T(8,128)(2,1)S(1)} %copy.85, bf16[128,256]{0,1:T(8,128)(2,1)S(1)} %slice.72), kind=kOutput, calls=%fused_computation.61 | convolution fusion | flops 671252480 | bytes 9519104 | tf_op jit(solution)/shard_map/rc,pkc->prk/dot_general | solution.py:365
  241.4 3.5 %fusion.3 = (f32[128]{0:T(128)}, bf16[16,128,512]{2,1,0:T(8,128)(2,1)}) fusion(bf16[16,128,512]{2,1,0:T(8,128)(2,1)S(1)} %get-tuple-element.7, f32[16,512]{1,0:T(8,128)S(1)} %copy-done.4, f32[128]{0:T(128)S(1)} %add_rsqrt_fusion, f32[16,512,128]{1,2,0:T(8,128)S(1)} %fusion.32, bf16[16,512,256]{2,1,0:T(8,128)(2,1)S(1)} %bitcast.116, ...), kind=kOutput, calls=%fused_computation.5 | convolution fusion | flops 545259392 | bytes 12682240 | tf_op jit(solution)/shard_map/rc,pkc->prk/dot_general | solution.py:366
  244.9 42.5 %shard_map.79 = (bf16[16,128,512]{2,1,0:T(8,128)(2,1)}, f32[16,1,128]{2,1,0:T(1,128)}) custom-call(bf16[16,128,512]{2,1,0:T(8,128)(2,1)} %get-tuple-element.35.refs_0_, f32[1,128]{1,0:T(1,128)} %bitcast.134), custom_call_target="tpu_custom_call" | custom-call | bytes 4210688 | tf_op jit(solution)/shard_map/pallas_call | solution.py:68
  288.2 1.9 convert_reduce_fusion
  290.1 1.4 multiply_reduce_fusion
  291.5 17.7 %shard_map.80 = f32[32,1,512]{2,1,0:T(1,128)} custom-call(f32[1,512]{1,0:T(1,128)} %bitcast.133), custom_call_target="tpu_custom_call" | custom-call | bytes 131072 | tf_op jit(solution)/shard_map/pallas_call | solution.py:68
  309.2 1.5 reduce_sum.89
  310.7 6.5 %shard_map.81 = f32[128,128]{1,0:T(8,128)} custom-call(f32[2,128,128]{2,1,0:T(8,128)} %bitcast.131), custom_call_target="tpu_custom_call" | custom-call | bytes 393216 | tf_op jit(solution)/shard_map/pallas_call | solution.py:220
  (65 shorter events, 11.9 us)
Async XLA Ops:
  7.2 166.5 %all-gather.2.cloned.1.call-start = ((), (), s32[]{:S(2)}) async-start(), calls=%async_computation.1 | async-start | bytes 6488064 | tf_op jit(solution)/shard_map/all_gather | solution.py:289
  9.8 300.9 %reduce-scatter.2.cloned.1.call-start = ((), (), s32[]{:S(2)}) async-start(), calls=%async_computation.2 | async-start | bytes 2228224 | tf_op jit(solution)/shard_map/reduce_scatter | solution.py:398
  10.7 129.6 %copy-start.3 = (f32[16,512]{1,0:T(8,128)}, f32[16,512]{1,0:T(8,128)S(1)}, u32[]{:S(2)}) copy-start(f32[16,512]{1,0:T(8,128)S(1)} %mul.265) | copy-start | bytes 98308
  10.7 0.9 copy-start
  134.4 5.8 %copy-start.9 = (bf16[128,512]{1,0:T(8,128)(2,1)S(1)}, bf16[128,512]{1,0:T(8,128)(2,1)}, u32[]{:S(2)}) copy-start(bf16[128,512]{1,0:T(8,128)(2,1)} %param.6) | copy-start | bytes 393220
  201.2 0.7 copy-start.5
  201.2 0.7 copy-start.7
  232.0 3.7 %copy-start.6 = (bf16[128,64]{1,0:T(8,128)(2,1)S(1)}, bf16[128,64]{1,0:T(8,128)(2,1)}, u32[]{:S(2)}) copy-start(bf16[128,64]{1,0:T(8,128)(2,1)} %copy-done.5) | copy-start | bytes 49156
  232.0 3.7 %copy-start.8 = (bf16[128,64]{1,0:T(8,128)(2,1)S(1)}, bf16[128,64]{1,0:T(8,128)(2,1)}, u32[]{:S(2)}) copy-start(bf16[128,64]{1,0:T(8,128)(2,1)} %copy-done.7) | copy-start | bytes 49156
  236.3 5.0 %copy-start.2 = (bf16[32,256,256]{2,1,0:T(8,128)(2,1)S(1)}, bf16[32,256,256]{2,1,0:T(8,128)(2,1)}, u32[]{:S(2)}) copy-start(bf16[32,256,256]{2,1,0:T(8,128)(2,1)} %get-tuple-element.8) | copy-start | bytes 12582916
  236.3 5.0 %copy-start.4 = (f32[16,512]{1,0:T(8,128)S(1)}, f32[16,512]{1,0:T(8,128)}, u32[]{:S(2)}) copy-start(f32[16,512]{1,0:T(8,128)} %copy-done.3) | copy-start | bytes 98308
  244.9 45.2 %copy-start.1 = (bf16[128,512]{1,0:T(8,128)(2,1)S(1)}, bf16[128,512]{1,0:T(8,128)(2,1)}, u32[]{:S(2)}) copy-start(bf16[128,512]{1,0:T(8,128)(2,1)} %side_ref.1) | copy-start | bytes 393220
Sparse Core Ops, SparseCore 0:
  10.1 163.5 all-gather.1
  235.0 69.4 reduce-scatter.1

commit v12 on v11

--- a/solution.py
+++ b/solution.py
@@ -230,6 +230,93 @@
     )(blocks)
 
 
+def group_kernel(routes, src_ref, out_ref, send_sems, recv_sems):
+    me = lax.axis_index("tensor")
+    dests, sources = routes(me)
+    barrier = pltpu.get_barrier_semaphore()
+    count = jnp.int32(0)
+    for peer in [d for d, _, _ in dests] + sources:
+
+        @pl.when(peer != me)
+        def _():
+            pl.semaphore_signal(barrier, inc=1, device_id={"tensor": peer}, device_id_type=MESH)
+
+        count = count + (peer != me).astype(jnp.int32)
+    pl.semaphore_wait(barrier, count)
+    copies = []
+    for index, (peer, slot, block) in enumerate(dests):
+        copy = pltpu.make_async_remote_copy(
+            src_ref=src_ref.at[block],
+            dst_ref=out_ref.at[slot],
+            send_sem=send_sems.at[index],
+            recv_sem=recv_sems.at[slot],
+            device_id={"tensor": peer},
+            device_id_type=MESH,
+        )
+        copies.append(copy)
+
+        @pl.when(peer != me)
+        def _():
+            copy.start()
+
+        @pl.when(peer == me)
+        def _():
+            out_ref[slot] = src_ref[block]
+
+    for (peer, _, _), copy in zip(dests, copies):
+
+        @pl.when(peer != me)
+        def _():
+            copy.wait_send()
+
+    for slot, peer in enumerate(sources):
+        arrival = pltpu.make_async_remote_copy(
+            src_ref=src_ref.at[0],
+            dst_ref=out_ref.at[slot],
+            send_sem=send_sems.at[0],
+            recv_sem=recv_sems.at[slot],
+            device_id={"tensor": peer},
+            device_id_type=MESH,
+        )
+
+        @pl.when(peer != me)
+        def _():
+            arrival.wait_recv()
+
+
+def group_exchange(routes, blocks, slots, collective_id):
+    return pl.pallas_call(
+        functools.partial(group_kernel, routes),
+        out_shape=jax.ShapeDtypeStruct((slots,) + blocks.shape[1:], blocks.dtype),
+        in_specs=[pl.BlockSpec(memory_space=pltpu.VMEM)],
+        out_specs=pl.BlockSpec(memory_space=pltpu.VMEM),
+        scratch_shapes=[pltpu.SemaphoreType.DMA((slots,)), pltpu.SemaphoreType.DMA((slots,))],
+        compiler_params=pltpu.CompilerParams(collective_id=collective_id, has_side_effects=True),
+        cost_estimate=pl.CostEstimate(
+            flops=0, bytes_accessed=2 * slots * blocks[0].size * blocks.dtype.itemsize, transcendentals=0
+        ),
+    )(blocks)
+
+
+def keyval_routes(me):
+    head_group = lax.rem(me // 2, KV_HEADS)
+    slot = 2 * (me // (2 * KV_HEADS)) + lax.rem(me, 2)
+    dests = [(KV_HEADS * head_group + m, slot, 0) for m in range(KV_HEADS)]
+    group = me // KV_HEADS
+    sources = [2 * group, 2 * group + 1, 2 * KV_HEADS + 2 * group, 2 * KV_HEADS + 2 * group + 1]
+    return dests, sources
+
+
+def term_routes(me):
+    group = me // KV_HEADS
+    slot = lax.rem(me, KV_HEADS)
+    targets = [2 * group, 2 * group + 1, 2 * KV_HEADS + 2 * group, 2 * KV_HEADS + 2 * group + 1]
+    dests = [(target, slot, m) for m, target in enumerate(targets)]
+    head_group = lax.rem(me // 2, KV_HEADS)
+    sources = [KV_HEADS * head_group + m for m in range(KV_HEADS)]
+    return dests, sources
+
+
 HD = 128
 KV_HEADS = 4
 HEADS_DEV = 4
@@ -305,13 +392,9 @@
     )
     query_proj = jnp.concatenate([engine_proj[:, :split_cols], ring_proj], axis=1)
     keyval_part = engine_proj[:, split_cols:]
-    (keyval_blocks,) = exchange("tensor", [keyval_part], [False], 1)
-    keyval_full = keyval_blocks.transpose(1, 0, 2).reshape(seq_length, keyval_total)
-    group_slot = tensor_slot // devices_per_group
-    key_block = lax.dynamic_slice_in_dim(keyval_full, group_slot * head_size, head_size, 1)
-    value_block = lax.dynamic_slice_in_dim(
-        keyval_full, (kv_heads + group_slot) * head_size, head_size, 1
-    )
+    keyval_pieces = group_exchange(keyval_routes, keyval_part[None], 4, 1)
+    key_block = jnp.concatenate([keyval_pieces[0], keyval_pieces[1]], axis=1)
+    value_block = jnp.concatenate([keyval_pieces[2], keyval_pieces[3]], axis=1)
     cosine_table, sine_table = rope_tables(seq_length, head_size)
     cos_heads = cosine_table[:, None, :]
     sin_heads = sine_table[:, None, :]
@@ -348,15 +431,11 @@
         .astype(jnp.bfloat16)
         .reshape(seq_length, heads_here * head_size)
     )
-    grad_terms = jnp.zeros((seq_length, keyval_total), jnp.float32)
-    grad_terms = lax.dynamic_update_slice_in_dim(
-        grad_terms, unrotate(grad_krot, cosine_table, sine_table), group_slot * head_size, 1
-    )
-    grad_terms = lax.dynamic_update_slice_in_dim(
-        grad_terms, grad_value, (kv_heads + group_slot) * head_size, 1
-    )
-    term_blocks = grad_terms.reshape(seq_length, tensor_count, group_cols).transpose(1, 0, 2)
-    (keyval_terms,) = exchange("tensor", [term_blocks], [True], 2)
+    grad_key = unrotate(grad_krot, cosine_table, sine_table)
+    term_blocks = jnp.stack(
+        [grad_key[:, :group_cols], grad_key[:, group_cols:], grad_value[:, :group_cols], grad_value[:, group_cols:]]
+    )
+    keyval_terms = group_exchange(term_routes, term_blocks, 4, 2)
     grad_keyval = jnp.sum(keyval_terms, axis=0).astype(jnp.bfloat16)
     engine_blocks = engine_full.reshape(tensor_count, local_cols, split_cols + group_cols)
     ring_blocks = ring_full.reshape(tensor_count, local_cols, query_cols - split_cols)

time: 327 us -> 318 us (0.972)
  Pallas kernels: 231 us -> 224 us
    pallas_call x4 -> x2, Pallas kernels: 102 us -> 66.3 us  [exchange_multi(): pl.pallas_call(functools.partial(exchange_kernel, axes, sizes, per_peer),...]
    pallas_call x0 -> x2, Pallas kernels: none -> 27.4 us  [group_exchange(): pl.pallas_call(functools.partial(group_kernel, routes), out_shape=jax.Sha...]
  transfers between devices with their start and end apart: 2 -> 2, of which waited for: 1 -> 1; matrix products, arithmetic and copies ran while one was open for 10% -> 10% of each run, Pallas kernels for 56% -> 60%
where the time goes in v12:
time: 318 us; the launch traced here: 316 us
  Pallas kernels  224 us (70%)
  waiting for transfers between devices  22.1 us (7%)
  matrix products  21.7 us (7%)
  local copies, waits for them, and re-layouts  19.9 us (6%)
  between operations  14.3 us (4%)
  other arithmetic  13.8 us (4%)
    pallas_call x1, Pallas kernels, ring_gather(): pl.pallas_call(functools.partial(ring_gather_kernel, pair_count, ring_cou...  123 us
    pallas_call x2, Pallas kernels, exchange_multi(): pl.pallas_call(functools.partial(exchange_kernel, axes, sizes, per_peer),...  66.3 us
    pallas_call x2, Pallas kernels, group_exchange(): pl.pallas_call(functools.partial(group_kernel, routes), out_shape=jax.Sha...  27.4 us
    all_gather x1, waiting for transfers between devices, on_device(): engine_full = lax.all_gather(engine_block, 'dp', axis=0, tiled=True)  22.1 us
    pallas_call x1, Pallas kernels, pair_sum(): pl.pallas_call(functools.partial(pair_sum_kernel, ring_count), out_shape=...  6.5 us
  transfers between devices with their start and end apart: 2, of which 1 were waited for; matrix products, arithmetic and copies ran while one was open for 10% of the time, Pallas kernels for 60%

profile of v12, /device:TPU:6, one launch (start us, length us, event | category | flops | bytes accessed | tf_op | source)
XLA Modules:
  0.0 315.6 jit_solution(3803236138864764448)
XLA Ops:
  7.2 1.0 fusion.56
  10.6 0.9 copy-done
  11.5 123.5 %shard_map.76 = (bf16[32,256,256]{2,1,0:T(8,128)(2,1)}, bf16[16,128,512]{2,1,0:T(8,128)(2,1)S(1)}) custom-call(bf16[256,256]{1,0:T(8,128)(2,1)S(1)} %get-tuple-element.26.block_ref, bf16[128,512]{1,0:T(8,128)(2,1)S(1)} %copy-done), custom_call_target="tpu_custom_call" | custom-call | bytes 12582912 | tf_op jit(solution)/shard_map/pallas_call | solution.py:178
  135.5 1.9 fusion.5
  137.4 3.9 %copy.61 = bf16[128,16,512]{0,2,1:T(8,128)(2,1)} copy(bf16[128,16,512]{2,0,1:T(8,128)(2,1)} %fusion.5) | data formatting | bytes 4194304 | tf_op jit(solution)/shard_map/transpose | solution.py:385
  141.5 6.2 %copy.86 = bf16[128,2,16,128,2]{3,0,1,2,4:T(8,128)(2,1)} copy(bf16[128,2,16,128,2]{0,4,3,2,1:T(2,128)(2,1)} %bitcast.123) | data formatting | bytes 4194304 | tf_op jit(solution)/shard_map/reshape;reshape | solution.py:459
  147.7 3.8 %fusion.18 = bf16[16,2,8,128]{3,2,1,0:T(8,128)(2,1)S(1)} fusion(bf16[128,8192]{0,1:T(8,128)(2,1)} %bitcast.124, bf16[8192,256]{1,0:T(8,128)(2,1)} %bitcast.126), kind=kOutput, calls=%fused_computation.31 | convolution fusion | flops 536903680 | bytes 6356992 | tf_op jit(solution)/shard_map/dot_general | solution.py:390
  151.5 22.1 %all-gather.2.cloned.1.call-done = bf16[8192,320]{1,0:T(8,128)(2,1)} async-done(((bf16[256,320]{1,0:T(8,128)(2,1)}), bf16[8192,320]{1,0:T(8,128)(2,1)}) %all-gather.2.cloned.1.call-update) | async-done | bytes 5242896 | tf_op jit(solution)/shard_map/all_gather | solution.py:376
  173.6 4.7 %convolution_convert_fusion.1 = bf16[128,320]{1,0:T(8,128)(2,1)S(1)} fusion(bf16[128,8192]{0,1:T(8,128)(2,1)} %bitcast.125, bf16[8192,320]{1,0:T(8,128)(2,1)} %all-gather.2.cloned.1.call-done), kind=kOutput, calls=%fused_computation.26 | convolution fusion | flops 671129600 | bytes 7421952 | tf_op jit(solution)/shard_map/dot_general | solution.py:387
  178.9 14.2 %shard_map.77 = bf16[4,128,64]{2,1,0:T(8,128)(2,1)} custom-call(bf16[1,128,64]{2,1,0:T(8,128)(2,1)} %slice_bitcast_fusion.9.src_ref), custom_call_target="tpu_custom_call" | custom-call | bytes 131072 | tf_op jit(solution)/shard_map/pallas_call | solution.py:288
  197.0 13.2 %shard_map.78 = f32[4,128,64]{2,1,0:T(8,128)} custom-call(f32[4,128,64]{2,1,0:T(8,128)} %pad_maximum_fusion.1.src_ref), custom_call_target="tpu_custom_call" | custom-call | bytes 262144 | tf_op jit(solution)/shard_map/pallas_call | solution.py:288
  210.2 1.0 reduce_sum.84
  211.3 1.5 fusion.20
  212.8 1.5 fusion.19
  214.3 1.5 pad_maximum_fusion
  215.8 2.9 copy.87
  220.2 5.0 %fusion.31 = f32[16,512,128]{1,2,0:T(8,128)S(1)} fusion(bf16[16,512,320]{2,1,0:T(8,128)(2,1)} %bitcast.122, bf16[128,64]{0,1:T(8,128)(2,1)S(1)} %copy.80, bf16[128,256]{0,1:T(8,128)(2,1)S(1)} %slice.96), kind=kOutput, calls=%fused_computation.61 | convolution fusion | flops 671252480 | bytes 9519104 | tf_op jit(solution)/shard_map/rc,pkc->prk/dot_general | solution.py:444
  225.2 3.5 %fusion.3 = (f32[128]{0:T(128)}, bf16[16,128,512]{2,1,0:T(8,128)(2,1)}) fusion(bf16[16,128,512]{2,1,0:T(8,128)(2,1)S(1)} %get-tuple-element.7, f32[16,512]{1,0:T(8,128)S(1)} %mul.257, f32[128]{0:T(128)S(1)} %add_rsqrt_fusion, f32[16,512,128]{1,2,0:T(8,128)S(1)} %fusion.31, bf16[16,512,256]{2,1,0:T(8,128)(2,1)S(1)} %bitcast.127, ...), kind=kOutput, calls=%fused_computation.5 | convolution fusion | flops 545259392 | bytes 12682240 | tf_op jit(solution)/shard_map/rc,pkc->prk/dot_general | solution.py:445
  228.8 48.8 %shard_map.79 = (bf16[16,128,512]{2,1,0:T(8,128)(2,1)}, f32[16,1,128]{2,1,0:T(1,128)}) custom-call(bf16[16,128,512]{2,1,0:T(8,128)(2,1)} %get-tuple-element.41.refs_0_, f32[1,128]{1,0:T(1,128)} %bitcast.139), custom_call_target="tpu_custom_call" | custom-call | bytes 4210688 | tf_op jit(solution)/shard_map/pallas_call | solution.py:68
  278.3 1.9 convert_reduce_fusion
  280.2 1.4 multiply_reduce_fusion
  281.6 17.5 %shard_map.80 = f32[32,1,512]{2,1,0:T(1,128)} custom-call(f32[1,512]{1,0:T(1,128)} %bitcast.138), custom_call_target="tpu_custom_call" | custom-call | bytes 131072 | tf_op jit(solution)/shard_map/pallas_call | solution.py:68
  299.1 1.5 reduce_sum.89
  300.6 6.5 %shard_map.81 = f32[128,128]{1,0:T(8,128)} custom-call(f32[2,128,128]{2,1,0:T(8,128)} %bitcast.136), custom_call_target="tpu_custom_call" | custom-call | bytes 393216 | tf_op jit(solution)/shard_map/pallas_call | solution.py:220
  (48 shorter events, 11.5 us)
Async XLA Ops:
  7.2 166.4 %all-gather.2.cloned.1.call-start = ((), (), s32[]{:S(2)}) async-start(), calls=%async_computation.1 | async-start | bytes 6488064 | tf_op jit(solution)/shard_map/all_gather | solution.py:376
  9.8 290.8 %reduce-scatter.2.cloned.1.call-start = ((), (), s32[]{:S(2)}) async-start(), calls=%async_computation.2 | async-start | bytes 2228224 | tf_op jit(solution)/shard_map/reduce_scatter | solution.py:477
  10.6 0.9 copy-start
  135.5 5.8 %copy-start.3 = (bf16[128,512]{1,0:T(8,128)(2,1)S(1)}, bf16[128,512]{1,0:T(8,128)(2,1)}, u32[]{:S(2)}) copy-start(bf16[128,512]{1,0:T(8,128)(2,1)} %param.6) | copy-start | bytes 393220
  220.2 5.0 %copy-start.2 = (bf16[32,256,256]{2,1,0:T(8,128)(2,1)S(1)}, bf16[32,256,256]{2,1,0:T(8,128)(2,1)}, u32[]{:S(2)}) copy-start(bf16[32,256,256]{2,1,0:T(8,128)(2,1)} %get-tuple-element.8) | copy-start | bytes 12582916
  228.8 51.4 %copy-start.1 = (bf16[128,512]{1,0:T(8,128)(2,1)S(1)}, bf16[128,512]{1,0:T(8,128)(2,1)}, u32[]{:S(2)}) copy-start(bf16[128,512]{1,0:T(8,128)(2,1)} %side_ref.1) | copy-start | bytes 393220
Sparse Core Ops, SparseCore 0:
  10.1 163.4 all-gather.1
  218.9 73.9 reduce-scatter.1

commit v13 on v12

--- a/solution.py
+++ b/solution.py
@@ -456,20 +456,26 @@
     pair_count = 2
     ring_count = dp_count // pair_count
     block_rows = model_width // dp_count
-    normed_pairs = normed_full.reshape(
-        seq_length, pair_count, ring_count, block_rows // 2, 2
-    ).transpose(0, 2, 1, 3, 4)
-    keyval_partials = jnp.concatenate(
+    normed_pairs = normed_full.reshape(seq_length, pair_count, ring_count, block_rows // 2, 2)
+    zero_cols = jnp.zeros_like(grad_keyval)
+    paired_grads = jnp.stack(
+        [
+            jnp.concatenate([grad_keyval, zero_cols], axis=1),
+            jnp.concatenate([zero_cols, grad_keyval], axis=1),
+        ],
+        axis=1,
+    )
+    keyval_partials = jnp.stack(
         [
             jnp.einsum(
-                "rbaq,rc->baqc",
-                normed_pairs[..., half],
-                grad_keyval,
+                "rbqt,rtc->bqc",
+                normed_pairs[:, pair],
+                paired_grads,
                 preferred_element_type=jnp.float32,
             )
-            for half in range(2)
+            for pair in range(pair_count)
         ],
-        axis=-1,
+        axis=1,
     ).reshape(model_width // 2, 2 * group_cols)
     ring_groups = [
         [pair * ring_count + slot for slot in range(ring_count)] for pair in range(pair_count)

time: 318 us -> 322 us (1.013)
  Pallas kernels: 224 us -> 219 us
  waiting for transfers between devices: 22.1 us -> 26.6 us
  other arithmetic: 13.8 us -> 17.2 us
    another operation x1 -> x2, local copies, waits for them, and re-layouts: 6.15 us -> 1.48 us  [the longest x1 1.47 us: on_device(): jnp.stack([jnp.einsum('rbqt,rtc->bqc', normed_pairs[:, pair], paired_grad...]
    all_gather x1, waiting for transfers between devices: 22.1 us -> 26.6 us  [on_device(): engine_full = lax.all_gather(engine_block, 'dp', axis=0, tiled=True)]
    slice x0 -> x1, local copies, waits for them, and re-layouts: none -> 3.59 us  [on_device(): normed_pairs[:, pair]]
  transfers between devices with their start and end apart: 2 -> 2, of which waited for: 1 -> 1; matrix products, arithmetic and copies ran while one was open for 10% -> 10% of each run, Pallas kernels for 60% -> 59%
where the time goes in v13:
time: 322 us; the launch traced here: 319 us
  Pallas kernels  219 us (68%)
  waiting for transfers between devices  26.6 us (8%)
  matrix products  23.6 us (7%)
  local copies, waits for them, and re-layouts  18.4 us (6%)
  other arithmetic  17.2 us (5%)
  between operations  14.4 us (4%)
    pallas_call x1, Pallas kernels, ring_gather(): pl.pallas_call(functools.partial(ring_gather_kernel, pair_count, ring_cou...  120 us
    pallas_call x2, Pallas kernels, exchange_multi(): pl.pallas_call(functools.partial(exchange_kernel, axes, sizes, per_peer),...  66.4 us
    all_gather x1, waiting for transfers between devices, on_device(): engine_full = lax.all_gather(engine_block, 'dp', axis=0, tiled=True)  26.6 us
    pallas_call x2, Pallas kernels, group_exchange(): pl.pallas_call(functools.partial(group_kernel, routes), out_shape=jax.Sha...  25.7 us
    pallas_call x1, Pallas kernels, pair_sum(): pl.pallas_call(functools.partial(pair_sum_kernel, ring_count), out_shape=...  6.5 us
  transfers between devices with their start and end apart: 2, of which 1 were waited for; matrix products, arithmetic and copies ran while one was open for 10% of the time, Pallas kernels for 59%

profile of v13, /device:TPU:6, one launch (start us, length us, event | category | flops | bytes accessed | tf_op | source)
XLA Modules:
  0.0 319.3 jit_solution(5770485022189197096)
XLA Ops:
  11.5 120.4 %shard_map.76 = (bf16[32,256,256]{2,1,0:T(8,128)(2,1)}, bf16[16,128,512]{2,1,0:T(8,128)(2,1)S(1)}) custom-call(bf16[256,256]{1,0:T(8,128)(2,1)S(1)} %get-tuple-element.28.block_ref, bf16[128,512]{1,0:T(8,128)(2,1)S(1)} %copy-done), custom_call_target="tpu_custom_call" | custom-call | bytes 12582912 | tf_op jit(solution)/shard_map/pallas_call | solution.py:178
  133.0 1.9 fusion.5
  134.9 3.9 %copy.66 = bf16[128,16,512]{0,2,1:T(8,128)(2,1)} copy(bf16[128,16,512]{2,0,1:T(8,128)(2,1)} %fusion.5) | data formatting | bytes 4194304 | tf_op jit(solution)/shard_map/transpose | solution.py:385
  140.1 3.6 %fusion.54 = (bf16[128,1,16,128,2]{0,4,3,2,1:T(2,128)(2,1)}, bf16[128,1,16,128,2]{0,4,3,2,1:T(2,128)(2,1)S(1)}) fusion(bf16[128,2,16,128,2]{0,4,3,2,1:T(2,128)(2,1)} %bitcast.132), kind=kLoop, calls=%fused_computation.107 | loop fusion | bytes 4194304 | tf_op jit(solution)/shard_map/slice | solution.py:472
  143.7 3.2 %fusion.18 = bf16[16,2,8,128]{3,2,1,0:T(8,128)(2,1)S(1)} fusion(bf16[128,8192]{0,1:T(8,128)(2,1)S(1)} %bitcast.134, bf16[8192,256]{1,0:T(8,128)(2,1)} %bitcast.135), kind=kOutput, calls=%fused_computation.33 | convolution fusion | flops 536903680 | bytes 6356992 | tf_op jit(solution)/shard_map/dot_general | solution.py:390
  146.9 26.6 %all-gather.2.cloned.1.call-done = bf16[8192,320]{1,0:T(8,128)(2,1)} async-done(((bf16[256,320]{1,0:T(8,128)(2,1)}), bf16[8192,320]{1,0:T(8,128)(2,1)}) %all-gather.2.cloned.1.call-update) | async-done | bytes 5242896 | tf_op jit(solution)/shard_map/all_gather | solution.py:376
  173.5 4.7 %convolution_convert_fusion.1 = bf16[128,320]{1,0:T(8,128)(2,1)S(1)} fusion(bf16[128,8192]{0,1:T(8,128)(2,1)} %bitcast.133, bf16[8192,320]{1,0:T(8,128)(2,1)} %all-gather.2.cloned.1.call-done), kind=kOutput, calls=%fused_computation.28 | convolution fusion | flops 671129600 | bytes 7421952 | tf_op jit(solution)/shard_map/dot_general | solution.py:387
  179.5 12.5 %shard_map.77 = bf16[4,128,64]{2,1,0:T(8,128)(2,1)} custom-call(bf16[1,128,64]{2,1,0:T(8,128)(2,1)} %slice_bitcast_fusion.5.src_ref), custom_call_target="tpu_custom_call" | custom-call | bytes 131072 | tf_op jit(solution)/shard_map/pallas_call | solution.py:288
  192.0 1.4 slice_bitcast_fusion.7
  194.3 1.6 fusion.33
  196.8 1.3 fusion.20
  198.3 1.1 fusion.17
  201.1 1.2 convolution_bitcast_fusion.5
  204.1 13.2 %shard_map.78 = f32[4,128,64]{2,1,0:T(8,128)} custom-call(f32[4,128,64]{2,1,0:T(8,128)} %pad_maximum_fusion.1.src_ref), custom_call_target="tpu_custom_call" | custom-call | bytes 262144 | tf_op jit(solution)/shard_map/pallas_call | solution.py:288
  218.4 1.6 convolution_bitcast_fusion.1
  220.7 1.5 copy.95
  223.8 5.0 %fusion.29 = f32[16,512,128]{1,2,0:T(8,128)S(1)} fusion(bf16[16,512,320]{2,1,0:T(8,128)(2,1)} %bitcast.131, bf16[128,64]{0,1:T(8,128)(2,1)S(1)} %copy.85, bf16[128,256]{0,1:T(8,128)(2,1)S(1)} %slice.96), kind=kOutput, calls=%fused_computation.61 | convolution fusion | flops 671252480 | bytes 9519104 | tf_op jit(solution)/shard_map/rc,pkc->prk/dot_general | solution.py:444
  228.8 3.5 %fusion.3 = (f32[128]{0:T(128)}, bf16[16,128,512]{2,1,0:T(8,128)(2,1)}) fusion(bf16[16,128,512]{2,1,0:T(8,128)(2,1)S(1)} %get-tuple-element.7, f32[16,512]{1,0:T(8,128)S(1)} %copy-done.11, f32[128]{0:T(128)S(1)} %copy-done.16, f32[16,512,128]{1,2,0:T(8,128)S(1)} %fusion.29, bf16[16,512,256]{2,1,0:T(8,128)(2,1)S(1)} %bitcast.136, ...), kind=kOutput, calls=%fused_computation.5 | convolution fusion | flops 545259392 | bytes 12682240 | tf_op jit(solution)/shard_map/rc,pkc->prk/dot_general | solution.py:445
  232.3 48.8 %shard_map.79 = (bf16[16,128,512]{2,1,0:T(8,128)(2,1)}, f32[16,1,128]{2,1,0:T(1,128)}) custom-call(bf16[16,128,512]{2,1,0:T(8,128)(2,1)} %get-tuple-element.45.refs_0_, f32[1,128]{1,0:T(1,128)} %bitcast.146), custom_call_target="tpu_custom_call" | custom-call | bytes 4210688 | tf_op jit(solution)/shard_map/pallas_call | solution.py:68
  281.9 1.9 convert_reduce_fusion
  283.8 1.4 multiply_reduce_fusion
  285.2 17.6 %shard_map.80 = f32[32,1,512]{2,1,0:T(1,128)} custom-call(f32[1,512]{1,0:T(1,128)} %bitcast.145), custom_call_target="tpu_custom_call" | custom-call | bytes 131072 | tf_op jit(solution)/shard_map/pallas_call | solution.py:68
  302.8 1.5 reduce_sum.89
  304.3 6.5 %shard_map.81 = f32[128,128]{1,0:T(8,128)} custom-call(f32[2,128,128]{2,1,0:T(8,128)} %bitcast.143), custom_call_target="tpu_custom_call" | custom-call | bytes 393216 | tf_op jit(solution)/shard_map/pallas_call | solution.py:220
  (75 shorter events, 18.9 us)
Async XLA Ops:
  7.2 166.3 %all-gather.2.cloned.1.call-start = ((), (), s32[]{:S(2)}) async-start(), calls=%async_computation.1 | async-start | bytes 6488064 | tf_op jit(solution)/shard_map/all_gather | solution.py:376
  9.8 294.5 %reduce-scatter.2.cloned.1.call-start = ((), (), s32[]{:S(2)}) async-start(), calls=%async_computation.2 | async-start | bytes 2228224 | tf_op jit(solution)/shard_map/reduce_scatter | solution.py:483
  10.6 128.2 %copy-start.10 = (f32[16,512]{1,0:T(8,128)}, f32[16,512]{1,0:T(8,128)S(1)}, u32[]{:S(2)}) copy-start(f32[16,512]{1,0:T(8,128)S(1)} %mul.257) | copy-start | bytes 98308
  10.6 0.9 copy-start
  132.4 0.5 copy-start.15
  133.0 5.9 %copy-start.14 = (bf16[128,512]{1,0:T(8,128)(2,1)S(1)}, bf16[128,512]{1,0:T(8,128)(2,1)}, u32[]{:S(2)}) copy-start(bf16[128,512]{1,0:T(8,128)(2,1)} %param.6) | copy-start | bytes 393220
  139.0 4.7 %copy-start.2 = (bf16[128,16,512]{0,2,1:T(8,128)(2,1)S(1)}, bf16[128,16,512]{0,2,1:T(8,128)(2,1)}, u32[]{:S(2)}) copy-start(bf16[128,16,512]{0,2,1:T(8,128)(2,1)} %copy.66) | copy-start | bytes 6291460
  195.9 0.9 copy-start.6
  195.9 0.9 copy-start.8
  200.4 0.7 copy-start.4
  220.7 2.3 copy-start.5
  220.7 2.3 copy-start.12
  220.7 2.3 copy-start.13
  220.7 2.6 copy-start.7
  220.7 2.6 copy-start.9
  223.7 5.1 %copy-start.3 = (bf16[32,256,256]{2,1,0:T(8,128)(2,1)S(1)}, bf16[32,256,256]{2,1,0:T(8,128)(2,1)}, u32[]{:S(2)}) copy-start(bf16[32,256,256]{2,1,0:T(8,128)(2,1)} %get-tuple-element.8) | copy-start | bytes 12582916
  223.7 5.1 %copy-start.11 = (f32[16,512]{1,0:T(8,128)S(1)}, f32[16,512]{1,0:T(8,128)}, u32[]{:S(2)}) copy-start(f32[16,512]{1,0:T(8,128)} %copy-done.10) | copy-start | bytes 98308
  223.7 5.1 %copy-start.16 = (f32[128]{0:T(128)S(1)}, f32[128]{0:T(128)}, u32[]{:S(2)}) copy-start(f32[128]{0:T(128)} %copy-done.15) | copy-start | bytes 1540
  232.3 51.5 %copy-start.1 = (bf16[128,512]{1,0:T(8,128)(2,1)S(1)}, bf16[128,512]{1,0:T(8,128)(2,1)}, u32[]{:S(2)}) copy-start(bf16[128,512]{1,0:T(8,128)(2,1)} %side_ref.1) | copy-start | bytes 393220
Sparse Core Ops, SparseCore 0:
  10.1 163.3 all-gather.1
  222.4 74.4 reduce-scatter.1

commit v14 on v12

--- a/solution.py
+++ b/solution.py
@@ -470,7 +470,7 @@
             for half in range(2)
         ],
         axis=-1,
-    ).reshape(model_width // 2, 2 * group_cols)
+    ).reshape(model_width // 2, 2 * group_cols).astype(jnp.bfloat16)
     ring_groups = [
         [pair * ring_count + slot for slot in range(ring_count)] for pair in range(pair_count)
     ]
@@ -490,7 +490,9 @@
     (gain_parts,) = exchange("dp", [gain_part], [False], 4)
     grad_gain = jnp.sum(gain_parts, axis=(0, 1))
     lane_rows = ring_sums.size // (pair_count * 128)
-    keyval_sums = pair_sum(ring_sums.reshape(pair_count, lane_rows, 128), ring_count, 7)
+    keyval_sums = pair_sum(
+        ring_sums.astype(jnp.float32).reshape(pair_count, lane_rows, 128), ring_count, 7
+    )
     keyval_weight_grad = keyval_sums.reshape(-1, group_cols)
     return (grad_input, grad_gain, keyval_weight_grad.astype(jnp.bfloat16))
 

time: 318 us -> 317 us (level)
  transfers between devices with their start and end apart: 2 -> 2, of which waited for: 1 -> 1; matrix products, arithmetic and copies ran while one was open for 10% -> 10% of each run, Pallas kernels for 60% -> 59%
where the time goes in v14:
time: 317 us; the launch traced here: 315 us
  Pallas kernels  223 us (70%)
  waiting for transfers between devices  22.3 us (7%)
  matrix products  21.7 us (7%)
  local copies, waits for them, and re-layouts  19.6 us (6%)
  between operations  14.4 us (5%)
  other arithmetic  13.9 us (4%)
    pallas_call x1, Pallas kernels, ring_gather(): pl.pallas_call(functools.partial(ring_gather_kernel, pair_count, ring_cou...  121 us
    pallas_call x2, Pallas kernels, exchange_multi(): pl.pallas_call(functools.partial(exchange_kernel, axes, sizes, per_peer),...  65.7 us
    pallas_call x2, Pallas kernels, group_exchange(): pl.pallas_call(functools.partial(group_kernel, routes), out_shape=jax.Sha...  29.3 us
    all_gather x1, waiting for transfers between devices, on_device(): engine_full = lax.all_gather(engine_block, 'dp', axis=0, tiled=True)  22.3 us
    pallas_call x1, Pallas kernels, pair_sum(): pl.pallas_call(functools.partial(pair_sum_kernel, ring_count), out_shape=...  6.5 us
  transfers between devices with their start and end apart: 2, of which 1 were waited for; matrix products, arithmetic and copies ran while one was open for 10% of the time, Pallas kernels for 59%

profile of v14, /device:TPU:6, one launch (start us, length us, event | category | flops | bytes accessed | tf_op | source)
XLA Modules:
  0.0 314.7 jit_solution(2034334572942449454)
XLA Ops:
  7.2 1.0 fusion.54
  11.6 121.3 %shard_map.76 = (bf16[32,256,256]{2,1,0:T(8,128)(2,1)}, bf16[16,128,512]{2,1,0:T(8,128)(2,1)S(1)}) custom-call(bf16[256,256]{1,0:T(8,128)(2,1)S(1)} %get-tuple-element.26.block_ref, bf16[128,512]{1,0:T(8,128)(2,1)S(1)} %copy-done), custom_call_target="tpu_custom_call" | custom-call | bytes 12582912 | tf_op jit(solution)/shard_map/pallas_call | solution.py:178
  133.9 1.9 fusion.5
  135.8 3.9 %copy.61 = bf16[128,16,512]{0,2,1:T(8,128)(2,1)} copy(bf16[128,16,512]{2,0,1:T(8,128)(2,1)} %fusion.5) | data formatting | bytes 4194304 | tf_op jit(solution)/shard_map/transpose | solution.py:385
  139.9 6.2 %copy.86 = bf16[128,2,16,128,2]{3,0,1,2,4:T(8,128)(2,1)} copy(bf16[128,2,16,128,2]{0,4,3,2,1:T(2,128)(2,1)} %bitcast.124) | data formatting | bytes 4194304 | tf_op jit(solution)/shard_map/reshape;reshape | solution.py:459
  146.0 1.3 dynamic_slice.3
  147.4 3.8 %fusion.18 = bf16[16,2,8,128]{3,2,1,0:T(8,128)(2,1)S(1)} fusion(bf16[128,8192]{0,1:T(8,128)(2,1)} %bitcast.125, bf16[8192,256]{1,0:T(8,128)(2,1)} %bitcast.127), kind=kOutput, calls=%fused_computation.32 | convolution fusion | flops 536903680 | bytes 6356992 | tf_op jit(solution)/shard_map/dot_general | solution.py:390
  151.2 22.3 %all-gather.2.cloned.1.call-done = bf16[8192,320]{1,0:T(8,128)(2,1)} async-done(((bf16[256,320]{1,0:T(8,128)(2,1)}), bf16[8192,320]{1,0:T(8,128)(2,1)}) %all-gather.2.cloned.1.call-update) | async-done | bytes 5242896 | tf_op jit(solution)/shard_map/all_gather | solution.py:376
  173.5 4.7 %convolution_convert_fusion.3 = bf16[128,320]{1,0:T(8,128)(2,1)S(1)} fusion(bf16[128,8192]{0,1:T(8,128)(2,1)} %bitcast.126, bf16[8192,320]{1,0:T(8,128)(2,1)} %all-gather.2.cloned.1.call-done), kind=kOutput, calls=%fused_computation.27 | convolution fusion | flops 671129600 | bytes 7421952 | tf_op jit(solution)/shard_map/dot_general | solution.py:387
  178.8 16.1 %shard_map.77 = bf16[4,128,64]{2,1,0:T(8,128)(2,1)} custom-call(bf16[1,128,64]{2,1,0:T(8,128)(2,1)} %slice_bitcast_fusion.9.src_ref), custom_call_target="tpu_custom_call" | custom-call | bytes 131072 | tf_op jit(solution)/shard_map/pallas_call | solution.py:288
  198.8 13.2 %shard_map.78 = f32[4,128,64]{2,1,0:T(8,128)} custom-call(f32[4,128,64]{2,1,0:T(8,128)} %pad_maximum_fusion.1.src_ref), custom_call_target="tpu_custom_call" | custom-call | bytes 262144 | tf_op jit(solution)/shard_map/pallas_call | solution.py:288
  212.0 1.0 reduce_sum.84
  213.1 1.5 convolution_convert_fusion.1
  214.6 1.5 convolution_convert_fusion
  216.5 1.3 copy.87
  218.3 5.0 %fusion.29 = f32[16,512,128]{1,2,0:T(8,128)S(1)} fusion(bf16[16,512,320]{2,1,0:T(8,128)(2,1)} %bitcast.123, bf16[128,64]{0,1:T(8,128)(2,1)S(1)} %copy.80, bf16[128,256]{0,1:T(8,128)(2,1)S(1)} %slice.96), kind=kOutput, calls=%fused_computation.61 | convolution fusion | flops 671252480 | bytes 9519104 | tf_op jit(solution)/shard_map/rc,pkc->prk/dot_general | solution.py:444
  223.4 3.5 %fusion.3 = (f32[128]{0:T(128)}, bf16[16,128,512]{2,1,0:T(8,128)(2,1)}) fusion(bf16[16,128,512]{2,1,0:T(8,128)(2,1)S(1)} %get-tuple-element.7, f32[16,512]{1,0:T(8,128)S(1)} %copy-done.4, f32[128]{0:T(128)S(1)} %copy-done.8, f32[16,512,128]{1,2,0:T(8,128)S(1)} %fusion.29, bf16[16,512,256]{2,1,0:T(8,128)(2,1)S(1)} %bitcast.128, bf16[128,512]{0,1:T(8,128)(2,1)S(1)} %bitcast.136), kind=kOutput, calls=%fused_computation.5 | convolution fusion | flops 545259392 | bytes 12682240 | tf_op jit(solution)/shard_map/rc,pkc->prk/dot_general | solution.py:445
  226.9 48.8 %shard_map.79 = (bf16[16,128,512]{2,1,0:T(8,128)(2,1)}, f32[16,1,128]{2,1,0:T(1,128)}) custom-call(bf16[16,128,512]{2,1,0:T(8,128)(2,1)} %get-tuple-element.41.refs_0_, f32[1,128]{1,0:T(1,128)} %bitcast.140), custom_call_target="tpu_custom_call" | custom-call | bytes 4210688 | tf_op jit(solution)/shard_map/pallas_call | solution.py:68
  276.4 1.9 convert_reduce_fusion
  278.4 1.4 multiply_reduce_fusion
  279.8 16.9 %shard_map.80 = f32[32,1,512]{2,1,0:T(1,128)} custom-call(f32[1,512]{1,0:T(1,128)} %bitcast.139), custom_call_target="tpu_custom_call" | custom-call | bytes 131072 | tf_op jit(solution)/shard_map/pallas_call | solution.py:68
  296.7 1.5 reduce_sum.89
  298.2 1.5 convert.34.block_ref
  299.7 6.5 %shard_map.81 = f32[128,128]{1,0:T(8,128)} custom-call(f32[2,128,128]{2,1,0:T(8,128)} %convert.34.block_ref), custom_call_target="tpu_custom_call" | custom-call | bytes 393216 | tf_op jit(solution)/shard_map/pallas_call | solution.py:220
  (59 shorter events, 12.3 us)
Async XLA Ops:
  7.2 166.3 %all-gather.2.cloned.1.call-start = ((), (), s32[]{:S(2)}) async-start(), calls=%async_computation.1 | async-start | bytes 6488064 | tf_op jit(solution)/shard_map/all_gather | solution.py:376
  9.8 288.4 %reduce-scatter.2.cloned.1.call-start = ((), (), s32[]{:S(2)}) async-start(), calls=%async_computation.2 | async-start | bytes 1114112 | tf_op jit(solution)/shard_map/reduce_scatter | solution.py:477
  10.6 129.1 %copy-start.3 = (f32[16,512]{1,0:T(8,128)}, f32[16,512]{1,0:T(8,128)S(1)}, u32[]{:S(2)}) copy-start(f32[16,512]{1,0:T(8,128)S(1)} %mul.257) | copy-start | bytes 98308
  10.6 0.9 copy-start
  133.3 0.6 copy-start.7
  133.9 5.8 %copy-start.5 = (bf16[128,512]{1,0:T(8,128)(2,1)S(1)}, bf16[128,512]{1,0:T(8,128)(2,1)}, u32[]{:S(2)}) copy-start(bf16[128,512]{1,0:T(8,128)(2,1)} %param.6) | copy-start | bytes 393220
  218.3 5.0 %copy-start.2 = (bf16[32,256,256]{2,1,0:T(8,128)(2,1)S(1)}, bf16[32,256,256]{2,1,0:T(8,128)(2,1)}, u32[]{:S(2)}) copy-start(bf16[32,256,256]{2,1,0:T(8,128)(2,1)} %get-tuple-element.8) | copy-start | bytes 12582916
  218.3 5.0 %copy-start.4 = (f32[16,512]{1,0:T(8,128)S(1)}, f32[16,512]{1,0:T(8,128)}, u32[]{:S(2)}) copy-start(f32[16,512]{1,0:T(8,128)} %copy-done.3) | copy-start | bytes 98308
  218.3 5.0 %copy-start.8 = (f32[128]{0:T(128)S(1)}, f32[128]{0:T(128)}, u32[]{:S(2)}) copy-start(f32[128]{0:T(128)} %copy-done.7) | copy-start | bytes 1540
  226.9 51.5 %copy-start.1 = (bf16[128,512]{1,0:T(8,128)(2,1)S(1)}, bf16[128,512]{1,0:T(8,128)(2,1)}, u32[]{:S(2)}) copy-start(bf16[128,512]{1,0:T(8,128)(2,1)} %side_ref.1) | copy-start | bytes 393220
  226.9 51.5 %copy-start.6 = (f32[512]{0:T(512)S(1)}, f32[512]{0:T(512)}, u32[]{:S(2)}) copy-start(f32[512]{0:T(512)} %dynamic_slice.3) | copy-start | bytes 6148
Sparse Core Ops, SparseCore 0:
  10.1 163.3 all-gather.1
  218.0 69.1 reduce-scatter.1

commit v15 on v12

--- a/solution.py
+++ b/solution.py
@@ -315,6 +315,73 @@
     head_group = lax.rem(me // 2, KV_HEADS)
     sources = [KV_HEADS * head_group + m for m in range(KV_HEADS)]
     return dests, sources
+
+
+def gain_kernel(ring_count, part_ref, out_ref, send_sems, recv_sems):
+    pair_slot = lax.axis_index("dp") // ring_count
+    ring_slot = lax.axis_index("dp") % ring_count
+    me = pair_slot * ring_count + ring_slot
+    partner = (1 - pair_slot) * ring_count + ring_slot
+    peers = [pair_slot * ring_count + lax.rem(ring_slot + step, ring_count) for step in range(1, ring_count)]
+    barrier = pltpu.get_barrier_semaphore()
+    for peer in [partner] + peers:
+        pl.semaphore_signal(barrier, inc=1, device_id={"dp": peer}, device_id_type=MESH)
+    pl.semaphore_wait(barrier, ring_count)
+    swap = pltpu.make_async_remote_copy(
+        src_ref=part_ref,
+        dst_ref=out_ref.at[me],
+        send_sem=send_sems.at[0, 0],
+        recv_sem=recv_sems.at[0, 0],
+        device_id={"dp": partner},
+        device_id_type=MESH,
+    )
+    swap.start()
+    copies = []
+    for index, peer in enumerate(peers):
+        copy = pltpu.make_async_remote_copy(
+            src_ref=part_ref,
+            dst_ref=out_ref.at[me],
+            send_sem=send_sems.at[1, index],
+            recv_sem=recv_sems.at[1, index],
+            device_id={"dp": peer},
+            device_id_type=MESH,
+        )
+        copy.start()
+        copies.append(copy)
+    out_ref[me] = part_ref[...]
+    swap.wait_send()
+    swap.wait_recv()
+    for index, peer in enumerate(peers):
+        copy = pltpu.make_async_remote_copy(
+            src_ref=out_ref.at[partner],
+            dst_ref=out_ref.at[partner],
+            send_sem=send_sems.at[2, index],
+            recv_sem=recv_sems.at[2, index],
+            device_id={"dp": peer},
+            device_id_type=MESH,
+        )
+        copy.start()
+        copies.append(copy)
+    for copy in copies:
+        copy.wait_send()
+    for copy in copies:
+        copy.wait_recv()
+
+
+def gain_allgather(part, collective_id):
+    count = lax.axis_size("dp")
+    ring_count = count // 2
+    return pl.pallas_call(
+        functools.partial(gain_kernel, ring_count),
+        out_shape=jax.ShapeDtypeStruct((count,) + part.shape, part.dtype),
+        in_specs=[pl.BlockSpec(memory_space=pltpu.VMEM)],
+        out_specs=pl.BlockSpec(memory_space=pltpu.VMEM),
+        scratch_shapes=[pltpu.SemaphoreType.DMA((3, ring_count)), pltpu.SemaphoreType.DMA((3, ring_count))],
+        compiler_params=pltpu.CompilerParams(collective_id=collective_id, has_side_effects=True),
+        cost_estimate=pl.CostEstimate(
+            flops=0, bytes_accessed=4 * count * part.size * part.dtype.itemsize, transcendentals=0
+        ),
+    )(part)
 
 
 HD = 128
@@ -487,7 +554,7 @@
         jnp.bfloat16
     )
     gain_part = jnp.sum(grad_normed * unit_rows, axis=0).reshape(1, local_cols)
-    (gain_parts,) = exchange("dp", [gain_part], [False], 4)
+    gain_parts = gain_allgather(gain_part, 4)
     grad_gain = jnp.sum(gain_parts, axis=(0, 1))
     lane_rows = ring_sums.size // (pair_count * 128)
     keyval_sums = pair_sum(ring_sums.reshape(pair_count, lane_rows, 128), ring_count, 7)

time: 318 us -> 319 us (level)
    pallas_call x2 -> x1, Pallas kernels: 66.3 us -> 48.8 us  [exchange_multi(): pl.pallas_call(functools.partial(exchange_kernel, axes, sizes, per_peer),...]
    pallas_call x0 -> x1, Pallas kernels: none -> 17.5 us  [gain_allgather(): pl.pallas_call(functools.partial(gain_kernel, ring_count), out_shape=jax....]
where the time goes in v15:
time: 319 us; the launch traced here: 316 us
  Pallas kernels  224 us (70%)
  waiting for transfers between devices  22.1 us (7%)
  matrix products  21.7 us (7%)
  local copies, waits for them, and re-layouts  19.9 us (6%)
  between operations  14.3 us (4%)
  other arithmetic  13.8 us (4%)
    pallas_call x1, Pallas kernels, ring_gather(): pl.pallas_call(functools.partial(ring_gather_kernel, pair_count, ring_cou...  123 us
    pallas_call x1, Pallas kernels, exchange_multi(): pl.pallas_call(functools.partial(exchange_kernel, axes, sizes, per_peer),...  48.8 us
    pallas_call x2, Pallas kernels, group_exchange(): pl.pallas_call(functools.partial(group_kernel, routes), out_shape=jax.Sha...  27.4 us
    all_gather x1, waiting for transfers between devices, on_device(): engine_full = lax.all_gather(engine_block, 'dp', axis=0, tiled=True)  22.1 us
    pallas_call x1, Pallas kernels, gain_allgather(): pl.pallas_call(functools.partial(gain_kernel, ring_count), out_shape=jax....  17.5 us
    pallas_call x1, Pallas kernels, pair_sum(): pl.pallas_call(functools.partial(pair_sum_kernel, ring_count), out_shape=...  6.65 us
  transfers between devices with their start and end apart: 2, of which 1 were waited for; matrix products, arithmetic and copies ran while one was open for 10% of the time, Pallas kernels for 60%

profile of v15, /device:TPU:6, one launch (start us, length us, event | category | flops | bytes accessed | tf_op | source)
XLA Modules:
  0.0 315.7 jit_solution(11398463558516133879)
XLA Ops:
  7.2 1.0 fusion.56
  10.6 0.9 copy-done
  11.5 123.5 %shard_map.76 = (bf16[32,256,256]{2,1,0:T(8,128)(2,1)}, bf16[16,128,512]{2,1,0:T(8,128)(2,1)S(1)}) custom-call(bf16[256,256]{1,0:T(8,128)(2,1)S(1)} %get-tuple-element.26.block_ref, bf16[128,512]{1,0:T(8,128)(2,1)S(1)} %copy-done), custom_call_target="tpu_custom_call" | custom-call | bytes 12582912 | tf_op jit(solution)/shard_map/pallas_call | solution.py:178
  135.5 1.9 fusion.5
  137.4 3.9 %copy.61 = bf16[128,16,512]{0,2,1:T(8,128)(2,1)} copy(bf16[128,16,512]{2,0,1:T(8,128)(2,1)} %fusion.5) | data formatting | bytes 4194304 | tf_op jit(solution)/shard_map/transpose | solution.py:452
  141.5 6.2 %copy.86 = bf16[128,2,16,128,2]{3,0,1,2,4:T(8,128)(2,1)} copy(bf16[128,2,16,128,2]{0,4,3,2,1:T(2,128)(2,1)} %bitcast.123) | data formatting | bytes 4194304 | tf_op jit(solution)/shard_map/reshape;reshape | solution.py:526
  147.7 3.8 %fusion.18 = bf16[16,2,8,128]{3,2,1,0:T(8,128)(2,1)S(1)} fusion(bf16[128,8192]{0,1:T(8,128)(2,1)} %bitcast.124, bf16[8192,256]{1,0:T(8,128)(2,1)} %bitcast.126), kind=kOutput, calls=%fused_computation.31 | convolution fusion | flops 536903680 | bytes 6356992 | tf_op jit(solution)/shard_map/dot_general | solution.py:457
  151.5 22.1 %all-gather.2.cloned.1.call-done = bf16[8192,320]{1,0:T(8,128)(2,1)} async-done(((bf16[256,320]{1,0:T(8,128)(2,1)}), bf16[8192,320]{1,0:T(8,128)(2,1)}) %all-gather.2.cloned.1.call-update) | async-done | bytes 5242896 | tf_op jit(solution)/shard_map/all_gather | solution.py:443
  173.6 4.7 %convolution_convert_fusion.1 = bf16[128,320]{1,0:T(8,128)(2,1)S(1)} fusion(bf16[128,8192]{0,1:T(8,128)(2,1)} %bitcast.125, bf16[8192,320]{1,0:T(8,128)(2,1)} %all-gather.2.cloned.1.call-done), kind=kOutput, calls=%fused_computation.26 | convolution fusion | flops 671129600 | bytes 7421952 | tf_op jit(solution)/shard_map/dot_general | solution.py:454
  178.9 14.2 %shard_map.77 = bf16[4,128,64]{2,1,0:T(8,128)(2,1)} custom-call(bf16[1,128,64]{2,1,0:T(8,128)(2,1)} %slice_bitcast_fusion.9.src_ref), custom_call_target="tpu_custom_call" | custom-call | bytes 131072 | tf_op jit(solution)/shard_map/pallas_call | solution.py:288
  197.0 13.2 %shard_map.78 = f32[4,128,64]{2,1,0:T(8,128)} custom-call(f32[4,128,64]{2,1,0:T(8,128)} %pad_maximum_fusion.1.src_ref), custom_call_target="tpu_custom_call" | custom-call | bytes 262144 | tf_op jit(solution)/shard_map/pallas_call | solution.py:288
  210.2 1.0 reduce_sum.84
  211.3 1.5 fusion.20
  212.8 1.5 fusion.19
  214.3 1.5 pad_maximum_fusion
  215.8 2.9 copy.87
  220.2 5.0 %fusion.31 = f32[16,512,128]{1,2,0:T(8,128)S(1)} fusion(bf16[16,512,320]{2,1,0:T(8,128)(2,1)} %bitcast.122, bf16[128,64]{0,1:T(8,128)(2,1)S(1)} %copy.80, bf16[128,256]{0,1:T(8,128)(2,1)S(1)} %slice.96), kind=kOutput, calls=%fused_computation.61 | convolution fusion | flops 671252480 | bytes 9519104 | tf_op jit(solution)/shard_map/rc,pkc->prk/dot_general | solution.py:511
  225.2 3.5 %fusion.3 = (f32[128]{0:T(128)}, bf16[16,128,512]{2,1,0:T(8,128)(2,1)}) fusion(bf16[16,128,512]{2,1,0:T(8,128)(2,1)S(1)} %get-tuple-element.7, f32[16,512]{1,0:T(8,128)S(1)} %mul.257, f32[128]{0:T(128)S(1)} %add_rsqrt_fusion, f32[16,512,128]{1,2,0:T(8,128)S(1)} %fusion.31, bf16[16,512,256]{2,1,0:T(8,128)(2,1)S(1)} %bitcast.127, ...), kind=kOutput, calls=%fused_computation.5 | convolution fusion | flops 545259392 | bytes 12682240 | tf_op jit(solution)/shard_map/rc,pkc->prk/dot_general | solution.py:512
  228.8 48.8 %shard_map.79 = (bf16[16,128,512]{2,1,0:T(8,128)(2,1)}, f32[16,1,128]{2,1,0:T(1,128)}) custom-call(bf16[16,128,512]{2,1,0:T(8,128)(2,1)} %get-tuple-element.41.refs_0_, f32[1,128]{1,0:T(1,128)} %bitcast.139), custom_call_target="tpu_custom_call" | custom-call | bytes 4210688 | tf_op jit(solution)/shard_map/pallas_call | solution.py:68
  278.3 1.9 convert_reduce_fusion
  280.2 1.4 multiply_reduce_fusion
  281.6 17.5 %shard_map.80 = f32[32,1,512]{2,1,0:T(1,128)} custom-call(f32[1,512]{1,0:T(1,128)} %bitcast.138), custom_call_target="tpu_custom_call" | custom-call | bytes 262144 | tf_op jit(solution)/shard_map/pallas_call | solution.py:374
  299.1 1.5 reduce_sum.89
  300.6 6.7 %shard_map.81 = f32[128,128]{1,0:T(8,128)} custom-call(f32[2,128,128]{2,1,0:T(8,128)} %bitcast.136), custom_call_target="tpu_custom_call" | custom-call | bytes 393216 | tf_op jit(solution)/shard_map/pallas_call | solution.py:220
  (48 shorter events, 11.5 us)
Async XLA Ops:
  7.2 166.4 %all-gather.2.cloned.1.call-start = ((), (), s32[]{:S(2)}) async-start(), calls=%async_computation.1 | async-start | bytes 6488064 | tf_op jit(solution)/shard_map/all_gather | solution.py:443
  9.8 290.7 %reduce-scatter.2.cloned.1.call-start = ((), (), s32[]{:S(2)}) async-start(), calls=%async_computation.2 | async-start | bytes 2228224 | tf_op jit(solution)/shard_map/reduce_scatter | solution.py:544
  10.6 0.9 copy-start
  135.5 5.8 %copy-start.3 = (bf16[128,512]{1,0:T(8,128)(2,1)S(1)}, bf16[128,512]{1,0:T(8,128)(2,1)}, u32[]{:S(2)}) copy-start(bf16[128,512]{1,0:T(8,128)(2,1)} %param.6) | copy-start | bytes 393220
  220.2 5.0 %copy-start.2 = (bf16[32,256,256]{2,1,0:T(8,128)(2,1)S(1)}, bf16[32,256,256]{2,1,0:T(8,128)(2,1)}, u32[]{:S(2)}) copy-start(bf16[32,256,256]{2,1,0:T(8,128)(2,1)} %get-tuple-element.8) | copy-start | bytes 12582916
  228.8 51.4 %copy-start.1 = (bf16[128,512]{1,0:T(8,128)(2,1)S(1)}, bf16[128,512]{1,0:T(8,128)(2,1)}, u32[]{:S(2)}) copy-start(bf16[128,512]{1,0:T(8,128)(2,1)} %side_ref.1) | copy-start | bytes 393220
Sparse Core Ops, SparseCore 0:
  10.1 163.4 all-gather.1
  218.9 73.5 reduce-scatter.1

commit v16 on v12

--- a/solution.py
+++ b/solution.py
@@ -100,19 +100,6 @@
         peer = lax.rem(side_me + step, side_count)
         pl.semaphore_signal(barrier, inc=1, device_id={"tensor": peer}, device_id_type=MESH)
     pl.semaphore_wait(barrier, 3 + side_count - 1)
-    side_copies = []
-    for step in range(1, side_count):
-        peer = lax.rem(side_me + step, side_count)
-        copy = pltpu.make_async_remote_copy(
-            src_ref=side_ref,
-            dst_ref=side_out.at[side_me],
-            send_sem=side_send.at[step],
-            recv_sem=side_recv.at[step],
-            device_id={"tensor": peer},
-            device_id_type=MESH,
-        )
-        copy.start()
-        side_copies.append(copy)
     swap = pltpu.make_async_remote_copy(
         src_ref=block_ref,
         dst_ref=out_ref.at[me],
@@ -151,6 +138,19 @@
 
     right_copies = send(0, 0, right, ring_slot)
     left_copies = send(1, 0, left, ring_slot) if left_steps > 0 else []
+    side_copies = []
+    for step in range(1, side_count):
+        peer = lax.rem(side_me + step, side_count)
+        copy = pltpu.make_async_remote_copy(
+            src_ref=side_ref,
+            dst_ref=side_out.at[side_me],
+            send_sem=side_send.at[step],
+            recv_sem=side_recv.at[step],
+            device_id={"tensor": peer},
+            device_id_type=MESH,
+        )
+        copy.start()
+        side_copies.append(copy)
     for step in range(1, right_steps):
         for copy in right_copies:
             copy.wait_recv()

time: 318 us -> 310 us (0.975)
  Pallas kernels: 224 us -> 200 us
  waiting for transfers between devices: 22.1 us -> 38.4 us
    pallas_call x1, Pallas kernels: 123 us -> 107 us  [ring_gather(): pl.pallas_call(functools.partial(ring_gather_kernel, pair_count, ring_cou...]
    all_gather x1, waiting for transfers between devices: 22.1 us -> 38.4 us  [on_device(): engine_full = lax.all_gather(engine_block, 'dp', axis=0, tiled=True)]
    pallas_call x2, Pallas kernels: 27.4 us -> 21.8 us  [group_exchange(): pl.pallas_call(functools.partial(group_kernel, routes), out_shape=jax.Sha...]
  transfers between devices with their start and end apart: 2 -> 2, of which waited for: 1 -> 1; matrix products, arithmetic and copies ran while one was open for 10% -> 11% of each run, Pallas kernels for 60% -> 56%
where the time goes in v16:
time: 310 us; the launch traced here: 308 us
  Pallas kernels  200 us (65%)
  waiting for transfers between devices  38.4 us (12%)
  matrix products  21.7 us (7%)
  local copies, waits for them, and re-layouts  19.9 us (6%)
  between operations  14.3 us (5%)
  other arithmetic  13.9 us (4%)
    pallas_call x1, Pallas kernels, ring_gather(): pl.pallas_call(functools.partial(ring_gather_kernel, pair_count, ring_cou...  107 us
    pallas_call x2, Pallas kernels, exchange_multi(): pl.pallas_call(functools.partial(exchange_kernel, axes, sizes, per_peer),...  64.3 us
    all_gather x1, waiting for transfers between devices, on_device(): engine_full = lax.all_gather(engine_block, 'dp', axis=0, tiled=True)  38.4 us
    pallas_call x2, Pallas kernels, group_exchange(): pl.pallas_call(functools.partial(group_kernel, routes), out_shape=jax.Sha...  21.8 us
    pallas_call x1, Pallas kernels, pair_sum(): pl.pallas_call(functools.partial(pair_sum_kernel, ring_count), out_shape=...  6.5 us
  transfers between devices with their start and end apart: 2, of which 1 were waited for; matrix products, arithmetic and copies ran while one was open for 11% of the time, Pallas kernels for 56%

profile of v16, /device:TPU:6, one launch (start us, length us, event | category | flops | bytes accessed | tf_op | source)
XLA Modules:
  0.0 307.8 jit_solution(2984824066308716147)
XLA Ops:
  7.2 1.0 fusion.56
  10.6 0.9 copy-done
  11.5 106.9 %shard_map.76 = (bf16[32,256,256]{2,1,0:T(8,128)(2,1)}, bf16[16,128,512]{2,1,0:T(8,128)(2,1)S(1)}) custom-call(bf16[256,256]{1,0:T(8,128)(2,1)S(1)} %get-tuple-element.26.block_ref, bf16[128,512]{1,0:T(8,128)(2,1)S(1)} %copy-done), custom_call_target="tpu_custom_call" | custom-call | bytes 12582912 | tf_op jit(solution)/shard_map/pallas_call | solution.py:178
  119.0 1.9 fusion.5
  120.9 3.9 %copy.61 = bf16[128,16,512]{0,2,1:T(8,128)(2,1)} copy(bf16[128,16,512]{2,0,1:T(8,128)(2,1)} %fusion.5) | data formatting | bytes 4194304 | tf_op jit(solution)/shard_map/transpose | solution.py:385
  124.9 6.2 %copy.86 = bf16[128,2,16,128,2]{3,0,1,2,4:T(8,128)(2,1)} copy(bf16[128,2,16,128,2]{0,4,3,2,1:T(2,128)(2,1)} %bitcast.123) | data formatting | bytes 4194304 | tf_op jit(solution)/shard_map/reshape;reshape | solution.py:459
  131.1 3.8 %fusion.18 = bf16[16,2,8,128]{3,2,1,0:T(8,128)(2,1)S(1)} fusion(bf16[128,8192]{0,1:T(8,128)(2,1)} %bitcast.124, bf16[8192,256]{1,0:T(8,128)(2,1)} %bitcast.126), kind=kOutput, calls=%fused_computation.31 | convolution fusion | flops 536903680 | bytes 6356992 | tf_op jit(solution)/shard_map/dot_general | solution.py:390
  134.9 38.4 %all-gather.2.cloned.1.call-done = bf16[8192,320]{1,0:T(8,128)(2,1)} async-done(((bf16[256,320]{1,0:T(8,128)(2,1)}), bf16[8192,320]{1,0:T(8,128)(2,1)}) %all-gather.2.cloned.1.call-update) | async-done | bytes 5242896 | tf_op jit(solution)/shard_map/all_gather | solution.py:376
  173.3 4.7 %convolution_convert_fusion.1 = bf16[128,320]{1,0:T(8,128)(2,1)S(1)} fusion(bf16[128,8192]{0,1:T(8,128)(2,1)} %bitcast.125, bf16[8192,320]{1,0:T(8,128)(2,1)} %all-gather.2.cloned.1.call-done), kind=kOutput, calls=%fused_computation.26 | convolution fusion | flops 671129600 | bytes 7421952 | tf_op jit(solution)/shard_map/dot_general | solution.py:387
  178.7 10.2 %shard_map.77 = bf16[4,128,64]{2,1,0:T(8,128)(2,1)} custom-call(bf16[1,128,64]{2,1,0:T(8,128)(2,1)} %slice_bitcast_fusion.9.src_ref), custom_call_target="tpu_custom_call" | custom-call | bytes 131072 | tf_op jit(solution)/shard_map/pallas_call | solution.py:288
  192.7 11.6 %shard_map.78 = f32[4,128,64]{2,1,0:T(8,128)} custom-call(f32[4,128,64]{2,1,0:T(8,128)} %pad_maximum_fusion.1.src_ref), custom_call_target="tpu_custom_call" | custom-call | bytes 262144 | tf_op jit(solution)/shard_map/pallas_call | solution.py:288
  204.4 1.0 reduce_sum.84
  205.4 1.5 fusion.20
  207.0 1.5 fusion.19
  208.5 1.5 pad_maximum_fusion
  210.0 2.9 copy.87
  214.4 5.0 %fusion.31 = f32[16,512,128]{1,2,0:T(8,128)S(1)} fusion(bf16[16,512,320]{2,1,0:T(8,128)(2,1)} %bitcast.122, bf16[128,64]{0,1:T(8,128)(2,1)S(1)} %copy.80, bf16[128,256]{0,1:T(8,128)(2,1)S(1)} %slice.96), kind=kOutput, calls=%fused_computation.61 | convolution fusion | flops 671252480 | bytes 9519104 | tf_op jit(solution)/shard_map/rc,pkc->prk/dot_general | solution.py:444
  219.4 3.5 %fusion.3 = (f32[128]{0:T(128)}, bf16[16,128,512]{2,1,0:T(8,128)(2,1)}) fusion(bf16[16,128,512]{2,1,0:T(8,128)(2,1)S(1)} %get-tuple-element.7, f32[16,512]{1,0:T(8,128)S(1)} %mul.257, f32[128]{0:T(128)S(1)} %add_rsqrt_fusion, f32[16,512,128]{1,2,0:T(8,128)S(1)} %fusion.31, bf16[16,512,256]{2,1,0:T(8,128)(2,1)S(1)} %bitcast.127, ...), kind=kOutput, calls=%fused_computation.5 | convolution fusion | flops 545259392 | bytes 12682240 | tf_op jit(solution)/shard_map/rc,pkc->prk/dot_general | solution.py:445
  222.9 47.0 %shard_map.79 = (bf16[16,128,512]{2,1,0:T(8,128)(2,1)}, f32[16,1,128]{2,1,0:T(1,128)}) custom-call(bf16[16,128,512]{2,1,0:T(8,128)(2,1)} %get-tuple-element.41.refs_0_, f32[1,128]{1,0:T(1,128)} %bitcast.139), custom_call_target="tpu_custom_call" | custom-call | bytes 4210688 | tf_op jit(solution)/shard_map/pallas_call | solution.py:68
  270.7 1.9 convert_reduce_fusion
  272.6 1.4 multiply_reduce_fusion
  274.0 17.3 %shard_map.80 = f32[32,1,512]{2,1,0:T(1,128)} custom-call(f32[1,512]{1,0:T(1,128)} %bitcast.138), custom_call_target="tpu_custom_call" | custom-call | bytes 131072 | tf_op jit(solution)/shard_map/pallas_call | solution.py:68
  291.3 1.5 reduce_sum.89
  292.8 6.5 %shard_map.81 = f32[128,128]{1,0:T(8,128)} custom-call(f32[2,128,128]{2,1,0:T(8,128)} %bitcast.136), custom_call_target="tpu_custom_call" | custom-call | bytes 393216 | tf_op jit(solution)/shard_map/pallas_call | solution.py:220
  (48 shorter events, 11.5 us)
Async XLA Ops:
  7.2 166.2 %all-gather.2.cloned.1.call-start = ((), (), s32[]{:S(2)}) async-start(), calls=%async_computation.1 | async-start | bytes 6488064 | tf_op jit(solution)/shard_map/all_gather | solution.py:376
  9.8 283.0 %reduce-scatter.2.cloned.1.call-start = ((), (), s32[]{:S(2)}) async-start(), calls=%async_computation.2 | async-start | bytes 2228224 | tf_op jit(solution)/shard_map/reduce_scatter | solution.py:477
  10.6 0.9 copy-start
  119.0 5.8 %copy-start.3 = (bf16[128,512]{1,0:T(8,128)(2,1)S(1)}, bf16[128,512]{1,0:T(8,128)(2,1)}, u32[]{:S(2)}) copy-start(bf16[128,512]{1,0:T(8,128)(2,1)} %param.6) | copy-start | bytes 393220
  214.4 5.0 %copy-start.2 = (bf16[32,256,256]{2,1,0:T(8,128)(2,1)S(1)}, bf16[32,256,256]{2,1,0:T(8,128)(2,1)}, u32[]{:S(2)}) copy-start(bf16[32,256,256]{2,1,0:T(8,128)(2,1)} %get-tuple-element.8) | copy-start | bytes 12582916
  222.9 49.7 %copy-start.1 = (bf16[128,512]{1,0:T(8,128)(2,1)S(1)}, bf16[128,512]{1,0:T(8,128)(2,1)}, u32[]{:S(2)}) copy-start(bf16[128,512]{1,0:T(8,128)(2,1)} %side_ref.1) | copy-start | bytes 393220
Sparse Core Ops, SparseCore 0:
  10.1 163.1 all-gather.1
  213.0 72.2 reduce-scatter.1

commit v17 on v16

--- a/solution.py
+++ b/solution.py
@@ -371,7 +371,7 @@
     score_scale = head_size ** (-0.5)
     tensor_slot = lax.axis_index("tensor")
     gain_local = lax.dynamic_slice_in_dim(gain, tensor_slot * local_cols, local_cols, 0)
-    split_cols = query_cols // 2
+    split_cols = query_cols * 3 // 8
     engine_block = jnp.concatenate([w_query[:, :split_cols], w_keyval], axis=1)
     engine_full = lax.all_gather(engine_block, "dp", axis=0, tiled=True)
     ring_blocks_out, input_blocks = ring_gather(w_query[:, split_cols:], inputs, 6)

time: 310 us -> 304 us (0.981)
  waiting for transfers between devices: 38.4 us -> 4.32 us
  Pallas kernels: 200 us -> 222 us
  matrix products: 21.7 us -> 25.3 us
    all_gather x1, waiting for transfers between devices: 38.4 us -> 4.29 us  [on_device(): engine_full = lax.all_gather(engine_block, 'dp', axis=0, tiled=True)]
    pallas_call x1, Pallas kernels: 107 us -> 131 us  [ring_gather(): pl.pallas_call(functools.partial(ring_gather_kernel, pair_count, ring_cou...]
    dot_general x1, matrix products: 3.54 us -> 7.38 us  [on_device(): jnp.einsum('rc,pkc->prk', grad_query[:, split_cols:], ring_blocks, prefer...]
  transfers between devices with their start and end apart: 2 -> 2, of which waited for: 1 -> 1; matrix products, arithmetic and copies ran while one was open for 11% -> 13% of each run, Pallas kernels for 56% -> 64%
where the time goes in v17:
time: 304 us; the launch traced here: 302 us
  Pallas kernels  222 us (73%)
  matrix products  25.3 us (8%)
  local copies, waits for them, and re-layouts  21.5 us (7%)
  between operations  14.3 us (5%)
  other arithmetic  13.8 us (5%)
  waiting for transfers between devices  4.32 us (1%)
    pallas_call x1, Pallas kernels, ring_gather(): pl.pallas_call(functools.partial(ring_gather_kernel, pair_count, ring_cou...  131 us
    pallas_call x2, Pallas kernels, exchange_multi(): pl.pallas_call(functools.partial(exchange_kernel, axes, sizes, per_peer),...  63.4 us
    pallas_call x2, Pallas kernels, group_exchange(): pl.pallas_call(functools.partial(group_kernel, routes), out_shape=jax.Sha...  21.8 us
    dot_general x1, matrix products, on_device(): jnp.einsum('rc,pkc->prk', grad_query[:, split_cols:], ring_blocks, prefer...  7.38 us
    pallas_call x1, Pallas kernels, pair_sum(): pl.pallas_call(functools.partial(pair_sum_kernel, ring_count), out_shape=...  6.5 us
    another operation x1, local copies, waits for them, and re-layouts, on_device(): normed_full.reshape(seq_length, pair_count, ring_count, block_rows // 2, 2)  6.16 us
  transfers between devices with their start and end apart: 2, of which 1 were waited for; matrix products, arithmetic and copies ran while one was open for 13% of the time, Pallas kernels for 64%

profile of v17, /device:TPU:6, one launch (start us, length us, event | category | flops | bytes accessed | tf_op | source)
XLA Modules:
  0.0 301.6 jit_solution(17617463867708208285)
XLA Ops:
  7.2 0.9 slice.67
  9.8 1.0 slice.66.block_ref
  12.6 130.6 %shard_map.76 = (bf16[32,256,320]{2,1,0:T(8,128)(2,1)}, bf16[16,128,512]{2,1,0:T(8,128)(2,1)S(1)}) custom-call(bf16[256,320]{1,0:T(8,128)(2,1)S(1)} %slice.66.block_ref, bf16[128,512]{1,0:T(8,128)(2,1)S(1)} %copy-done), custom_call_target="tpu_custom_call" | custom-call | bytes 14680064 | tf_op jit(solution)/shard_map/pallas_call | solution.py:178
  143.7 1.9 fusion.5
  145.6 3.9 %copy.93 = bf16[128,16,512]{0,2,1:T(8,128)(2,1)} copy(bf16[128,16,512]{2,0,1:T(8,128)(2,1)} %fusion.5) | data formatting | bytes 4194304 | tf_op jit(solution)/shard_map/transpose | solution.py:385
  149.6 6.2 %copy.119 = bf16[128,2,16,128,2]{3,0,1,2,4:T(8,128)(2,1)} copy(bf16[128,2,16,128,2]{0,4,3,2,1:T(2,128)(2,1)} %bitcast.115) | data formatting | bytes 4194304 | tf_op jit(solution)/shard_map/reshape;reshape | solution.py:459
  155.8 5.8 %convolution_convert_fusion.1 = bf16[128,320]{0,1:T(8,128)(2,1)S(1)} fusion(bf16[128,8192]{0,1:T(8,128)(2,1)} %bitcast.116, bf16[8192,320]{1,0:T(8,128)(2,1)} %bitcast.118), kind=kOutput, calls=%fused_computation.27 | convolution fusion | flops 671129600 | bytes 7421952 | tf_op jit(solution)/shard_map/dot_general | solution.py:390
  161.7 4.3 %all-gather.2.cloned.1.call-done = bf16[8192,256]{1,0:T(8,128)(2,1)} async-done(((bf16[256,256]{1,0:T(8,128)(2,1)}), bf16[8192,256]{1,0:T(8,128)(2,1)}) %all-gather.2.cloned.1.call-update) | async-done | bytes 4194320 | tf_op jit(solution)/shard_map/all_gather | solution.py:376
  165.9 3.8 %convolution_convert_fusion.2 = bf16[128,256]{1,0:T(8,128)(2,1)S(1)} fusion(bf16[128,8192]{0,1:T(8,128)(2,1)} %bitcast.117, bf16[8192,256]{1,0:T(8,128)(2,1)} %all-gather.2.cloned.1.call-done), kind=kOutput, calls=%fused_computation.28 | convolution fusion | flops 536903680 | bytes 6356992 | tf_op jit(solution)/shard_map/dot_general | solution.py:387
  170.4 10.2 %shard_map.77 = bf16[4,128,64]{2,1,0:T(8,128)(2,1)} custom-call(bf16[1,128,64]{2,1,0:T(8,128)(2,1)} %slice_bitcast_fusion.8.src_ref), custom_call_target="tpu_custom_call" | custom-call | bytes 131072 | tf_op jit(solution)/shard_map/pallas_call | solution.py:288
  184.7 11.6 %shard_map.78 = f32[4,128,64]{2,1,0:T(8,128)} custom-call(f32[4,128,64]{2,1,0:T(8,128)} %pad_maximum_fusion.1.src_ref), custom_call_target="tpu_custom_call" | custom-call | bytes 262144 | tf_op jit(solution)/shard_map/pallas_call | solution.py:288
  196.4 1.0 reduce_sum.84
  197.4 1.5 fusion.19
  199.0 1.5 fusion.18
  200.5 1.5 pad_maximum_fusion
  202.0 2.9 copy.120
  206.6 3.7 %fusion.38 = f32[16,512,128]{1,2,0:T(8,128)S(1)} fusion(bf16[16,512,256]{2,1,0:T(8,128)(2,1)} %bitcast.120, bf16[128,64]{1,0:T(8,128)(2,1)S(1)} %copy.114, bf16[128,192]{1,0:T(8,128)(2,1)S(1)} %copy.145), kind=kOutput, calls=%fused_computation.71 | convolution fusion | flops 537001984 | bytes 8454144 | tf_op jit(solution)/shard_map/rc,pkc->prk/dot_general | solution.py:444
  210.3 7.4 %fusion.3 = (f32[128]{0:T(128)}, bf16[16,128,512]{2,1,0:T(8,128)(2,1)}) fusion(bf16[16,128,512]{2,1,0:T(8,128)(2,1)S(1)} %get-tuple-element.7, f32[16,512]{1,0:T(8,128)S(1)} %mul.257, f32[128]{0:T(128)S(1)} %add_rsqrt_fusion, f32[16,512,128]{1,2,0:T(8,128)S(1)} %fusion.38, bf16[16,512,320]{2,1,0:T(8,128)(2,1)} %bitcast.119, bf16[128,512]{0,1:T(8,128)(2,1)S(1)} %bitcast.129), kind=kOutput, calls=%fused_computation.5 | convolution fusion | flops 679477120 | bytes 13747200 | tf_op jit(solution)/shard_map/rc,pkc->prk/dot_general | solution.py:445
  217.7 47.0 %shard_map.79 = (bf16[16,128,512]{2,1,0:T(8,128)(2,1)}, f32[16,1,128]{2,1,0:T(1,128)}) custom-call(bf16[16,128,512]{2,1,0:T(8,128)(2,1)} %get-tuple-element.44.refs_0_, f32[1,128]{1,0:T(1,128)} %bitcast.134), custom_call_target="tpu_custom_call" | custom-call | bytes 4210688 | tf_op jit(solution)/shard_map/pallas_call | solution.py:68
  265.5 1.9 convert_reduce_fusion
  267.4 1.4 multiply_reduce_fusion
  268.8 16.3 %shard_map.80 = f32[32,1,512]{2,1,0:T(1,128)} custom-call(f32[1,512]{1,0:T(1,128)} %bitcast.133), custom_call_target="tpu_custom_call" | custom-call | bytes 131072 | tf_op jit(solution)/shard_map/pallas_call | solution.py:68
  285.1 1.5 reduce_sum.89
  286.6 6.5 %shard_map.81 = f32[128,128]{1,0:T(8,128)} custom-call(f32[2,128,128]{2,1,0:T(8,128)} %bitcast.131), custom_call_target="tpu_custom_call" | custom-call | bytes 393216 | tf_op jit(solution)/shard_map/pallas_call | solution.py:220
  (51 shorter events, 12.9 us)
Async XLA Ops:
  7.2 158.8 %all-gather.2.cloned.1.call-start = ((), (), s32[]{:S(2)}) async-start(), calls=%async_computation.1 | async-start | bytes 4325376 | tf_op jit(solution)/shard_map/all_gather | solution.py:376
  9.8 276.8 %reduce-scatter.2.cloned.1.call-start = ((), (), s32[]{:S(2)}) async-start(), calls=%async_computation.2 | async-start | bytes 2228224 | tf_op jit(solution)/shard_map/reduce_scatter | solution.py:477
  11.7 0.9 copy-start
  143.7 5.8 %copy-start.2 = (bf16[128,512]{1,0:T(8,128)(2,1)S(1)}, bf16[128,512]{1,0:T(8,128)(2,1)}, u32[]{:S(2)}) copy-start(bf16[128,512]{1,0:T(8,128)(2,1)} %param.6) | copy-start | bytes 393220
  217.7 49.7 %copy-start.1 = (bf16[128,512]{1,0:T(8,128)(2,1)S(1)}, bf16[128,512]{1,0:T(8,128)(2,1)}, u32[]{:S(2)}) copy-start(bf16[128,512]{1,0:T(8,128)(2,1)} %side_ref.1) | copy-start | bytes 393220
Sparse Core Ops, SparseCore 0:
  10.7 155.2 all-gather.1
  205.0 72.5 reduce-scatter.1
